TPU v7x, 32 devices: a whole 2x2x4 slice. The times are simulated.
32 devices in a mesh: dp: 8 (over z, y), tensor: 4 (over x, core).
Axes of the slice: x: 2, y: 2, z: 4, core: 2. Of those that a mesh axis runs over, the one named last changes fastest.
Arguments:
- signal: bfloat16 [26112, 512], P('dp', 'tensor'), may hold values from -6 to 6
- horizon: int32 [32], P('dp'), may hold values from 96 to 720, as said below
- down_a: bfloat16 [6144, 512], P('dp', 'tensor'), may hold values from -0.078125 to 0.078125
- iso_a: bfloat16 [34816, 512], P('dp', 'tensor'), may hold values from -0.046875 to 0.046875
- up_a: bfloat16 [512, 12, 512], P('dp', None, 'tensor'), may hold values from -0.25 to 0.25
- down_b: bfloat16 [8192, 512], P('dp', 'tensor'), may hold values from -0.0625 to 0.0625
- iso_b: bfloat16 [26112, 512], P('dp', 'tensor'), may hold values from -0.0546875 to 0.0546875
- up_b: bfloat16 [512, 16, 512], P('dp', None, 'tensor'), may hold values from -0.25 to 0.25
- merge_w: bfloat16 [1024, 512], P('dp', 'tensor'), may hold values from -0.1875 to 0.1875
- ff_in: bfloat16 [512, 2048], P(None, 'tensor'), may hold values from -0.25 to 0.25
- ff_out: bfloat16 [2048, 512], P('tensor'), may hold values from -0.125 to 0.125
- norm_gain: float32 [512], P('tensor'), may hold values from 0.1 to 1.9
- norm_bias: float32 [512], P('tensor'), may hold values from -4 to 4
- first_gain: float32 [512], P('tensor'), may hold values from 0.1 to 1.9
- first_bias: float32 [512], P('tensor'), may hold values from -4 to 4
- last_gain: float32 [512], P('tensor'), may hold values from 0.1 to 1.9
- last_bias: float32 [512], P('tensor'), may hold values from -4 to 4
- cotangent: bfloat16 [26112, 512], P('dp', 'tensor'), may hold values from -6 to 6
Outputs:
- series_out: bfloat16 [26112, 512], P('dp', 'tensor')
- grad_input: float32 [26112, 512], P('dp', 'tensor')
- grad_down_a: float32 [6144, 512], P('dp', 'tensor')
- grad_iso_a: float32 [34816, 512], P('dp', 'tensor')
- grad_up_a: float32 [512, 12, 512], P('dp', None, 'tensor')
- grad_down_b: float32 [8192, 512], P('dp', 'tensor')
- grad_iso_b: float32 [26112, 512], P('dp', 'tensor')
- grad_up_b: float32 [512, 16, 512], P('dp', None, 'tensor')
- grad_merge: float32 [1024, 512], P('dp', 'tensor')
- grad_ff_in: float32 [512, 2048], P(None, 'tensor')
- grad_ff_out: float32 [2048, 512], P('tensor')
- grad_norm_gain: float32 [512], P('tensor')
- grad_norm_bias: float32 [512], P('tensor')
- grad_first_gain: float32 [512], P('tensor')
- grad_first_bias: float32 [512], P('tensor')
- grad_last_gain: float32 [512], P('tensor')
- grad_last_bias: float32 [512], P('tensor')
Inputs may be any that keep to these rules, and one draw needn't show every extreme that they name: Each series' horizon is one of 96, 192, 336 and 720; some series has 720.
All inputs are finite; a program needn't handle non-finite values.
Results may differ from a plain program's by a relative error of at most 0.014.
Values may be sent and summed in bfloat16 or wider, within the bound.
No kernel may reach another device: no remote copies, remote signals or barrier semaphores. Data moves between devices by JAX's collectives and lax.ppermute only.
A program may use at most 384 MiB of HBM per device.

v0:
```python
from functools import partial

import jax
import jax.numpy as jnp
from jax import lax
from jax.sharding import PartitionSpec as P

D = 512
SA = 12
SB = 16
IN_LEN = 96
L = 816
MA = 68
MB = 51


EPS = 1e-05


def channel_gather(operand):
    return lax.all_gather(operand, "tensor", axis=1, tiled=True)


def channel_sum(operand):
    return lax.psum_scatter(operand, "tensor", scatter_dimension=1, tiled=True)


def row_totals(first, second):
    return lax.psum((first, second), "tensor")


def matmul(left, right):
    return jnp.dot(left, right, preferred_element_type=jnp.float32)


def over_rows(left, right):
    return lax.dot_general(
        left, right, (((0,), (0,)), ((), ())), preferred_element_type=jnp.float32
    )


def against(left, right):
    return lax.dot_general(
        left, right, (((1,), (1,)), ((), ())), preferred_element_type=jnp.float32
    )


def norm_forward(operand, gain_vec, bias_vec):
    row_total, row_square = row_totals(
        jnp.sum(operand, axis=1, keepdims=True), jnp.sum(operand * operand, axis=1, keepdims=True)
    )
    row_mean = row_total / D
    inv_std = lax.rsqrt(row_square / D - row_mean * row_mean + EPS)
    normed = (operand - row_mean) * inv_std
    return (normed * gain_vec + bias_vec, (normed, inv_std))


def norm_backward(upstream, gain_vec, stored):
    normed, inv_std = stored
    scaled = upstream * gain_vec
    first_sum, second_sum = row_totals(
        jnp.sum(scaled, axis=1, keepdims=True), jnp.sum(scaled * normed, axis=1, keepdims=True)
    )
    result = inv_std * (scaled - first_sum / D - normed * second_sum / D)
    return (result, jnp.sum(upstream * normed, axis=0), jnp.sum(upstream, axis=0))


def unfold(sequence, span_len):
    padded = jnp.pad(sequence, ((0, 0), (span_len - 1, 0), (0, 0)))
    return jnp.concatenate(
        [padded[:, offset : offset + span_len, :] for offset in range(span_len)], axis=2
    )


def fold(windows, series_count, span_len):
    zeros_in = jnp.zeros((series_count, span_len, D), jnp.float32)
    _, back = jax.vjp(lambda seq_in: unfold(seq_in, span_len), zeros_in)
    return back(windows)[0]


def body(
    signal,
    horizon,
    down_a,
    iso_a,
    up_a,
    down_b,
    iso_b,
    up_b,
    merge_w,
    ff_in,
    ff_out,
    norm_gain,
    norm_bias,
    first_gain,
    first_bias,
    last_gain,
    last_bias,
    cotangent,
):
    row_count = signal.shape[0]
    col_count = signal.shape[1]
    series_count = row_count // L
    short_a = row_count // SA
    short_b = row_count // SB
    wd_a, wi_a, wu_a, wd_b, wi_b, wu_b, w_merge = (
        lax.all_gather(down_a, "dp", axis=0, tiled=True),
        lax.all_gather(iso_a, "dp", axis=0, tiled=True),
        lax.all_gather(up_a, "dp", axis=0, tiled=True),
        lax.all_gather(down_b, "dp", axis=0, tiled=True),
        lax.all_gather(iso_b, "dp", axis=0, tiled=True),
        lax.all_gather(up_b, "dp", axis=0, tiled=True),
        lax.all_gather(merge_w, "dp", axis=0, tiled=True),
    )
    x_full = channel_gather(signal)
    x_float = signal.astype(jnp.float32)
    window_a = x_full.reshape(short_a, SA * D)
    window_b = x_full.reshape(short_b, SB * D)
    down_act_a = jnp.tanh(matmul(window_a, wd_a))
    down_act_b = jnp.tanh(matmul(window_b, wd_b))
    down_low_a = down_act_a.astype(jnp.bfloat16)
    down_low_b = down_act_b.astype(jnp.bfloat16)
    down_full = channel_gather(jnp.concatenate([down_low_a, down_low_b], axis=0))
    taps_a = unfold(down_full[:short_a].reshape(series_count, MA, D), MA).reshape(short_a, MA * D)
    taps_b = unfold(down_full[short_a:].reshape(series_count, MB, D), MB).reshape(short_b, MB * D)
    iso_act_a = jnp.tanh(matmul(taps_a, wi_a))
    iso_act_b = jnp.tanh(matmul(taps_b, wi_b))
    middle_a, store_mid_a = norm_forward(
        iso_act_a + down_low_a.astype(jnp.float32), norm_gain, norm_bias
    )
    middle_b, store_mid_b = norm_forward(
        iso_act_b + down_low_b.astype(jnp.float32), norm_gain, norm_bias
    )
    middle_full = channel_gather(jnp.concatenate([middle_a, middle_b], axis=0).astype(jnp.bfloat16))
    mid_full_a = middle_full[:short_a]
    mid_full_b = middle_full[short_a:]
    up_act_a = jnp.tanh(
        matmul(mid_full_a, wu_a.reshape(D, SA * col_count)).reshape(row_count, col_count)
    )
    up_act_b = jnp.tanh(
        matmul(mid_full_b, wu_b.reshape(D, SB * col_count)).reshape(row_count, col_count)
    )
    branch_a, store_br_a = norm_forward(up_act_a + x_float, norm_gain, norm_bias)
    branch_b, store_br_b = norm_forward(up_act_b + x_float, norm_gain, norm_bias)
    pair_full = channel_gather(jnp.concatenate([branch_a, branch_b], axis=0).astype(jnp.bfloat16))
    merge_in = jnp.concatenate([pair_full[:row_count], pair_full[row_count:]], axis=1)
    merged = matmul(merge_in, w_merge)
    first_out, store_first = norm_forward(merged, first_gain, first_bias)
    first_full = channel_gather(first_out.astype(jnp.bfloat16))
    hidden_pre = matmul(first_full, ff_in)
    hidden = jax.nn.gelu(hidden_pre, approximate=False).astype(jnp.bfloat16)
    feed = channel_sum(matmul(hidden, ff_out))
    last_out, store_last = norm_forward(merged + feed, last_gain, last_bias)
    positions = lax.broadcasted_iota(jnp.int32, (series_count, L), 1)
    out_mask = (positions < IN_LEN + horizon[:, None]).astype(jnp.float32).reshape(row_count, 1)
    series_out = (last_out * out_mask).astype(jnp.bfloat16)
    upstream = cotangent.astype(jnp.float32) * out_mask
    grad_sum, grad_last_gain, grad_last_bias = norm_backward(upstream, last_gain, store_last)
    grad_feed = channel_gather(grad_sum.astype(jnp.bfloat16))
    grad_ff_out = over_rows(hidden, grad_feed)
    grad_hidden = against(grad_feed, ff_out)
    _, gelu_back = jax.vjp(partial(jax.nn.gelu, approximate=False), hidden_pre)
    grad_hpre = gelu_back(grad_hidden)[0].astype(jnp.bfloat16)
    grad_ff_in = over_rows(first_full, grad_hpre)
    grad_first = channel_sum(against(grad_hpre, ff_in))
    grad_merged_norm, grad_first_gain, grad_first_bias = norm_backward(
        grad_first, first_gain, store_first
    )
    grad_merged = (grad_merged_norm + grad_sum).astype(jnp.bfloat16)
    grad_merge = over_rows(merge_in, grad_merged)
    grad_pair_full = against(grad_merged, w_merge)
    grad_pair = channel_sum(jnp.concatenate([grad_pair_full[:, :D], grad_pair_full[:, D:]], axis=0))
    grad_resid_a, gain_part_one, bias_part_one = norm_backward(
        grad_pair[:row_count], norm_gain, store_br_a
    )
    grad_resid_b, gain_part_two, bias_part_two = norm_backward(
        grad_pair[row_count:], norm_gain, store_br_b
    )
    grad_upre_a = (
        (grad_resid_a * (1.0 - up_act_a * up_act_a))
        .astype(jnp.bfloat16)
        .reshape(short_a, SA * col_count)
    )
    grad_upre_b = (
        (grad_resid_b * (1.0 - up_act_b * up_act_b))
        .astype(jnp.bfloat16)
        .reshape(short_b, SB * col_count)
    )
    grad_up_a = over_rows(mid_full_a, grad_upre_a).reshape(D, SA, col_count)
    grad_up_b = over_rows(mid_full_b, grad_upre_b).reshape(D, SB, col_count)
    grad_mid_full_a = against(grad_upre_a, wu_a.reshape(D, SA * col_count))
    grad_mid_full_b = against(grad_upre_b, wu_b.reshape(D, SB * col_count))
    grad_middle = channel_sum(jnp.concatenate([grad_mid_full_a, grad_mid_full_b], axis=0))
    grad_inner_a, gain_part_three, bias_part_three = norm_backward(
        grad_middle[:short_a], norm_gain, store_mid_a
    )
    grad_inner_b, gain_part_four, bias_part_four = norm_backward(
        grad_middle[short_a:], norm_gain, store_mid_b
    )
    grad_ipre_a = (grad_inner_a * (1.0 - iso_act_a * iso_act_a)).astype(jnp.bfloat16)
    grad_ipre_b = (grad_inner_b * (1.0 - iso_act_b * iso_act_b)).astype(jnp.bfloat16)
    grad_iso_a = over_rows(taps_a, grad_ipre_a)
    grad_iso_b = over_rows(taps_b, grad_ipre_b)
    grad_taps_a = fold(
        against(grad_ipre_a, wi_a).reshape(series_count, MA, MA * D), series_count, MA
    ).reshape(short_a, D)
    grad_taps_b = fold(
        against(grad_ipre_b, wi_b).reshape(series_count, MB, MB * D), series_count, MB
    ).reshape(short_b, D)
    grad_down = channel_sum(jnp.concatenate([grad_taps_a, grad_taps_b], axis=0))
    grad_dpre_a = ((grad_down[:short_a] + grad_inner_a) * (1.0 - down_act_a * down_act_a)).astype(
        jnp.bfloat16
    )
    grad_dpre_b = ((grad_down[short_a:] + grad_inner_b) * (1.0 - down_act_b * down_act_b)).astype(
        jnp.bfloat16
    )
    grad_down_a = over_rows(window_a, grad_dpre_a)
    grad_down_b = over_rows(window_b, grad_dpre_b)
    grad_x_full = against(grad_dpre_a, wd_a).reshape(row_count, D) + against(
        grad_dpre_b, wd_b
    ).reshape(row_count, D)
    grad_input = channel_sum(grad_x_full) + grad_resid_a + grad_resid_b
    sum_down_a, sum_iso_a, sum_up_a, sum_down_b, sum_iso_b, sum_up_b, sum_merge = (
        lax.psum_scatter(grad_down_a, "dp", scatter_dimension=0, tiled=True),
        lax.psum_scatter(grad_iso_a, "dp", scatter_dimension=0, tiled=True),
        lax.psum_scatter(grad_up_a, "dp", scatter_dimension=0, tiled=True),
        lax.psum_scatter(grad_down_b, "dp", scatter_dimension=0, tiled=True),
        lax.psum_scatter(grad_iso_b, "dp", scatter_dimension=0, tiled=True),
        lax.psum_scatter(grad_up_b, "dp", scatter_dimension=0, tiled=True),
        lax.psum_scatter(grad_merge, "dp", scatter_dimension=0, tiled=True),
    )
    grad_norm_gain = gain_part_one + gain_part_two + gain_part_three + gain_part_four
    grad_norm_bias = bias_part_one + bias_part_two + bias_part_three + bias_part_four
    (
        sum_ff_in,
        sum_ff_out,
        sum_norm_gain,
        sum_norm_bias,
        sum_first_gain,
        sum_first_bias,
        sum_last_gain,
        sum_last_bias,
    ) = lax.psum(
        (
            grad_ff_in,
            grad_ff_out,
            grad_norm_gain,
            grad_norm_bias,
            grad_first_gain,
            grad_first_bias,
            grad_last_gain,
            grad_last_bias,
        ),
        "dp",
    )
    return (
        series_out,
        grad_input,
        sum_down_a,
        sum_iso_a,
        sum_up_a,
        sum_down_b,
        sum_iso_b,
        sum_up_b,
        sum_merge,
        sum_ff_in,
        sum_ff_out,
        sum_norm_gain,
        sum_norm_bias,
        sum_first_gain,
        sum_first_bias,
        sum_last_gain,
        sum_last_bias,
    )


def solution(mesh):
    in_specs = (
        P("dp", "tensor"),
        P("dp"),
        P("dp", "tensor"),
        P("dp", "tensor"),
        P("dp", None, "tensor"),
        P("dp", "tensor"),
        P("dp", "tensor"),
        P("dp", None, "tensor"),
        P("dp", "tensor"),
        P(None, "tensor"),
        P("tensor", None),
        P("tensor"),
        P("tensor"),
        P("tensor"),
        P("tensor"),
        P("tensor"),
        P("tensor"),
        P("dp", "tensor"),
    )
    out_specs = (
        P("dp", "tensor"),
        P("dp", "tensor"),
        P("dp", "tensor"),
        P("dp", "tensor"),
        P("dp", None, "tensor"),
        P("dp", "tensor"),
        P("dp", "tensor"),
        P("dp", None, "tensor"),
        P("dp", "tensor"),
        P(None, "tensor"),
        P("tensor", None),
        P("tensor"),
        P("tensor"),
        P("tensor"),
        P("tensor"),
        P("tensor"),
        P("tensor"),
    )
    return jax.shard_map(body, mesh=mesh, in_specs=in_specs, out_specs=out_specs, check_vma=False)
```

profile of v0, /device:TPU:0, one launch (start us, length us, event | category | flops | bytes accessed | tf_op | source)
XLA Modules:
  0.0 2445.1 jit_solution(7700934560776956939)
XLA Ops:
  12.0 45.2 %all-gather.21.cloned.1.call-done = bf16[512,12,128]{2,0,1:T(8,128)(2,1)} async-done(((bf16[64,12,128]{2,0,1:T(8,128)(2,1)}), bf16[512,12,128]{2,0,1:T(8,128)(2,1)}) %all-gather.21.cloned.1.call-update) | async-done | bytes 1572880 | tf_op jit(solution)/shard_map/all_gather | solution.py:109
  59.7 27.9 %all-gather.11.cloned.1.call-done = bf16[3264,512]{1,0:T(8,128)(2,1)} async-done(((bf16[3264,128]{1,0:T(8,128)(2,1)}), bf16[3264,512]{1,0:T(8,128)(2,1)}) %all-gather.11.cloned.1.call-update) | async-done | bytes 3342352 | tf_op jit(solution)/shard_map/all_gather | solution.py:21
  101.1 38.0 %all-gather.15.cloned.1.call-done = bf16[8192,128]{1,0:T(8,128)(2,1)} async-done(((bf16[1024,128]{1,0:T(8,128)(2,1)}), bf16[8192,128]{1,0:T(8,128)(2,1)}) %all-gather.15.cloned.1.call-update) | async-done | bytes 2097168 | tf_op jit(solution)/shard_map/all_gather | solution.py:110
  143.4 40.4 %all-gather.13.cloned.1.call-done = bf16[6144,128]{1,0:T(8,128)(2,1)} async-done(((bf16[768,128]{1,0:T(8,128)(2,1)}), bf16[6144,128]{1,0:T(8,128)(2,1)}) %all-gather.13.cloned.1.call-update) | async-done | bytes 1572880 | tf_op jit(solution)/shard_map/all_gather | solution.py:107
  525.7 14.1 fusion.39
  566.8 12.6 all-reduce.129
  586.2 32.8 %all_gather.49 = bf16[1024,128]{1,0:T(8,128)(2,1)} all-gather(bf16[128,128]{1,0:T(8,128)(2,1)S(1)} %copy-done.172), channel_id=1, replica_groups=mesh['dp'=8,'tensor'=4] {'dp'}, dimensions={0}, use_global_device_ids=true | all-gather | bytes 294912 | tf_op jit(solution)/shard_map/all_gather | solution.py:113
  619.1 15.1 all-gather.25.cloned.1.call-done
  655.4 31.2 %all-gather.27.cloned.1.call-done = bf16[3264,512]{1,0:T(8,128)(2,1)} async-done(((bf16[3264,128]{1,0:T(8,128)(2,1)}), bf16[3264,512]{1,0:T(8,128)(2,1)}) %all-gather.27.cloned.1.call-update) | async-done | bytes 3342352 | tf_op jit(solution)/shard_map/all_gather | solution.py:21
  686.6 18.5 multiply_convert_fusion
  711.9 60.9 %reduce-scatter.14.cloned.1.call-done = f32[3264,128]{1,0:T(8,128)} async-done(((f32[3264,512]{1,0:T(8,128)}), f32[3264,128]{1,0:T(8,128)}) %reduce-scatter.14.cloned.1.call-update) | async-done | bytes 1671184 | tf_op jit(solution)/shard_map/reduce_scatter | solution.py:25
  814.1 31.4 %all-gather.29.cloned.1.call-done = bf16[3264,512]{1,0:T(8,128)(2,1)} async-done(((bf16[3264,128]{1,0:T(8,128)(2,1)}), bf16[3264,512]{1,0:T(8,128)(2,1)}) %all-gather.29.cloned.1.call-update) | async-done | bytes 3342352 | tf_op jit(solution)/shard_map/all_gather | solution.py:21
  861.9 61.1 %reduce-scatter.16.cloned.1.call-done = f32[3264,128]{1,0:T(8,128)} async-done(((f32[3264,512]{1,0:T(8,128)}), f32[3264,128]{1,0:T(8,128)}) %reduce-scatter.16.cloned.1.call-update) | async-done | bytes 1671184 | tf_op jit(solution)/shard_map/reduce_scatter | solution.py:25
  977.3 105.6 %reduce-scatter.18.cloned.1.call-done = f32[6528,128]{1,0:T(8,128)} async-done(((f32[6528,512]{1,0:T(8,128)}), f32[6528,128]{1,0:T(8,128)}) %reduce-scatter.18.cloned.1.call-update) | async-done | bytes 3342352 | tf_op jit(solution)/shard_map/reduce_scatter | solution.py:25
  1117.1 25.9 %reduce-scatter.20.cloned.1.call-done = f32[476,128]{1,0:T(8,128)} async-done(((f32[476,512]{1,0:T(8,128)}), f32[476,128]{1,0:T(8,128)}) %reduce-scatter.20.cloned.1.call-update) | async-done | bytes 243728 | tf_op jit(solution)/shard_map/reduce_scatter | solution.py:25
  1152.7 13.2 fusion.58
  1165.9 17.5 reshape.245
  1202.4 17.3 fusion.60
  1219.7 30.0 %reshape.243 = f32[4,68,34816]{2,1,0:T(8,128)} reshape(f32[272,34816]{1,0:T(8,128)} %fusion.60) | data formatting | bytes 75759616 | tf_op jit(solution)/shard_map/reshape | solution.py:205
  1289.6 14.3 pad_add_fusion
  1311.4 22.4 reduce-scatter.22.cloned.1.call-done
  1397.4 12.8 fusion.57
  1410.3 15.0 fusion.59
  1426.1 22.3 all-reduce.121
  1450.5 53.4 %reduce-scatter.26.cloned.1.call-done = f32[768,128]{0,1:T(8,128)} async-done(((f32[6144,128]{0,1:T(8,128)}), f32[768,128]{0,1:T(8,128)}) %reduce-scatter.26.cloned.1.call-update) | async-done | bytes 393232 | tf_op jit(solution)/shard_map/reduce_scatter | solution.py:224
  1505.8 89.4 %reduce-scatter.32.cloned.1.call-done = f32[1024,128]{0,1:T(8,128)} async-done(((f32[8192,128]{0,1:T(8,128)}), f32[1024,128]{0,1:T(8,128)}) %reduce-scatter.32.cloned.1.call-update) | async-done | bytes 524304 | tf_op jit(solution)/shard_map/reduce_scatter | solution.py:227
  1597.3 61.2 %reduce-scatter.24.cloned.1.call-done = f32[3264,128]{1,0:T(8,128)} async-done(((f32[3264,512]{1,0:T(8,128)}), f32[3264,128]{1,0:T(8,128)}) %reduce-scatter.24.cloned.1.call-update) | async-done | bytes 1671184 | tf_op jit(solution)/shard_map/reduce_scatter | solution.py:25
  1667.1 98.1 %all-reduce.133.cloned.1.call-done = (f32[512,512]{1,0:T(8,128)}, f32[512,512]{1,0:T(8,128)}) async-done(((f32[512,512]{1,0:T(8,128)}, f32[512,512]{1,0:T(8,128)}), (f32[512,512]{1,0:T(8,128)}, f32[512,512]{1,0:T(8,128)})) %all-reduce.133.cloned.1.call-update) | async-done | bytes 2097168 | tf_op jit(solution)/shard_map/psum | solution.py:243
  1765.2 66.0 %reduce-scatter.38.cloned.1.call-done = f32[128,128]{1,0:T(8,128)} async-done(((f32[1024,128]{1,0:T(8,128)}), f32[128,128]{1,0:T(8,128)}) %reduce-scatter.38.cloned.1.call-update) | async-done | bytes 65552 | tf_op jit(solution)/shard_map/reduce_scatter | solution.py:230
  1831.2 78.1 %reduce-scatter.30.cloned.1.call-done = f32[64,12,128]{2,0,1:T(8,128)} async-done(((f32[512,12,128]{2,0,1:T(8,128)}), f32[64,12,128]{2,0,1:T(8,128)}) %reduce-scatter.30.cloned.1.call-update) | async-done | bytes 393232 | tf_op jit(solution)/shard_map/reduce_scatter | solution.py:226
  1909.3 221.7 %reduce-scatter.34.cloned.1.call-done = f32[3264,128]{1,0:T(8,128)} async-done(((f32[26112,128]{1,0:T(8,128)}), f32[3264,128]{1,0:T(8,128)}) %reduce-scatter.34.cloned.1.call-update) | async-done | bytes 1671184 | tf_op jit(solution)/shard_map/reduce_scatter | solution.py:228
  2131.0 302.3 %reduce-scatter.28.cloned.1.call-done = f32[4352,128]{1,0:T(8,128)} async-done(((f32[34816,128]{1,0:T(8,128)}), f32[4352,128]{1,0:T(8,128)}) %reduce-scatter.28.cloned.1.call-update) | async-done | bytes 2228240 | tf_op jit(solution)/shard_map/reduce_scatter | solution.py:225
  (798 shorter events, 732.7 us)
Async XLA Ops:
  7.2 679.5 %copy-start = (bf16[512,512]{1,0:T(8,128)(2,1)S(1)}, bf16[512,512]{1,0:T(8,128)(2,1)}, u32[]{:S(2)}) copy-start(bf16[512,512]{1,0:T(8,128)(2,1)} %param.27) | copy-start | bytes 1572868
  7.2 49.9 %all-gather.21.cloned.1.call-start = ((), (), s32[]{:S(2)}) async-start(), calls=%async_computation.18 | async-start | bytes 1769472 | tf_op jit(solution)/shard_map/all_gather | solution.py:109
  7.9 79.7 %all-gather.11.cloned.1.call-start = ((), (), s32[]{:S(2)}) async-start(), calls=%async_computation.13 | async-start | bytes 4177920 | tf_op jit(solution)/shard_map/all_gather | solution.py:21
  8.7 130.4 %all-gather.15.cloned.1.call-start = ((), (), s32[]{:S(2)}) async-start(), calls=%async_computation.15 | async-start | bytes 2359296 | tf_op jit(solution)/shard_map/all_gather | solution.py:110
  9.4 174.4 %all-gather.13.cloned.1.call-start = ((), (), s32[]{:S(2)}) async-start(), calls=%async_computation.14 | async-start | bytes 1769472 | tf_op jit(solution)/shard_map/all_gather | solution.py:107
  10.0 506.4 %all-gather.19.cloned.1.call-start = ((), (), s32[]{:S(2)}) async-start(), calls=%async_computation.17 | async-start | bytes 7520256 | tf_op jit(solution)/shard_map/all_gather | solution.py:111
  10.6 515.2 %all-gather.17.cloned.1.call-start = ((), (), s32[]{:S(2)}) async-start(), calls=%async_computation.16 | async-start | bytes 10027008 | tf_op jit(solution)/shard_map/all_gather | solution.py:108
  11.2 546.6 %all-gather.23.cloned.1.call-start = ((), (), s32[]{:S(2)}) async-start(), calls=%async_computation.19 | async-start | bytes 2359296 | tf_op jit(solution)/shard_map/all_gather | solution.py:112
  11.9 622.3 %all-gather.25.cloned.1.call-start = ((), (), s32[]{:S(2)}) async-start(), calls=%async_computation.20 | async-start | bytes 8355840 | tf_op jit(solution)/shard_map/all_gather | solution.py:21
  562.8 537.5 %copy-start.2 = (f32[3264,128]{1,0:T(8,128)}, f32[3264,128]{1,0:T(8,128)S(1)}, u32[]{:S(2)}) copy-start(f32[3264,128]{1,0:T(8,128)S(1)} %tanh.31) | copy-start | bytes 5013508
  580.4 519.9 %copy-start.147 = (f32[3264]{0:T(1024)}, f32[3264]{0:T(1024)S(1)}, u32[]{:S(2)}) copy-start(f32[3264]{0:T(1024)S(1)} %get-tuple-element.114) | copy-start | bytes 39172
  580.4 519.9 %copy-start.149 = (f32[3264]{0:T(1024)}, f32[3264]{0:T(1024)S(1)}, u32[]{:S(2)}) copy-start(f32[3264]{0:T(1024)S(1)} %get-tuple-element.115) | copy-start | bytes 39172
  580.4 519.9 %copy-start.151 = (f32[3264]{0:T(1024)}, f32[3264]{0:T(1024)S(1)}, u32[]{:S(2)}) copy-start(f32[3264]{0:T(1024)S(1)} %get-tuple-element.409) | copy-start | bytes 39172
  580.4 519.9 %copy-start.153 = (f32[3264]{0:T(1024)}, f32[3264]{0:T(1024)S(1)}, u32[]{:S(2)}) copy-start(f32[3264]{0:T(1024)S(1)} %get-tuple-element.410) | copy-start | bytes 39172
  586.2 100.5 %all-gather.27.cloned.1.call-start = ((), (), s32[]{:S(2)}) async-start(), calls=%async_computation.21 | async-start | bytes 4177920 | tf_op jit(solution)/shard_map/all_gather | solution.py:21
  655.3 117.5 %reduce-scatter.14.cloned.1.call-start = ((), (), s32[]{:S(2)}) async-start(), calls=%async_computation.22 | async-start | bytes 8355840 | tf_op jit(solution)/shard_map/reduce_scatter | solution.py:25
  711.7 133.8 %all-gather.29.cloned.1.call-start = ((), (), s32[]{:S(2)}) async-start(), calls=%async_computation.23 | async-start | bytes 4177920 | tf_op jit(solution)/shard_map/all_gather | solution.py:21
  814.0 108.9 %reduce-scatter.16.cloned.1.call-start = ((), (), s32[]{:S(2)}) async-start(), calls=%async_computation.24 | async-start | bytes 8355840 | tf_op jit(solution)/shard_map/reduce_scatter | solution.py:25
  861.8 221.1 %reduce-scatter.18.cloned.1.call-start = ((), (), s32[]{:S(2)}) async-start(), calls=%async_computation.25 | async-start | bytes 16711680 | tf_op jit(solution)/shard_map/reduce_scatter | solution.py:25
  977.3 165.6 %reduce-scatter.20.cloned.1.call-start = ((), (), s32[]{:S(2)}) async-start(), calls=%async_computation.26 | async-start | bytes 1228800 | tf_op jit(solution)/shard_map/reduce_scatter | solution.py:25
  1117.0 216.8 %reduce-scatter.22.cloned.1.call-start = ((), (), s32[]{:S(2)}) async-start(), calls=%async_computation.27 | async-start | bytes 1228800 | tf_op jit(solution)/shard_map/reduce_scatter | solution.py:25
  1308.0 140.3 %reduce-scatter.36.cloned.1.call-start = ((), (), s32[]{:S(2)}) async-start(), calls=%async_computation.34 | async-start | bytes 4718592 | tf_op jit(solution)/shard_map/reduce_scatter | solution.py:229
  1311.2 192.8 %reduce-scatter.26.cloned.1.call-start = ((), (), s32[]{:S(2)}) async-start(), calls=%async_computation.29 | async-start | bytes 3538944 | tf_op jit(solution)/shard_map/reduce_scatter | solution.py:224
  1339.6 255.6 %reduce-scatter.32.cloned.1.call-start = ((), (), s32[]{:S(2)}) async-start(), calls=%async_computation.32 | async-start | bytes 4718592 | tf_op jit(solution)/shard_map/reduce_scatter | solution.py:227
  1345.7 312.8 %reduce-scatter.24.cloned.1.call-start = ((), (), s32[]{:S(2)}) async-start(), calls=%async_computation.28 | async-start | bytes 8355840 | tf_op jit(solution)/shard_map/reduce_scatter | solution.py:25
  1379.1 386.2 %all-reduce.133.cloned.1.call-start = ((), (), s32[]{:S(2)}) async-start(), calls=%async_computation.36 | async-start | bytes 4194304 | tf_op jit(solution)/shard_map/psum | solution.py:243
  1388.3 443.0 %reduce-scatter.38.cloned.1.call-start = ((), (), s32[]{:S(2)}) async-start(), calls=%async_computation.35 | async-start | bytes 589824 | tf_op jit(solution)/shard_map/reduce_scatter | solution.py:230
  1394.3 515.1 %reduce-scatter.30.cloned.1.call-start = ((), (), s32[]{:S(2)}) async-start(), calls=%async_computation.31 | async-start | bytes 3538944 | tf_op jit(solution)/shard_map/reduce_scatter | solution.py:226
  1397.1 733.9 %reduce-scatter.34.cloned.1.call-start = ((), (), s32[]{:S(2)}) async-start(), calls=%async_computation.33 | async-start | bytes 15040512 | tf_op jit(solution)/shard_map/reduce_scatter | solution.py:228
  1410.2 1023.1 %reduce-scatter.28.cloned.1.call-start = ((), (), s32[]{:S(2)}) async-start(), calls=%async_computation.30 | async-start | bytes 20054016 | tf_op jit(solution)/shard_map/reduce_scatter | solution.py:225
  1425.4 233.1 %copy-start.3 = (f32[3264,128]{1,0:T(8,128)S(1)}, f32[3264,128]{1,0:T(8,128)}, u32[]{:S(2)}) copy-start(f32[3264,128]{1,0:T(8,128)} %copy-done.2) | copy-start | bytes 5013508
  1595.2 842.6 %copy-start.1 = (bf16[512,512]{1,0:T(8,128)(2,1)S(1)}, bf16[512,512]{1,0:T(8,128)(2,1)}, u32[]{:S(2)}) copy-start(bf16[512,512]{1,0:T(8,128)(2,1)} %param.27) | copy-start | bytes 1572868
  (184 other events, 5701.1 us)
Sparse Core Ops, SparseCore 0:
  10.2 46.8 all-gather.20
  58.7 28.8 all-gather.10
  89.7 49.2 all-gather.14
  141.1 42.6 all-gather.12
  185.8 102.7 all-gather.18
  290.6 129.7 all-gather.16
  422.6 47.4 all-gather.22
  586.3 47.8 all-gather.24
  655.5 31.1 all-gather.26
  711.8 60.9 reduce-scatter.13
  814.2 31.2 all-gather.28
  861.9 60.9 reduce-scatter.15
  977.4 105.4 reduce-scatter.17
  1117.1 25.7 reduce-scatter.19
  1308.1 25.6 reduce-scatter.21
  1337.3 88.4 reduce-scatter.35
  1429.6 74.2 reduce-scatter.25
  1507.8 87.3 reduce-scatter.31
  1597.8 60.6 reduce-scatter.23
  1663.1 102.1 all-reduce.132
  1769.5 61.6 reduce-scatter.37
  1835.4 73.8 reduce-scatter.29
  1913.6 217.3 reduce-scatter.33
  2135.9 297.3 reduce-scatter.27
where the time goes:
time: 2460 us; the launch traced here: 2450 us
  waiting for transfers between devices  1480 us (60%)
  local copies, waits for them, and re-layouts  493 us (20%)
  matrix products  186 us (8%)
  blocking collectives  149 us (6%)
  other arithmetic  120 us (5%)
    reduce_scatter x6, waiting for transfers between devices, channel_sum(): return lax.psum_scatter(operand, 'tensor', scatter_dimension=1, tiled=True)  337 us
    reduce_scatter x1, waiting for transfers between devices, body(): lax.psum_scatter(grad_iso_a, 'dp', scatter_dimension=0, tiled=True)  302 us
    reduce_scatter x1, waiting for transfers between devices, body(): lax.psum_scatter(grad_iso_b, 'dp', scatter_dimension=0, tiled=True)  222 us
    concatenate x119, local copies, waits for them, and re-layouts, unfold(): jnp.concatenate([padded[:, offset:offset + span_len, :] for offset in ran...  191 us
    unnamed x507, local copies, waits for them, and re-layouts  133 us
    all_gather x4, waiting for transfers between devices, channel_gather(): return lax.all_gather(operand, 'tensor', axis=1, tiled=True)  106 us
    psum x1, waiting for transfers between devices, body(): lax.psum((grad_ff_in, grad_ff_out, grad_norm_gain, grad_norm_bias, grad_f...  98.1 us
    reduce_scatter x1, waiting for transfers between devices, body(): lax.psum_scatter(grad_down_b, 'dp', scatter_dimension=0, tiled=True)  89.4 us
  transfers between devices with their start and end apart: 24, of which 20 were waited for; matrix products, arithmetic and copies ran while one was open for 20% of the time, Pallas kernels for 0%

commit v1 on v0

v1 whole, which is shorter than its diff:
```python
from functools import partial

import jax
import jax.numpy as jnp
from jax import lax
from jax.sharding import PartitionSpec as P

D = 512
SA = 12
SB = 16
IN_LEN = 96
L = 816
MA = 68
MB = 51


EPS = 1e-05
BF = jnp.bfloat16
F32 = jnp.float32


def matmul(left, right):
    return jnp.dot(left, right, preferred_element_type=F32)


def over_rows(left, right):
    return lax.dot_general(left, right, (((0,), (0,)), ((), ())), preferred_element_type=F32)


def against(left, right):
    return lax.dot_general(left, right, (((1,), (1,)), ((), ())), preferred_element_type=F32)


def swap(value, mask):
    return lax.ppermute(value, "tensor", [(i, i ^ mask) for i in range(4)])


def by_xor(blocks):
    t = lax.axis_index("tensor")
    low = (t % 2) == 0
    high = (t // 2) == 0
    mid = [jnp.where(low, blocks[k], blocks[k ^ 1]) for k in range(4)]
    return [jnp.where(high, mid[k], mid[k ^ 2]) for k in range(4)]


def lanes(value):
    width = value.shape[1] // 4
    return [value[:, i * width : (i + 1) * width] for i in range(4)]


def own_lanes(value):
    width = value.shape[1] // 4
    return lax.dynamic_slice_in_dim(value, lax.axis_index("tensor") * width, width, 1)


def gather_blocks(value):
    across = swap(value, 2)
    return by_xor([value, swap(value, 1), across, swap(across, 1)])


def channel_gather(value):
    return jnp.concatenate(gather_blocks(value), axis=1)


def to_rows(value):
    t = lax.axis_index("tensor")
    count = value.shape[0] // 4
    send = [lax.dynamic_slice_in_dim(value, (t ^ k) * count, count, 0) for k in range(4)]
    return jnp.concatenate(by_xor([send[0]] + [swap(send[k], k) for k in (1, 2, 3)]), axis=1)


def to_channels(value):
    send = by_xor(lanes(value))
    return jnp.concatenate(by_xor([send[0]] + [swap(send[k], k) for k in (1, 2, 3)]), axis=0)


def quarter_sum(blocks):
    send = by_xor(blocks)
    mine = send[0] + swap(send[1].astype(BF), 1).astype(F32)
    other = send[2] + swap(send[3].astype(BF), 1).astype(F32)
    return mine + swap(other.astype(BF), 2).astype(F32)


def ring_order(count):
    return list(range(0, count, 2)) + list(range(1, count, 2))[::-1]


def ring_gather(value):
    count = lax.axis_size("dp")
    order = ring_order(count)
    table = jnp.array(order, jnp.int32)
    place = jnp.array([order.index(i) for i in range(count)], jnp.int32)[lax.axis_index("dp")]
    up = [(order[i], order[(i + 1) % count]) for i in range(count)]
    down = [(b, a) for a, b in up]
    result = jnp.zeros((count,) + value.shape, value.dtype)
    result = lax.dynamic_update_index_in_dim(result, value, lax.axis_index("dp"), 0)
    ahead = behind = value
    for step in range(1, count // 2 + 1):
        ahead = lax.ppermute(ahead, "dp", up)
        result = lax.dynamic_update_index_in_dim(result, ahead, table[(place - step) % count], 0)
        if step <= (count - 1) // 2:
            behind = lax.ppermute(behind, "dp", down)
            result = lax.dynamic_update_index_in_dim(
                result, behind, table[(place + step) % count], 0
            )
    return result


def exchange_sum(blocks):
    got = lax.all_to_all(blocks.astype(BF), "dp", 0, 0, tiled=True)
    return jnp.sum(got.astype(F32), axis=0)


def scatter_sum(value):
    return lax.psum_scatter(value.astype(BF), "dp", scatter_dimension=0, tiled=True).astype(F32)


def norm_forward(operand, gain_vec, bias_vec):
    row_mean = jnp.mean(operand, axis=1, keepdims=True)
    row_square = jnp.mean(operand * operand, axis=1, keepdims=True)
    inv_std = lax.rsqrt(row_square - row_mean * row_mean + EPS)
    normed = (operand - row_mean) * inv_std
    return (normed * gain_vec + bias_vec, (normed, inv_std))


def norm_backward(upstream, gain_vec, stored):
    normed, inv_std = stored
    scaled = upstream * gain_vec
    first_mean = jnp.mean(scaled, axis=1, keepdims=True)
    second_mean = jnp.mean(scaled * normed, axis=1, keepdims=True)
    result = inv_std * (scaled - first_mean - normed * second_mean)
    return (result, jnp.sum(upstream * normed, axis=0), jnp.sum(upstream, axis=0))


def tap_plan(rows_held):
    count = lax.axis_size("dp")
    taps = max(-(-(i * rows_held % D + rows_held) // D) for i in range(count))
    start = lax.axis_index("dp") * rows_held
    return taps, start // D, start % D


def iso_forward(act_all, weight, span_len):
    groups = act_all.shape[0]
    series = act_all.shape[1] // span_len
    taps, first, offset = tap_plan(weight.shape[0])
    wide = lax.dynamic_update_slice_in_dim(
        jnp.zeros((taps * D, weight.shape[1]), BF), weight, offset, 0
    )
    timed = act_all.reshape(groups, series, span_len, D).transpose(2, 0, 1, 3)
    timed = timed.reshape(span_len, groups * series, D)
    timed = jnp.pad(timed, ((span_len - 1, taps), (0, 0), (0, 0)))
    timed = lax.dynamic_slice_in_dim(timed, first, span_len + taps - 1, 0)
    columns = jnp.concatenate([timed[j : j + span_len] for j in range(taps)], axis=2)
    columns = columns.reshape(span_len * groups * series, taps * D)
    pre = matmul(columns, wide).reshape(span_len, groups, series, -1)
    pre = pre.transpose(1, 2, 0, 3).reshape(groups, series * span_len, -1)
    return pre, (columns, wide)


def iso_backward(grad_all, stored, rows_held, span_len):
    columns, wide = stored
    groups = grad_all.shape[0]
    series = grad_all.shape[1] // span_len
    taps, first, offset = tap_plan(rows_held)
    timed = grad_all.reshape(groups, series, span_len, -1).transpose(2, 0, 1, 3)
    timed = timed.reshape(span_len * groups * series, -1)
    grad_wide = over_rows(columns, timed)
    grad_weight = lax.dynamic_slice_in_dim(grad_wide, offset, rows_held, 0)
    spread = against(timed, wide).reshape(span_len, groups * series, taps * D)
    total = jnp.zeros((span_len + taps - 1, groups * series, D), F32)
    for j in range(taps):
        total = total.at[j : j + span_len].add(spread[:, :, j * D : (j + 1) * D])
    padded = jnp.zeros((2 * span_len - 1 + taps, groups * series, D), F32)
    padded = lax.dynamic_update_slice_in_dim(padded, total, first, 0)
    back = padded[span_len - 1 : 2 * span_len - 1].reshape(span_len, groups, series, D)
    return grad_weight, back.transpose(1, 2, 0, 3).reshape(groups, series * span_len, D)


def body(
    signal,
    horizon,
    down_a,
    iso_a,
    up_a,
    down_b,
    iso_b,
    up_b,
    merge_w,
    ff_in,
    ff_out,
    norm_gain,
    norm_bias,
    first_gain,
    first_bias,
    last_gain,
    last_bias,
    cotangent,
):
    row_count, col_count = signal.shape
    part_rows = row_count // 4
    series_count = row_count // L
    short_a = row_count // SA
    short_b = row_count // SB
    t = lax.axis_index("tensor")
    wd_a = ring_gather(down_a).reshape(SA * D, col_count)
    wd_b = ring_gather(down_b).reshape(SB * D, col_count)
    x_full = channel_gather(signal)
    vectors = channel_gather(
        jnp.stack([norm_gain, norm_bias, first_gain, first_bias, last_gain, last_bias])
    )
    n_gain, n_bias, f_gain, f_bias, l_gain, l_bias = (vectors[i : i + 1] for i in range(6))
    cot_rows = to_rows(cotangent)
    wu_a = lax.all_gather(up_a, "dp", axis=0, tiled=True).reshape(D, SA * col_count)
    wu_b = lax.all_gather(up_b, "dp", axis=0, tiled=True).reshape(D, SB * col_count)
    w_merge = channel_gather(ring_gather(merge_w).reshape(2 * D, col_count))
    w_in = channel_gather(ff_in)
    w_out = jnp.concatenate(gather_blocks(ff_out), axis=0)

    window_a = x_full.reshape(short_a, SA * D)
    window_b = x_full.reshape(short_b, SB * D)
    down_act = jnp.concatenate(
        [jnp.tanh(matmul(window_a, wd_a)), jnp.tanh(matmul(window_b, wd_b))], axis=0
    )
    down_low = down_act.astype(BF)
    high = (t // 2) == 0
    low = (t % 2) == 0
    across = swap(down_low, 2)
    pair = jnp.concatenate(
        [jnp.where(high, down_low, across), jnp.where(high, across, down_low)], axis=1
    )
    pair_all = ring_gather(pair)
    mate_all = swap(pair_all, 1)
    even = jnp.where(low, pair_all, mate_all)
    odd = jnp.where(low, mate_all, pair_all)
    down_all = jnp.concatenate(
        [even[..., :col_count], odd[..., :col_count], even[..., col_count:], odd[..., col_count:]],
        axis=2,
    )
    down_full = lax.dynamic_index_in_dim(down_all, lax.axis_index("dp"), 0, keepdims=False)

    part_a, iso_store_a = iso_forward(down_all[:, :short_a], iso_a, MA)
    part_b, iso_store_b = iso_forward(down_all[:, short_a:], iso_b, MB)
    iso_pre = exchange_sum(jnp.concatenate([part_a, part_b], axis=1))
    iso_act = jnp.tanh(channel_gather(iso_pre))
    middle, store_mid = norm_forward(iso_act + down_full.astype(F32), n_gain, n_bias)
    middle = middle.astype(BF)

    up_act_a = jnp.tanh(matmul(middle[:short_a], wu_a).reshape(row_count, col_count))
    up_act_b = jnp.tanh(matmul(middle[short_a:], wu_b).reshape(row_count, col_count))

    x_rows = lax.dynamic_slice_in_dim(x_full, t * part_rows, part_rows, 0).astype(F32)
    branch_a, store_br_a = norm_forward(
        to_rows(up_act_a.astype(BF)).astype(F32) + x_rows, n_gain, n_bias
    )
    branch_b, store_br_b = norm_forward(
        to_rows(up_act_b.astype(BF)).astype(F32) + x_rows, n_gain, n_bias
    )
    merge_in = jnp.concatenate([branch_a.astype(BF), branch_b.astype(BF)], axis=1)
    merged = matmul(merge_in, w_merge)
    first_out, store_first = norm_forward(merged, f_gain, f_bias)
    first_low = first_out.astype(BF)
    hidden_pre = matmul(first_low, w_in)
    hidden = jax.nn.gelu(hidden_pre, approximate=False).astype(BF)
    feed = matmul(hidden, w_out)
    last_out, store_last = norm_forward(merged + feed, l_gain, l_bias)
    position = t * part_rows + lax.broadcasted_iota(jnp.int32, (part_rows, 1), 0)
    limit = jnp.broadcast_to(horizon[:, None], (series_count, L)).reshape(row_count, 1)
    limit = lax.dynamic_slice_in_dim(limit, t * part_rows, part_rows, 0)
    out_mask = (position % L < IN_LEN + limit).astype(F32)
    series_out = to_channels((last_out * out_mask).astype(BF))
    upstream = cot_rows.astype(F32) * out_mask
    grad_sum, grad_last_gain, grad_last_bias = norm_backward(upstream, l_gain, store_last)
    grad_feed = grad_sum.astype(BF)
    grad_ff_out = over_rows(hidden, grad_feed)
    grad_hidden = against(grad_feed, w_out)
    _, gelu_back = jax.vjp(partial(jax.nn.gelu, approximate=False), hidden_pre)
    grad_hpre = gelu_back(grad_hidden)[0].astype(BF)
    grad_ff_in = over_rows(first_low, grad_hpre)
    grad_first = against(grad_hpre, w_in)
    grad_merged_norm, grad_first_gain, grad_first_bias = norm_backward(
        grad_first, f_gain, store_first
    )
    grad_merged = (grad_merged_norm + grad_sum).astype(BF)
    grad_merge = over_rows(merge_in, grad_merged)
    grad_pair = against(grad_merged, w_merge)
    grad_resid_a, gain_one, bias_one = norm_backward(grad_pair[:, :D], n_gain, store_br_a)
    grad_resid_b, gain_two, bias_two = norm_backward(grad_pair[:, D:], n_gain, store_br_b)

    resid_a = to_channels(grad_resid_a.astype(BF)).astype(F32)
    resid_b = to_channels(grad_resid_b.astype(BF)).astype(F32)
    grad_upre_a = (resid_a * (1.0 - up_act_a * up_act_a)).astype(BF).reshape(short_a, -1)
    grad_upre_b = (resid_b * (1.0 - up_act_b * up_act_b)).astype(BF).reshape(short_b, -1)
    part_mid = jnp.concatenate([against(grad_upre_a, wu_a), against(grad_upre_b, wu_b)], axis=0)
    grad_up_a = over_rows(middle[:short_a], grad_upre_a).reshape(D, SA, col_count)
    grad_up_b = over_rows(middle[short_a:], grad_upre_b).reshape(D, SB, col_count)
    blocks = lanes(part_mid)
    keep = jnp.concatenate([jnp.where(low, blocks[0], blocks[1]), jnp.where(low, blocks[2], blocks[3])], axis=1)
    give = jnp.concatenate([jnp.where(low, blocks[1], blocks[0]), jnp.where(low, blocks[3], blocks[2])], axis=1)
    keep = keep + swap(give, 1)
    keep = keep + swap(keep, 2)
    mate = swap(keep, 1)
    even = jnp.where(low, keep, mate)
    odd = jnp.where(low, mate, keep)
    grad_middle = jnp.concatenate(
        [even[:, :col_count], odd[:, :col_count], even[:, col_count:], odd[:, col_count:]], axis=1
    )
    grad_inner, gain_mid, bias_mid = norm_backward(grad_middle, n_gain, store_mid)
    grad_ipre = own_lanes((grad_inner * (1.0 - iso_act * iso_act)).astype(BF))
    grad_ipre_all = ring_gather(grad_ipre)
    grad_iso_a, back_a = iso_backward(grad_ipre_all[:, :short_a], iso_store_a, iso_a.shape[0], MA)
    grad_iso_b, back_b = iso_backward(grad_ipre_all[:, short_a:], iso_store_b, iso_b.shape[0], MB)
    back = jnp.concatenate([back_a, back_b], axis=1)
    groups = back.shape[0]
    back = quarter_sum([back[..., i * col_count : (i + 1) * col_count] for i in range(4)])
    grad_down = exchange_sum(back)
    grad_dpre = ((grad_down + own_lanes(grad_inner)) * (1.0 - down_act * down_act)).astype(BF)
    grad_dpre_a, grad_dpre_b = grad_dpre[:short_a], grad_dpre[short_a:]
    grad_down_a = over_rows(window_a, grad_dpre_a)
    grad_down_b = over_rows(window_b, grad_dpre_b)
    grad_x = against(grad_dpre_a, wd_a).reshape(row_count, D) + against(
        grad_dpre_b, wd_b
    ).reshape(row_count, D)
    grad_input = quarter_sum(lanes(grad_x)) + resid_a + resid_b

    sum_up_a = scatter_sum(grad_up_a)
    sum_up_b = scatter_sum(grad_up_b)
    sum_down_a = scatter_sum(grad_down_a)
    sum_down_b = scatter_sum(grad_down_b)
    sum_merge = scatter_sum(quarter_sum(lanes(grad_merge)))
    ff_own = jnp.concatenate(
        [
            quarter_sum(lanes(grad_ff_in)),
            quarter_sum([grad_ff_out[i * D : (i + 1) * D] for i in range(4)]),
        ],
        axis=0,
    )
    ff_total = ring_gather(scatter_sum(ff_own).astype(BF)).reshape(2 * D, D).astype(F32)
    sums = jnp.stack(
        [
            gain_one + gain_two + 0.25 * gain_mid,
            bias_one + bias_two + 0.25 * bias_mid,
            grad_first_gain,
            grad_first_bias,
            grad_last_gain,
            grad_last_bias,
        ]
    )
    sums = own_lanes(lax.psum(sums, ("dp", "tensor")))
    return (
        series_out,
        grad_input,
        sum_down_a,
        grad_iso_a,
        sum_up_a,
        sum_down_b,
        grad_iso_b,
        sum_up_b,
        sum_merge,
        ff_total[:D],
        ff_total[D:],
        sums[0],
        sums[1],
        sums[2],
        sums[3],
        sums[4],
        sums[5],
    )


def solution(mesh):
    in_specs = (
        P("dp", "tensor"),
        P("dp"),
        P("dp", "tensor"),
        P("dp", "tensor"),
        P("dp", None, "tensor"),
        P("dp", "tensor"),
        P("dp", "tensor"),
        P("dp", None, "tensor"),
        P("dp", "tensor"),
        P(None, "tensor"),
        P("tensor", None),
        P("tensor"),
        P("tensor"),
        P("tensor"),
        P("tensor"),
        P("tensor"),
        P("tensor"),
        P("dp", "tensor"),
    )
    out_specs = (
        P("dp", "tensor"),
        P("dp", "tensor"),
        P("dp", "tensor"),
        P("dp", "tensor"),
        P("dp", None, "tensor"),
        P("dp", "tensor"),
        P("dp", "tensor"),
        P("dp", None, "tensor"),
        P("dp", "tensor"),
        P(None, "tensor"),
        P("tensor", None),
        P("tensor"),
        P("tensor"),
        P("tensor"),
        P("tensor"),
        P("tensor"),
        P("tensor"),
    )
    return jax.shard_map(body, mesh=mesh, in_specs=in_specs, out_specs=out_specs, check_vma=False)
```

time: 2460 us -> 975 us (0.40)
  waiting for transfers between devices: 1480 us -> 227 us
  local copies, waits for them, and re-layouts: 493 us -> 257 us
  blocking collectives: 149 us -> 53.8 us
  starting transfers between devices: 1.44 us -> 89.1 us
  matrix products: 186 us -> 150 us
  other arithmetic: 120 us -> 151 us
    reduce_scatter x13 -> x6, waiting for transfers between devices: 1150 us -> 27.7 us  [scatter_sum(): lax.psum_scatter(value.astype(BF), 'dp', scatter_dimension=0, tiled=True)]
    all_gather x10 -> x2, waiting for transfers between devices: 229 us -> 0.01 us  [the longest x1 0.01 us: body(): lax.all_gather(up_a, 'dp', axis=0, tiled=True).reshape(D, SA * col_count)]
    ppermute x0 -> x98, waiting for transfers between devices: none -> 183 us  [the longest x56 81.5 us: swap(): return lax.ppermute(value, 'tensor', [(i, i ^ mask) for i in range(4)])]
    concatenate x119 -> x4, local copies, waits for them, and re-layouts: 191 us -> 25 us  [the longest x3 23.9 us: iso_forward(): jnp.concatenate([timed[j:j + span_len] for j in range(taps)], axis=2)]
    psum x1 -> x0, waiting for transfers between devices: 98.1 us -> none  [body(): lax.psum((grad_ff_in, grad_ff_out, grad_norm_gain, grad_norm_bias, grad_f...]
    unnamed x507 -> x223, local copies, waits for them, and re-layouts: 133 us -> 35.1 us
    dynamic_update_slice x0 -> x52, local copies, waits for them, and re-layouts: none -> 85.9 us  [the longest x25 30.2 us: ring_gather(): lax.dynamic_update_index_in_dim(result, ahead, table[(place - step) % cou...]
    ppermute x0 -> x98, starting transfers between devices: none -> 79.1 us  [the longest x56 32.5 us: swap(): return lax.ppermute(value, 'tensor', [(i, i ^ mask) for i in range(4)])]
  transfers between devices with their start and end apart: 24 -> 108, of which waited for: 20 -> 41; matrix products, arithmetic and copies ran while one was open for 20% -> 50% of each run, Pallas kernels for 0% -> 0%
where the time goes in v1:
time: 975 us; the launch traced here: 963 us
  local copies, waits for them, and re-layouts  257 us (26%)
  waiting for transfers between devices  227 us (23%)
  other arithmetic  151 us (15%)
  matrix products  150 us (15%)
  starting transfers between devices  89.1 us (9%)
  blocking collectives  53.8 us (6%)
  between operations  35.3 us (4%)
    ppermute x56, waiting for transfers between devices, swap(): return lax.ppermute(value, 'tensor', [(i, i ^ mask) for i in range(4)])  81.5 us
    dot_general x9, matrix products, matmul(): return jnp.dot(left, right, preferred_element_type=F32)  65 us
    psum x1, blocking collectives, body(): sums = own_lanes(lax.psum(sums, ('dp', 'tensor')))  53.8 us
    ppermute x18, waiting for transfers between devices, ring_gather(): behind = lax.ppermute(behind, 'dp', down)  52.4 us
    dot_general x9, matrix products, against(): lax.dot_general(left, right, (((1,), (1,)), ((), ())), preferred_element_...  50.7 us
    ppermute x24, waiting for transfers between devices, ring_gather(): ahead = lax.ppermute(ahead, 'dp', up)  48.7 us
    scatter-add x15, other arithmetic, iso_backward(): total = total.at[j:j + span_len].add(spread[:, :, j * D:(j + 1) * D])  39.3 us
    unnamed x223, local copies, waits for them, and re-layouts  35.1 us
  transfers between devices with their start and end apart: 108, of which 41 were waited for; matrix products, arithmetic and copies ran while one was open for 50% of the time, Pallas kernels for 0%

profile of v1, /device:TPU:0, one launch (start us, length us, event | category | flops | bytes accessed | tf_op | source)
XLA Modules:
  0.0 962.9 jit_solution(12522362180640404888)
XLA Ops:
  41.1 11.8 %collective-permute-done.11 = bf16[1024,128]{1,0:T(8,128)(2,1)S(1)} collective-permute-done((bf16[1024,128]{1,0:T(8,128)(2,1)S(1)}, bf16[1024,128]{1,0:T(8,128)(2,1)S(1)}, u32[]{:S(2)}, u32[]{:S(2)}) %collective-permute-start.11) | collective-permute-done | bytes 262176 | tf_op jit(solution)/shard_map/ppermute | solution.py:102
  55.0 6.5 collective-permute-done.6
  120.4 10.6 %collective-permute-done.21 = bf16[476,256]{1,0:T(8,128)(2,1)S(1)} collective-permute-done((bf16[476,256]{1,0:T(8,128)(2,1)S(1)}, bf16[476,256]{1,0:T(8,128)(2,1)S(1)}, u32[]{:S(2)}, u32[]{:S(2)}) %collective-permute-start.21) | collective-permute-done | bytes 243744 | tf_op jit(solution)/shard_map/ppermute | solution.py:102
  172.6 21.0 %fusion.53 = bf16[8,4,68,128]{3,2,1,0:T(8,128)(2,1)S(1)} fusion(bf16[68,8,4,4608]{3,0,2,1:T(8,128)(2,1)S(1)} %bitcast.258, bf16[4608,128]{1,0:T(8,128)(2,1)} %constant_dynamic-update-slice_fusion), kind=kOutput, calls=%fused_computation.173 | convolution fusion | flops 2567192576 | bytes 21790720 | tf_op jit(solution)/shard_map/dot_general | solution.py:23
  212.4 22.6 %dot_general.101 = bf16[51,8,4,4096]{3,2,1,0:T(4,128)(2,1)} reshape(bf16[51,32,4096]{2,1,0:T(8,128)(2,1)} %fusion.38) | data formatting | bytes 26738688 | tf_op jit(solution)/shard_map/dot_general | solution.py:23
  235.0 10.3 %fusion.54 = bf16[8,4,51,128]{3,1,0,2:T(4,128)(2,1)S(1)} fusion(bf16[51,8,4,4096]{3,2,1,0:T(4,128)(2,1)} %dot_general.101, bf16[4096,128]{1,0:T(8,128)(2,1)} %constant_dynamic-update-slice_fusion.2), kind=kOutput, calls=%fused_computation.174 | convolution fusion | flops 1711484928 | bytes 14835712 | tf_op jit(solution)/shard_map/dot_general | solution.py:23
  253.2 13.6 %collective-permute-done.42 = bf16[128,128]{1,0:T(8,128)(2,1)S(1)} collective-permute-done((bf16[128,128]{1,0:T(8,128)(2,1)S(1)}, bf16[128,128]{1,0:T(8,128)(2,1)S(1)}, u32[]{:S(2)}, u32[]{:S(2)}) %collective-permute-start.42) | collective-permute-done | bytes 32800 | tf_op jit(solution)/shard_map/ppermute | solution.py:99
  266.9 8.5 collective-permute-done.43
  350.4 19.4 %multiply_convert_fusion = (bf16[816,2048]{1,0:T(8,128)(2,1)S(1)}, f32[816,2048]{1,0:T(8,128)}, f32[816,2048]{1,0:T(8,128)}) fusion(bf16[512,512]{1,0:T(8,128)(2,1)S(1)} %copy-done.71, bf16[512,512]{1,0:T(8,128)(2,1)S(1)} %copy-done.70, bf16[512,512]{1,0:T(8,128)(2,1)S(1)} %copy-done.69, bf16[512,512]{1,0:T(8,128)(2,1)S(1)} %copy-done.68, ...), kind=kOutput, calls=%fused_computation.28 | convolution fusion | flops 1830379520 | bytes 20490624 | tf_op jit(solution)/shard_map/dot_general | solution.py:23
  373.6 7.2 add_convert_fusion
  445.6 18.4 %collective-permute-done.67 = f32[476,256]{1,0:T(8,128)} collective-permute-done((f32[476,256]{1,0:T(8,128)}, f32[476,256]{1,0:T(8,128)}, u32[]{:S(2)}, u32[]{:S(2)}) %collective-permute-start.67) | collective-permute-done | bytes 487456 | tf_op jit(solution)/shard_map/ppermute | solution.py:35
  491.9 21.0 %copy.121 = bf16[68,32,4608]{2,1,0:T(8,128)(2,1)} copy(bf16[68,32,4608]{2,0,1:T(8,128)(2,1)} %copy-done.11) | data formatting | bytes 40108032 | tf_op jit(solution)/shard_map/concatenate | solution.py:153
  518.0 6.4 dynamic_update_slice.196
  524.8 6.4 dynamic_update_slice.197
  538.0 6.4 dynamic_update_slice.199
  544.4 6.4 dynamic_update_slice.200
  551.3 6.4 dynamic_update_slice.201
  557.7 6.4 dynamic_update_slice.202
  564.3 6.4 dynamic_update_slice.203
  571.1 17.3 %fusion.56 = f32[68,32,4608]{2,1,0:T(8,128)} fusion(bf16[68,32,128]{2,1,0:T(8,128)(2,1)S(1)} %bitcast.272, bf16[4608,128]{1,0:T(8,128)(2,1)} %constant_dynamic-update-slice_fusion), kind=kOutput, calls=%fused_computation.176 | convolution fusion | flops 2566914048 | bytes 41844736 | tf_op jit(solution)/shard_map/dot_general | solution.py:31
  629.8 22.3 %dynamic_update_slice.204 = f32[144,32,512]{2,0,1:T(8,128)} dynamic-update-slice(f32[144,32,512]{2,0,1:T(8,128)} %broadcast_in_dim.247, f32[76,32,512]{2,0,1:T(8,128)} %copy.116, s32[]{:T(128)S(6)} %select_n.1414, s32[]{:T(128)} %constant.1016.clone.1, s32[]{:T(128)} %constant.1016.clone.1) | dynamic-update-slice | bytes 9961476 | tf_op jit(solution)/shard_map/dynamic_update_slice | solution.py:174
  659.9 12.2 %fusion.61 = f32[51,32,4096]{2,1,0:T(8,128)} fusion(bf16[51,32,128]{2,1,0:T(8,128)(2,1)S(1)} %bitcast.274, bf16[4096,128]{1,0:T(8,128)(2,1)} %constant_dynamic-update-slice_fusion.2), kind=kOutput, calls=%fused_computation.185 | convolution fusion | flops 1711276032 | bytes 28205056 | tf_op jit(solution)/shard_map/dot_general | solution.py:31
  725.6 53.8 %psum.7 = f32[6,512]{1,0:T(8,128)S(1)} all-reduce(f32[6,512]{1,0:T(8,128)S(1)} %stack.49), channel_id=1, replica_groups=mesh['dp'=8,'tensor'=4] {'dp','tensor'}, use_global_device_ids=true, to_apply=%region_38.39 | all-reduce | flops 3072 | bytes 24576 | tf_op jit(solution)/shard_map/psum | solution.py:348
  788.4 7.0 fusion.119
  796.8 16.2 %all-to-all-done.1 = bf16[8,476,128]{2,1,0:T(8,128)(2,1)} async-done(((bf16[8,476,128]{2,1,0:T(8,128)(2,1)}), bf16[8,476,128]{2,1,0:T(8,128)(2,1)}, u32[]{:S(2)}, u32[]{:S(2)}) %all-to-all-start.1) | async-done | bytes 974880 | tf_op jit(solution)/shard_map/all_to_all | solution.py:110
  818.8 10.2 %fusion.118 = f32[4608,128]{1,0:T(8,128)S(1)} fusion(bf16[2176,4608]{1,0:T(8,128)(2,1)} %bitcast.259, bf16[2176,128]{1,0:T(8,128)(2,1)} %bitcast.273), kind=kOutput, calls=%fused_computation.513 | convolution fusion | flops 2566914048 | bytes 22970368 | tf_op jit(solution)/shard_map/dot_general | solution.py:27
  844.1 8.4 reshape.948
  856.2 7.9 reshape.947
  864.2 9.4 add.1215
  899.9 16.2 %collective-permute-done.81 = bf16[3264,128]{1,0:T(8,128)(2,1)} collective-permute-done((bf16[3264,128]{1,0:T(8,128)(2,1)}, bf16[3264,128]{1,0:T(8,128)(2,1)}, u32[]{:S(2)}, u32[]{:S(2)}) %collective-permute-start.81) | collective-permute-done | bytes 835616 | tf_op jit(solution)/shard_map/ppermute | solution.py:35
  916.2 8.2 add_add_fusion
  926.1 27.7 %reduce-scatter.11.cloned.1.call-done = bf16[1024,128]{1,0:T(8,128)(2,1)} async-done(((bf16[8192,128]{1,0:T(8,128)(2,1)}), bf16[1024,128]{1,0:T(8,128)(2,1)}) %reduce-scatter.11.cloned.1.call-update) | async-done | bytes 262160 | tf_op jit(solution)/shard_map/reduce_scatter | solution.py:115
  (678 shorter events, 494.9 us)
Async XLA Ops:
  7.2 306.6 %all-gather.3.cloned.1.call-start = ((), (), s32[]{:S(2)}) async-start(), calls=%async_computation.8 | async-start | bytes 1769472 | tf_op jit(solution)/shard_map/all_gather | solution.py:213
  7.2 29.3 %collective-permute-start.3 = (bf16[768,128]{1,0:T(8,128)(2,1)}, bf16[768,128]{1,0:T(8,128)(2,1)}, u32[]{:S(2)}, u32[]{:S(2)}) collective-permute-start(bf16[768,128]{1,0:T(8,128)(2,1)} %param.66), channel_id=1, source_target_pairs={{0,8},{8,16},{16,24},{24,28},{28,20},{20,12},{12,4},{4,0},{1,9},{9... | collective-permute-start | bytes 589832 | tf_op jit(solution)/shard_map/ppermute | solution.py:99
  10.3 27.7 %collective-permute-start.4 = (bf16[768,128]{1,0:T(8,128)(2,1)}, bf16[768,128]{1,0:T(8,128)(2,1)}, u32[]{:S(2)}, u32[]{:S(2)}) collective-permute-start(bf16[768,128]{1,0:T(8,128)(2,1)} %param.66), channel_id=1, source_target_pairs={{8,0},{16,8},{24,16},{28,24},{20,28},{12,20},{4,12},{0,4},{9,1},{1... | collective-permute-start | bytes 589832 | tf_op jit(solution)/shard_map/ppermute | solution.py:102
  10.3 66.1 %collective-permute-start.1 = (bf16[3264,128]{1,0:T(8,128)(2,1)}, bf16[3264,128]{1,0:T(8,128)(2,1)S(1)}, u32[]{:S(2)}, u32[]{:S(2)}) collective-permute-start(bf16[3264,128]{1,0:T(8,128)(2,1)} %param.64), channel_id=1, source_target_pairs={{0,2},{1,3},{2,0},{3,1},{4,6},{5,7},{6,4},{7,5},{8,10},{9,11},{10,... | collective-permute-start | bytes 2506760 | tf_op jit(solution)/shard_map/ppermute | solution.py:35
  12.3 72.7 %collective-permute-start = (bf16[3264,128]{1,0:T(8,128)(2,1)}, bf16[3264,128]{1,0:T(8,128)(2,1)}, u32[]{:S(2)}, u32[]{:S(2)}) collective-permute-start(bf16[3264,128]{1,0:T(8,128)(2,1)} %param.64), channel_id=1, source_target_pairs={{0,1},{1,0},{2,3},{3,2},{4,5},{5,4},{6,7},{7,6},{8,9},{9,8},{10,11... | collective-permute-start | bytes 2506760 | tf_op jit(solution)/shard_map/ppermute | solution.py:35
  12.3 28.3 %collective-permute-start.10 = (bf16[1024,128]{1,0:T(8,128)(2,1)}, bf16[1024,128]{1,0:T(8,128)(2,1)S(1)}, u32[]{:S(2)}, u32[]{:S(2)}) collective-permute-start(bf16[1024,128]{1,0:T(8,128)(2,1)} %param.69), channel_id=1, source_target_pairs={{0,8},{8,16},{16,24},{24,28},{28,20},{20,12},{12,4},{4,0},{1,9},{9... | collective-permute-start | bytes 786440 | tf_op jit(solution)/shard_map/ppermute | solution.py:99
  13.9 305.4 %all-gather.5.cloned.1.call-start = ((), (), s32[]{:S(2)}) async-start(), calls=%async_computation.9 | async-start | bytes 2359296 | tf_op jit(solution)/shard_map/all_gather | solution.py:214
  106.9 171.4 %collective-permute-start.30 = (f32[6,128]{1,0:T(8,128)S(1)}, f32[6,128]{1,0:T(8,128)S(1)}, u32[]{:S(2)}, u32[]{:S(2)}) collective-permute-start(f32[6,128]{1,0:T(8,128)S(1)} %stack.44), channel_id=1, source_target_pairs={{0,2},{1,3},{2,0},{3,1},{4,6},{5,7},{6,4},{7,5},{8,10},{9,11},{10,... | collective-permute-start | bytes 9224 | tf_op jit(solution)/shard_map/ppermute | solution.py:35
  107.5 173.6 %collective-permute-start.29 = (f32[6,128]{1,0:T(8,128)S(1)}, f32[6,128]{1,0:T(8,128)S(1)}, u32[]{:S(2)}, u32[]{:S(2)}) collective-permute-start(f32[6,128]{1,0:T(8,128)S(1)} %stack.44), channel_id=1, source_target_pairs={{0,1},{1,0},{2,3},{3,2},{4,5},{5,4},{6,7},{7,6},{8,9},{9,8},{10,11... | collective-permute-start | bytes 9224 | tf_op jit(solution)/shard_map/ppermute | solution.py:35
  107.5 40.9 %collective-permute-start.38 = (bf16[128,128]{1,0:T(8,128)(2,1)S(1)}, bf16[128,128]{1,0:T(8,128)(2,1)S(1)}, u32[]{:S(2)}, u32[]{:S(2)}) collective-permute-start(bf16[128,128]{1,0:T(8,128)(2,1)S(1)} %copy-done.84), channel_id=1, source_target_pairs={{0,8},{8,16},{16,24},{24,28},{28,20},{20,12},{12,4},{4,0},{1,9},{9... | collective-permute-start | bytes 98312 | tf_op jit(solution)/shard_map/ppermute | solution.py:99
  148.4 150.2 %collective-permute-start.49 = (bf16[512,512]{1,0:T(8,128)(2,1)}, bf16[512,512]{1,0:T(8,128)(2,1)}, u32[]{:S(2)}, u32[]{:S(2)}) collective-permute-start(bf16[512,512]{1,0:T(8,128)(2,1)} %param.73), channel_id=1, source_target_pairs={{0,2},{1,3},{2,0},{3,1},{4,6},{5,7},{6,4},{7,5},{8,10},{9,11},{10,... | collective-permute-start | bytes 1572872 | tf_op jit(solution)/shard_map/ppermute | solution.py:35
  153.9 147.4 %collective-permute-start.52 = (bf16[512,512]{1,0:T(8,128)(2,1)}, bf16[512,512]{1,0:T(8,128)(2,1)}, u32[]{:S(2)}, u32[]{:S(2)}) collective-permute-start(bf16[512,512]{1,0:T(8,128)(2,1)} %param.74), channel_id=1, source_target_pairs={{0,2},{1,3},{2,0},{3,1},{4,6},{5,7},{6,4},{7,5},{8,10},{9,11},{10,... | collective-permute-start | bytes 1572872 | tf_op jit(solution)/shard_map/ppermute | solution.py:35
  154.5 96.7 %collective-permute-start.41 = (bf16[128,128]{1,0:T(8,128)(2,1)S(1)}, bf16[128,128]{1,0:T(8,128)(2,1)S(1)}, u32[]{:S(2)}, u32[]{:S(2)}) collective-permute-start(bf16[128,128]{1,0:T(8,128)(2,1)S(1)} %collective-permute-done.39), channel_id=1, source_target_pairs={{8,0},{16,8},{24,16},{28,24},{20,28},{12,20},{4,12},{0,4},{9,1},{1... | collective-permute-start | bytes 98312 | tf_op jit(solution)/shard_map/ppermute | solution.py:102
  246.6 56.1 %all-to-all-start = ((bf16[8,476,128]{2,1,0:T(8,128)(2,1)}), bf16[8,476,128]{2,1,0:T(8,128)(2,1)S(1)}, u32[]{:S(2)}, u32[]{:S(2)}) async-start(bf16[8,476,128]{2,1,0:T(8,128)(2,1)} %copy.105), calls=%async_computation | async-start | bytes 1966080 | tf_op jit(solution)/shard_map/all_to_all | solution.py:110
  251.1 473.0 %reduce-scatter.15.cloned.1.call-start = ((), (), s32[]{:S(2)}) async-start(), calls=%async_computation.14 | async-start | bytes 294912 | tf_op jit(solution)/shard_map/reduce_scatter | solution.py:115
  410.6 54.8 %collective-permute-start.85 = (bf16[512,512]{1,0:T(8,128)(2,1)}, bf16[512,512]{1,0:T(8,128)(2,1)}, u32[]{:S(2)}, u32[]{:S(2)}) collective-permute-start(bf16[512,512]{1,0:T(8,128)(2,1)} %get-tuple-element.341), channel_id=1, source_target_pairs={{0,1},{1,0},{2,3},{3,2},{4,5},{5,4},{6,7},{7,6},{8,9},{9,8},{10,11... | collective-permute-start | bytes 1572872 | tf_op jit(solution)/shard_map/ppermute | solution.py:35
  436.8 28.6 %collective-permute-start.87 = (bf16[512,512]{1,0:T(8,128)(2,1)}, bf16[512,512]{1,0:T(8,128)(2,1)}, u32[]{:S(2)}, u32[]{:S(2)}) collective-permute-start(bf16[512,512]{1,0:T(8,128)(2,1)} %add_convert_fusion.11), channel_id=1, source_target_pairs={{0,2},{1,3},{2,0},{3,1},{4,6},{5,7},{6,4},{7,5},{8,10},{9,11},{10,... | collective-permute-start | bytes 1572872 | tf_op jit(solution)/shard_map/ppermute | solution.py:35
  442.0 26.6 %collective-permute-start.88 = (bf16[512,512]{1,0:T(8,128)(2,1)}, bf16[512,512]{1,0:T(8,128)(2,1)}, u32[]{:S(2)}, u32[]{:S(2)}) collective-permute-start(bf16[512,512]{1,0:T(8,128)(2,1)} %get-tuple-element.343), channel_id=1, source_target_pairs={{0,1},{1,0},{2,3},{3,2},{4,5},{5,4},{6,7},{7,6},{8,9},{9,8},{10,11... | collective-permute-start | bytes 1572872 | tf_op jit(solution)/shard_map/ppermute | solution.py:35
  442.2 32.1 %collective-permute-start.90 = (bf16[512,512]{1,0:T(8,128)(2,1)}, bf16[512,512]{1,0:T(8,128)(2,1)}, u32[]{:S(2)}, u32[]{:S(2)}) collective-permute-start(bf16[512,512]{1,0:T(8,128)(2,1)} %add_convert_fusion.9), channel_id=1, source_target_pairs={{0,2},{1,3},{2,0},{3,1},{4,6},{5,7},{6,4},{7,5},{8,10},{9,11},{10,... | collective-permute-start | bytes 1572872 | tf_op jit(solution)/shard_map/ppermute | solution.py:35
  445.4 385.2 %reduce-scatter.17.cloned.1.call-start = ((), (), s32[]{:S(2)}) async-start(), calls=%async_computation.15 | async-start | bytes 1179648 | tf_op jit(solution)/shard_map/reduce_scatter | solution.py:115
  477.1 405.3 %reduce-scatter.9.cloned.1.call-start = ((), (), s32[]{:S(2)}) async-start(), calls=%async_computation.11 | async-start | bytes 1769472 | tf_op jit(solution)/shard_map/reduce_scatter | solution.py:115
  486.8 26.1 %collective-permute-start.72 = (bf16[476,128]{1,0:T(8,128)(2,1)S(1)}, bf16[476,128]{1,0:T(8,128)(2,1)S(1)}, u32[]{:S(2)}, u32[]{:S(2)}) collective-permute-start(bf16[476,128]{1,0:T(8,128)(2,1)S(1)} %collective-permute-done.70), channel_id=1, source_target_pairs={{8,0},{16,8},{24,16},{28,24},{20,28},{12,20},{4,12},{0,4},{9,1},{1... | collective-permute-start | bytes 365576 | tf_op jit(solution)/shard_map/ppermute | solution.py:102
  512.9 38.2 %collective-permute-start.74 = (bf16[476,128]{1,0:T(8,128)(2,1)S(1)}, bf16[476,128]{1,0:T(8,128)(2,1)S(1)}, u32[]{:S(2)}, u32[]{:S(2)}) collective-permute-start(bf16[476,128]{1,0:T(8,128)(2,1)S(1)} %collective-permute-done.72), channel_id=1, source_target_pairs={{8,0},{16,8},{24,16},{28,24},{20,28},{12,20},{4,12},{0,4},{9,1},{1... | collective-permute-start | bytes 365576 | tf_op jit(solution)/shard_map/ppermute | solution.py:102
  514.2 49.9 %collective-permute-start.75 = (bf16[476,128]{1,0:T(8,128)(2,1)S(1)}, bf16[476,128]{1,0:T(8,128)(2,1)S(1)}, u32[]{:S(2)}, u32[]{:S(2)}) collective-permute-start(bf16[476,128]{1,0:T(8,128)(2,1)S(1)} %collective-permute-done.73), channel_id=1, source_target_pairs={{0,8},{8,16},{16,24},{24,28},{28,20},{20,12},{12,4},{4,0},{1,9},{9... | collective-permute-start | bytes 365576 | tf_op jit(solution)/shard_map/ppermute | solution.py:99
  517.6 380.4 %reduce-scatter.13.cloned.1.call-start = ((), (), s32[]{:S(2)}) async-start(), calls=%async_computation.13 | async-start | bytes 2359296 | tf_op jit(solution)/shard_map/reduce_scatter | solution.py:115
  717.9 62.1 %collective-permute-start.76 = (bf16[8,476,128]{2,0,1:T(8,128)(2,1)}, bf16[8,476,128]{2,0,1:T(8,128)(2,1)}, u32[]{:S(2)}, u32[]{:S(2)}) collective-permute-start(bf16[8,476,128]{2,0,1:T(8,128)(2,1)} %get-tuple-element.319), channel_id=1, source_target_pairs={{0,1},{1,0},{2,3},{3,2},{4,5},{5,4},{6,7},{7,6},{8,9},{9,8},{10,11... | collective-permute-start | bytes 2924552 | tf_op jit(solution)/shard_map/ppermute | solution.py:35
  721.6 58.4 %collective-permute-start.78 = (bf16[8,476,128]{2,0,1:T(8,128)(2,1)}, bf16[8,476,128]{2,0,1:T(8,128)(2,1)S(1)}, u32[]{:S(2)}, u32[]{:S(2)}) collective-permute-start(bf16[8,476,128]{2,0,1:T(8,128)(2,1)} %add_convert_fusion.2), channel_id=1, source_target_pairs={{0,2},{1,3},{2,0},{3,1},{4,6},{5,7},{6,4},{7,5},{8,10},{9,11},{10,... | collective-permute-start | bytes 2924552 | tf_op jit(solution)/shard_map/ppermute | solution.py:35
  783.5 29.5 %all-to-all-start.1 = ((bf16[8,476,128]{2,1,0:T(8,128)(2,1)}), bf16[8,476,128]{2,1,0:T(8,128)(2,1)}, u32[]{:S(2)}, u32[]{:S(2)}) async-start(bf16[8,476,128]{2,1,0:T(8,128)(2,1)} %copy.120), calls=%async_computation.1 | async-start | bytes 1966080 | tf_op jit(solution)/shard_map/all_to_all | solution.py:110
  788.4 136.0 %reduce-scatter.7.cloned.1.call-start = ((), (), s32[]{:S(2)}) async-start(), calls=%async_computation.10 | async-start | bytes 1769472 | tf_op jit(solution)/shard_map/reduce_scatter | solution.py:115
  818.8 135.0 %reduce-scatter.11.cloned.1.call-start = ((), (), s32[]{:S(2)}) async-start(), calls=%async_computation.12 | async-start | bytes 2359296 | tf_op jit(solution)/shard_map/reduce_scatter | solution.py:115
  836.0 48.1 %collective-permute-start.93 = (bf16[128,512]{1,0:T(8,128)(2,1)}, bf16[128,512]{1,0:T(8,128)(2,1)S(1)}, u32[]{:S(2)}, u32[]{:S(2)}) collective-permute-start(bf16[128,512]{1,0:T(8,128)(2,1)} %collective-permute-done.91), channel_id=1, source_target_pairs={{0,8},{8,16},{16,24},{24,28},{28,20},{20,12},{12,4},{4,0},{1,9},{9... | collective-permute-start | bytes 393224 | tf_op jit(solution)/shard_map/ppermute | solution.py:99
  838.5 46.0 %collective-permute-start.94 = (bf16[128,512]{1,0:T(8,128)(2,1)}, bf16[128,512]{1,0:T(8,128)(2,1)S(1)}, u32[]{:S(2)}, u32[]{:S(2)}) collective-permute-start(bf16[128,512]{1,0:T(8,128)(2,1)} %collective-permute-done.92), channel_id=1, source_target_pairs={{8,0},{16,8},{24,16},{28,24},{20,28},{12,20},{4,12},{0,4},{9,1},{1... | collective-permute-start | bytes 393224 | tf_op jit(solution)/shard_map/ppermute | solution.py:102
  (182 other events, 1851.3 us)
Sparse Core Ops, SparseCore 0:
  14.0 51.2 all-gather.2
  109.0 53.3 all-gather.4
  445.5 60.9 reduce-scatter.14
  510.3 62.6 reduce-scatter.16
  577.2 64.8 reduce-scatter.8
  710.8 69.0 reduce-scatter.12
  818.9 64.3 reduce-scatter.6
  887.2 66.5 reduce-scatter.10

commit v2 on v1

v2 whole, which is shorter than its diff:
```python
from functools import partial

import jax
import jax.numpy as jnp
from jax import lax
from jax.experimental import pallas as pl
from jax.experimental.pallas import tpu as pltpu
from jax.sharding import PartitionSpec as P

D = 512
SA = 12
SB = 16
IN_LEN = 96
L = 816
MA = 68
MB = 51


EPS = 1e-05
BF = jnp.bfloat16
F32 = jnp.float32


XOR = (0, 2, 1, 3)
PARAMS = pltpu.CompilerParams(vmem_limit_bytes=56 << 20)


def dot(left, right):
    return jnp.dot(left, right, preferred_element_type=F32)


def dot_tn(left, right):
    return lax.dot_general(left, right, (((0,), (0,)), ((), ())), preferred_element_type=F32)


def dot_nt(left, right):
    return lax.dot_general(left, right, (((1,), (1,)), ((), ())), preferred_element_type=F32)


def swap(value, mask):
    return lax.ppermute(value, "tensor", [(i, i ^ mask) for i in range(4)])


def by_xor(blocks):
    t = lax.axis_index("tensor")
    low = (t % 2) == 0
    high = (t // 2) == 0
    mid = [jnp.where(low, blocks[k], blocks[k ^ 1]) for k in range(4)]
    return [jnp.where(high, mid[k], mid[k ^ 2]) for k in range(4)]


def lanes(value):
    width = value.shape[1] // 4
    return [value[:, i * width : (i + 1) * width] for i in range(4)]


def own_lanes(value):
    width = value.shape[1] // 4
    return lax.dynamic_slice_in_dim(value, lax.axis_index("tensor") * width, width, 1)


def lane_at(t, k, width=128):
    return pl.ds(pl.multiple_of((t ^ k) * width, width), width)


def ring_order(count):
    return list(range(0, count, 2)) + list(range(1, count, 2))[::-1]


def ring_gather(value):
    count = lax.axis_size("dp")
    order = ring_order(count)
    table = jnp.array(order, jnp.int32)
    place = jnp.array([order.index(i) for i in range(count)], jnp.int32)[lax.axis_index("dp")]
    up = [(order[i], order[(i + 1) % count]) for i in range(count)]
    down = [(b, a) for a, b in up]
    result = jnp.zeros((count,) + value.shape, value.dtype)
    result = lax.dynamic_update_index_in_dim(result, value, lax.axis_index("dp"), 0)
    ahead = behind = value
    for step in range(1, count // 2 + 1):
        ahead = lax.ppermute(ahead, "dp", up)
        result = lax.dynamic_update_index_in_dim(result, ahead, table[(place - step) % count], 0)
        if step <= (count - 1) // 2:
            behind = lax.ppermute(behind, "dp", down)
            result = lax.dynamic_update_index_in_dim(
                result, behind, table[(place + step) % count], 0
            )
    return result


def ring_list(value):
    count = lax.axis_size("dp")
    order = ring_order(count)
    table = jnp.array(order, jnp.int32)
    place = jnp.array([order.index(i) for i in range(count)], jnp.int32)[lax.axis_index("dp")]
    up = [(order[i], order[(i + 1) % count]) for i in range(count)]
    down = [(b, a) for a, b in up]
    ahead = behind = value
    blocks, steps = [value], [0]
    for step in range(1, count // 2 + 1):
        ahead = lax.ppermute(ahead, "dp", up)
        blocks.append(ahead)
        steps.append(-step)
        if step <= (count - 1) // 2:
            behind = lax.ppermute(behind, "dp", down)
            blocks.append(behind)
            steps.append(step)
    return blocks, table[(place + jnp.array(steps, jnp.int32)) % count]


def four(value):
    across = swap(value, 2)
    return [value, across, swap(value, 1), swap(across, 1)]


def after(values, *events):
    return lax.optimization_barrier(tuple(values) + events)[: len(values)]


def exchange_sum(blocks):
    got = lax.all_to_all(blocks.astype(BF), "dp", 0, 0, tiled=True)
    return jnp.sum(got.astype(F32), axis=0)


def scatter_sum(value):
    return lax.psum_scatter(value.astype(BF), "dp", scatter_dimension=0, tiled=True).astype(F32)


def norm_forward(operand, gain_vec, bias_vec):
    row_mean = jnp.mean(operand, axis=1, keepdims=True)
    row_square = jnp.mean(operand * operand, axis=1, keepdims=True)
    inv_std = lax.rsqrt(row_square - row_mean * row_mean + EPS)
    normed = (operand - row_mean) * inv_std
    return (normed * gain_vec + bias_vec, (normed, inv_std))


def norm_backward(upstream, gain_vec, stored):
    normed, inv_std = stored
    scaled = upstream * gain_vec
    first_mean = jnp.mean(scaled, axis=1, keepdims=True)
    second_mean = jnp.mean(scaled * normed, axis=1, keepdims=True)
    result = inv_std * (scaled - first_mean - normed * second_mean)
    return (result, jnp.sum(upstream * normed, axis=0), jnp.sum(upstream, axis=0))


def tap_plan(rows_held, span_len):
    count = lax.axis_size("dp")
    taps = max(-(-(i * rows_held % D + rows_held) // D) for i in range(count))
    start = lax.axis_index("dp") * rows_held
    first = jnp.minimum(start // D, span_len - taps)
    return taps, start - first * D, span_len - taps - first


def xor_order(blocks):
    moved = by_xor(blocks)
    return [moved[0], moved[2], moved[1], moved[3]]


def natural_order(blocks):
    return by_xor([blocks[0], blocks[2], blocks[1], blocks[3]])


def tap_columns(weight, taps, offset):
    width = weight.shape[1]
    wide = lax.dynamic_update_slice_in_dim(jnp.zeros((taps * D, width), BF), weight, offset, 0)
    wide = wide.reshape(taps, 4, D // 4, width)
    wide = xor_order([wide[:, i] for i in range(4)])
    return jnp.concatenate([jnp.concatenate([b[j] for b in wide], axis=0) for j in range(taps)], axis=1)


def tap_rows(grad, rows_held, offset):
    quarter = D // 4
    blocks = [grad[:, i * quarter : (i + 1) * quarter] for i in range(4)]
    wide = jnp.concatenate(natural_order(blocks), axis=1)
    return lax.dynamic_slice_in_dim(wide.reshape(-1, grad.shape[2]), offset, rows_held, 0)


def step_of(rows, span):
    step = lax.broadcasted_iota(jnp.int32, (rows, 128), 0)
    for at in range(span, rows, span):
        step = step - jnp.where(step >= span, span, 0)
    return step


def iso_forward_kernel(spans, reach_ref, pair_ref, mate_ref, w_a_ref, w_b_ref, out_ref):
    base = 0
    for scale, w_ref in enumerate((w_a_ref, w_b_ref)):
        rows, span = spans[scale]
        step = step_of(rows, span)
        reach = reach_ref[scale]
        width = out_ref.shape[2]
        taps = w_ref.shape[1] // width
        for g in range(out_ref.shape[0]):
            x = jnp.concatenate(
                [pair_ref[g, base : base + rows, :], mate_ref[g, base : base + rows, :]], axis=1
            )
            z = jnp.dot(x, w_ref[...], preferred_element_type=F32)
            total = z[:, :width]
            for j in range(1, taps):
                total = jnp.where(step >= 1, pltpu.roll(total, 1, 0), 0.0)
                total = total + z[:, j * width : (j + 1) * width]
            total = jnp.where(step >= reach, pltpu.roll(total, reach, 0), 0.0)
            out_ref[g, base : base + rows, :] = total.astype(BF)
        base += rows


def iso_backward_kernel(
    spans, reach_ref, grad_ref, pair_ref, mate_ref, w_a_ref, w_b_ref, ga_ref, gb_ref, back_ref, cols_ref
):
    base = 0
    start = pl.program_id(0) == 0
    for scale, (w_ref, gw_ref) in enumerate(((w_a_ref, ga_ref), (w_b_ref, gb_ref))):
        rows, span = spans[scale]
        step = step_of(rows, span)
        reach = reach_ref[scale]
        width = grad_ref.shape[2]
        taps = w_ref.shape[1] // width
        count = grad_ref.shape[0]
        for g in range(count):
            part = grad_ref[g, base : base + rows, :].astype(F32)
            part = jnp.where(step + reach < span, pltpu.roll(part, jnp.where(reach > 0, rows - reach, 0), 0), 0.0)
            for j in range(taps - 1, -1, -1):
                cols_ref[g * rows : (g + 1) * rows, j * width : (j + 1) * width] = part.astype(BF)
                if j:
                    part = jnp.where(step + 1 < span, pltpu.roll(part, rows - 1, 0), 0.0)
            back = lax.dot_general(
                cols_ref[g * rows : (g + 1) * rows, : taps * width],
                w_ref[...],
                (((1,), (1,)), ((), ())),
                preferred_element_type=F32,
            )
            back_ref[g, base : base + rows, :] = back.astype(BF)
        for half, x_ref in enumerate((pair_ref, mate_ref)):
            x = jnp.concatenate([x_ref[g, base : base + rows, :] for g in range(count)], axis=0)
            grad = lax.dot_general(
                x,
                cols_ref[: count * rows, : taps * width],
                (((0,), (0,)), ((), ())),
                preferred_element_type=F32,
            )
            tall = x_ref.shape[2]
            for j in range(taps):
                at = (j, slice(half * tall, (half + 1) * tall))
                new = grad[:, j * width : (j + 1) * width]
                gw_ref[at] = jnp.where(start, new, gw_ref[at] + new)
        base += rows


def iso_forward(reach, pair_all, mate_all, wide_a, wide_b, spans):
    groups, rows, half = pair_all.shape
    width = half // 2
    several = 4
    whole = lambda array: pl.BlockSpec(array.shape, lambda i: (0,) * len(array.shape))
    block = lambda width: pl.BlockSpec((several, rows, width), lambda i: (i, 0, 0))
    flops = 2 * groups * sum(r * D * w.shape[1] for (r, _), w in zip(spans, (wide_a, wide_b)))
    return pl.pallas_call(
        partial(iso_forward_kernel, spans),
        grid=(groups // several,),
        in_specs=[
            pl.BlockSpec(memory_space=pltpu.SMEM),
            block(half),
            block(half),
            whole(wide_a),
            whole(wide_b),
        ],
        out_specs=block(width),
        out_shape=jax.ShapeDtypeStruct((groups, rows, width), BF),
        compiler_params=pltpu.CompilerParams(vmem_limit_bytes=50 << 20),
        cost_estimate=pl.CostEstimate(
            flops=flops, bytes_accessed=2 * groups * rows * (D + width), transcendentals=0
        ),
    )(reach, pair_all, mate_all, wide_a, wide_b)


def iso_backward(reach, grad_all, pair_all, mate_all, wide_a, wide_b, spans):
    groups, rows, half = pair_all.shape
    width = half // 2
    several = 4
    whole = lambda array: pl.BlockSpec(array.shape, lambda i: (0,) * len(array.shape))
    block = lambda width: pl.BlockSpec((several, rows, width), lambda i: (i, 0, 0))
    taps = [w.shape[1] // width for w in (wide_a, wide_b)]
    grads = [jax.ShapeDtypeStruct((n, D, width), F32) for n in taps]
    flops = 4 * groups * sum(r * D * w.shape[1] for (r, _), w in zip(spans, (wide_a, wide_b)))
    return pl.pallas_call(
        partial(iso_backward_kernel, spans),
        grid=(groups // several,),
        in_specs=[
            pl.BlockSpec(memory_space=pltpu.SMEM),
            block(width),
            block(half),
            block(half),
            whole(wide_a),
            whole(wide_b),
        ],
        out_specs=[whole(grads[0]), whole(grads[1]), block(D)],
        out_shape=grads + [jax.ShapeDtypeStruct((groups, rows, D), BF)],
        scratch_shapes=[pltpu.VMEM((several * max(r for r, _ in spans), max(taps) * width), BF)],
        compiler_params=pltpu.CompilerParams(vmem_limit_bytes=50 << 20),
        cost_estimate=pl.CostEstimate(
            flops=flops, bytes_accessed=4 * groups * rows * D, transcendentals=0
        ),
    )(reach, grad_all, pair_all, mate_all, wide_a, wide_b)


def total_over(value, axis, count):
    mask = 1
    while mask < count:
        value = value + lax.ppermute(value, axis, [(i, i ^ mask) for i in range(count)])
        mask *= 2
    return value


def whole(array):
    return pl.BlockSpec(array.shape, lambda *_: (0,) * len(array.shape))


def scalars():
    return pl.BlockSpec(memory_space=pltpu.SMEM)


def cost(flops, *arrays):
    size = sum(a.size * a.dtype.itemsize for a in arrays)
    return pl.CostEstimate(flops=int(flops), bytes_accessed=int(size), transcendentals=0)


def shape_of(*dims, kind=F32):
    return jax.ShapeDtypeStruct(dims, kind)


def assemble(out_ref, index_ref, refs):
    rows = refs[0].shape[0]
    for i, ref in enumerate(refs):
        out_ref[pl.ds(pl.multiple_of(index_ref[i] * rows, rows), rows), :] = ref[...]


def strided(ref, start, count, stride):
    parts = [ref[j, pl.ds(start, count, stride=stride), :] for j in range(ref.shape[0])]
    return jnp.concatenate(parts, axis=1).astype(BF)


def positions(rows_held, stride, count):
    taps = max(-(-(i * rows_held % D + rows_held) // D) for i in range(count))
    return taps, [min(i * rows_held // D, stride - taps) for i in range(count)]


def down_kernel(count, place_ref, index_ref, *refs):
    blocks, parts, refs = refs[:4], refs[4 : 4 + 2 * count], refs[4 + 2 * count :]
    act_ref, low_ref, full_ref, xa_ref, xb_ref, xs_ref, wa_ref, wb_ref = refs
    t = place_ref[1]
    rows = blocks[0].shape[0]
    for k, part in zip(XOR, blocks):
        value = part[...]
        xs_ref[t ^ k, :rows, :] = value.astype(F32)
        full_ref[:, lane_at(t, k)] = value
    xs_ref[:, rows:, :] = jnp.zeros((4, xs_ref.shape[1] - rows, 128), F32)
    assemble(wa_ref, index_ref, parts[:count])
    assemble(wb_ref, index_ref, [v.at[: wb_ref.shape[0] // count] for v in parts[count:]])
    for stride, weight, out_ref in ((SA, wa_ref, xa_ref), (SB, wb_ref, xb_ref)):
        size = -(-rows // stride // 16) * 16
        taps, starts = positions(weight.shape[0] // count, stride, count)
        for i, start in enumerate(starts):
            for j in range(taps):
                part = xs_ref[t, pl.ds(start + j, size, stride=stride), :]
                out_ref[i, j * size : (j + 1) * size, :] = part.astype(BF)
    base = 0
    for stride, weight in ((SA, wa_ref), (SB, wb_ref)):
        count = -(-rows // stride // 16) * 16
        total = jnp.zeros((count, weight.shape[1]), F32)
        for r in range(stride):
            window = strided(xs_ref, r, count, stride)
            total = total + dot(window, weight[r * D : (r + 1) * D, :])
        total = jnp.tanh(total)
        act_ref[base : base + count, :] = total
        low_ref[base : base + count, :] = total.astype(BF)
        base += count


def down_forward(place, index, blocks, parts, counts, small, tall):
    rows, width = blocks[0].shape
    count = len(parts) // 2
    taps_a, _ = positions(SA * D // count, SA, count)
    taps_b, _ = positions(SB * D // count, SB, count)
    out = [
        shape_of(small, width),
        shape_of(small, width, kind=BF),
        shape_of(rows, D, kind=BF),
        shape_of(count, taps_a * counts[0], width, kind=BF),
        shape_of(count, taps_b * counts[1], width, kind=BF),
    ]
    return pl.pallas_call(
        partial(down_kernel, len(parts) // 2),
        in_specs=[scalars()] * 2 + [whole(v) for v in (*blocks, *parts)],
        out_specs=[whole(v) for v in out],
        out_shape=out,
        scratch_shapes=[
            pltpu.VMEM((4, tall, 128), F32),
            pltpu.VMEM((SA * D, width), BF),
            pltpu.VMEM((SB * D, width), BF),
        ],
        compiler_params=PARAMS,
        cost_estimate=cost(4 * rows * D * width, *blocks, *parts, *out),
    )(place, index, *blocks, *parts)


def up_kernel(
    place_ref, own_ref, across_ref, mate_ref, last_ref, pair_ref, far_ref, vec_ref, w_ref,
    send_ref, ua_ref, ub_ref, mid_ref, normed_ref, inv_ref, act_ref, ups_ref,
):
    t = place_ref[1]
    act = jnp.tanh(
        jnp.concatenate([own_ref[...], across_ref[...], mate_ref[...], last_ref[...]], axis=1)
    )
    down = jnp.concatenate([pair_ref[0], far_ref[0]], axis=1).astype(F32)
    gain = jnp.concatenate([vec_ref[0:1, lane_at(t, k)] for k in XOR], axis=1)
    bias = jnp.concatenate([vec_ref[1:2, lane_at(t, k)] for k in XOR], axis=1)
    middle, (normed, inv_std) = norm_forward(act + down, gain, bias)
    middle = middle.astype(BF)
    for at, k in enumerate(XOR):
        mid_ref[:, lane_at(t, k)] = middle[:, at * 128 : (at + 1) * 128]
    normed_ref[...] = normed
    inv_ref[...] = jnp.broadcast_to(inv_std, inv_ref.shape)
    act_ref[...] = act[:, :128]
    part_rows = send_ref.shape[2]
    base = column = 0
    for scale, (stride, u_ref) in enumerate(((SA, ua_ref), (SB, ub_ref))):
        count = u_ref.shape[0]
        wide = u_ref.shape[1]
        up = jnp.tanh(dot(mid_ref[base : base + count, :], w_ref[:, column : column + wide]))
        u_ref[...] = up
        for r in range(stride):
            ups_ref[pl.ds(r, count, stride=stride), :] = up[:, r * 128 : (r + 1) * 128]
        for j in range(4):
            send_ref[j, scale] = ups_ref[j * part_rows : (j + 1) * part_rows, :].astype(BF)
        base += count
        column += wide


def up_forward(place, blocks, pair_all, far_all, vec, weight, counts, part_rows, tall):
    small, width = blocks[0].shape
    out = [
        shape_of(4, 2, part_rows, width, kind=BF),
        shape_of(counts[0], SA * width),
        shape_of(counts[1], SB * width),
        shape_of(small, D, kind=BF),
        shape_of(small, D),
        shape_of(small, width),
        shape_of(small, width),
    ]
    group = pl.BlockSpec((1,) + pair_all.shape[1:], lambda i, place: (place[0], 0, 0))
    return pl.pallas_call(
        up_kernel,
        grid_spec=pltpu.PrefetchScalarGridSpec(
            num_scalar_prefetch=1,
            grid=(1,),
            in_specs=[whole(v) for v in blocks] + [group, group, whole(vec), whole(weight)],
            out_specs=[whole(v) for v in out],
            scratch_shapes=[pltpu.VMEM((tall, width), F32)],
        ),
        out_shape=out,
        compiler_params=PARAMS,
        cost_estimate=cost(2 * small * D * weight.shape[1] // 2, weight, *out),
    )(place, *blocks, pair_all, far_all, vec, weight)


def rows_kernel(
    place_ref, horizon_ref, up_ref, x_ref, cot_ref, vec_ref, *refs
):
    weights, merges = refs[:4], refs[4:8]
    out_ref, send_ref, keep_ref, give_ref, sums_ref, wm_ref, slope_ref = refs[8:15]
    hid_ref, hpre_ref, first_ref, feed_ref, pair_ref, merged_ref = refs[15:]
    t = place_ref[1]
    step = pl.program_id(0)
    tile = x_ref.shape[0]
    at = pl.ds(pl.multiple_of(step * tile, tile), tile)
    @pl.when(step == 0)
    def _():
        for k, merge in zip(XOR, merges):
            wm_ref[:, lane_at(t, k)] = merge[...]

    vec = [vec_ref[i : i + 1, :] for i in range(6)]
    x = x_ref[...].astype(F32)
    stored = []
    for scale in range(2):
        up = jnp.concatenate([up_ref[j, scale] for j in range(4)], axis=1).astype(F32)
        branch, kept = norm_forward(up + x, vec[0], vec[1])
        stored.append(kept)
        pair_ref[at, scale * D : (scale + 1) * D] = branch.astype(BF)
    merged = dot(pair_ref[at, :], wm_ref[...])
    first, first_kept = norm_forward(merged, vec[2], vec[3])
    first_ref[at, :] = first.astype(BF)
    feed = jnp.zeros((tile, D), F32)
    for k in range(4):
        pre = dot(first_ref[at, :], weights[k][:D, :])
        chance = 0.5 * (1.0 + lax.erf(pre * (0.5**0.5)))
        slope_ref[:, k * D : (k + 1) * D] = chance + pre * (
            jnp.exp(-0.5 * pre * pre) * 0.3989422804014327
        )
        hid_ref[at, k * D : (k + 1) * D] = (pre * chance).astype(BF)
        feed = feed + dot(hid_ref[at, k * D : (k + 1) * D], weights[k][D:, :])
    last, last_kept = norm_forward(merged + feed, vec[4], vec[5])
    time = step * tile + lax.broadcasted_iota(jnp.int32, (tile, 128), 0)
    mask = (time < IN_LEN + horizon_ref[t]).astype(F32)[:, :1]
    last = (last * mask).astype(BF)
    for j in range(4):
        out_ref[j] = last[:, j * 128 : (j + 1) * 128]
    upstream = jnp.concatenate([cot_ref[j] for j in range(4)], axis=1).astype(F32) * mask
    grad_sum, last_gain, last_bias = norm_backward(upstream, vec[4], last_kept)
    feed_ref[at, :] = grad_sum.astype(BF)
    grad_first = jnp.zeros((tile, D), F32)
    for k in range(4):
        grad_hidden = dot_nt(feed_ref[at, :], weights[k][D:, :])
        hpre_ref[at, k * D : (k + 1) * D] = (
            grad_hidden * slope_ref[:, k * D : (k + 1) * D]
        ).astype(BF)
        grad_first = grad_first + dot_nt(hpre_ref[at, k * D : (k + 1) * D], weights[k][:D, :])
    grad_merged, first_gain, first_bias = norm_backward(grad_first, vec[2], first_kept)
    merged_ref[at, :] = (grad_merged + grad_sum).astype(BF)
    gains = jnp.zeros((D,), F32)
    biases = jnp.zeros((D,), F32)
    for scale in range(2):
        grad_branch = dot_nt(merged_ref[at, :], wm_ref[scale * D : (scale + 1) * D, :])
        grad, gain, bias = norm_backward(grad_branch, vec[0], stored[scale])
        gains, biases = gains + gain, biases + bias
        grad = grad.astype(BF)
        for j in range(4):
            send_ref[j, scale] = grad[:, j * 128 : (j + 1) * 128]
    sums = (gains, biases, first_gain, first_bias, last_gain, last_bias)
    sums = jnp.concatenate([v[None, :] for v in sums] + [jnp.zeros((2, D), F32)], axis=0)
    sums_ref[...] = jnp.where(step == 0, sums, sums_ref[...] + sums)

    @pl.when(step == pl.num_programs(0) - 1)
    def _():
        wide = keep_ref.shape[1] // 2
        for i, (k, ref) in enumerate(zip(XOR, (keep_ref, keep_ref, give_ref, give_ref))):
            block = slice(i * D, (i + 1) * D)
            to = i % 2 * wide
            ref[:D, to : to + D] = dot_tn(first_ref[...], hpre_ref[:, block]).astype(BF)
            ref[D:, to : to + D] = dot_tn(hid_ref[:, block], feed_ref[...]).astype(BF)
            ref[:, to + D : to + wide] = dot_tn(
                pair_ref[...], merged_ref[:, lane_at(t, k)]
            ).astype(BF)


def rows_step(place, horizon, up_rows, x_full, cot_rows, vec, weights, merges):
    part_rows, width = cot_rows.shape[1:]
    steps = 3
    tile = part_rows // steps
    tall, wide = weights[0].shape[0], weights[0].shape[1] + width
    out = [
        shape_of(4, part_rows, width, kind=BF),
        shape_of(4, 2, part_rows, width, kind=BF),
        shape_of(tall, 2 * wide, kind=BF),
        shape_of(tall, 2 * wide, kind=BF),
        shape_of(8, D),
    ]
    three = pl.BlockSpec((4, tile, width), lambda i, place: (0, i, 0))
    four = pl.BlockSpec((4, 2, tile, width), lambda i, place: (0, 0, i, 0))
    once = lambda v: pl.BlockSpec(
        v.shape, lambda *_: (0,) * len(v.shape), pipeline_mode=pl.Buffered(1)
    )
    return pl.pallas_call(
        rows_kernel,
        grid_spec=pltpu.PrefetchScalarGridSpec(
            num_scalar_prefetch=1,
            grid=(steps,),
            in_specs=[
                scalars(),
                four,
                pl.BlockSpec((tile, D), lambda i, place: (place[1] * steps + i, 0)),
                three,
                whole(vec),
                *[once(v) for v in weights + merges],
            ],
            out_specs=[three, four, whole(out[2]), whole(out[3]), whole(out[4])],
            scratch_shapes=[
                pltpu.VMEM((2 * D, D), BF),
                pltpu.VMEM((tile, 4 * D), F32),
                pltpu.VMEM((part_rows, 4 * D), BF),
                pltpu.VMEM((part_rows, 4 * D), BF),
                pltpu.VMEM((part_rows, D), BF),
                pltpu.VMEM((part_rows, D), BF),
                pltpu.VMEM((part_rows, 2 * D), BF),
                pltpu.VMEM((part_rows, D), BF),
            ],
        ),
        out_shape=out,
        compiler_params=PARAMS,
        cost_estimate=cost(6 * part_rows * D * 10 * D, *weights, *merges, *out),
    )(place, horizon, up_rows, x_full, cot_rows, vec, *weights, *merges)


def up_back_kernel(
    place_ref, res_ref, ua_ref, ub_ref, mid_ref, w_ref, keep_ref, give_ref, grad_ref, rs_ref, cols_ref, part_ref
):
    t = place_ref[1]
    part_rows = res_ref.shape[2]
    rows = 4 * part_rows
    rs_ref[rows:, :] = jnp.zeros((rs_ref.shape[0] - rows, 128), F32)
    base = column = 0
    for scale, (stride, u_ref) in enumerate(((SA, ua_ref), (SB, ub_ref))):
        count, wide = u_ref.shape
        for j in range(4):
            rs_ref[j * part_rows : (j + 1) * part_rows, :] = res_ref[j, scale].astype(F32)
        for r in range(stride):
            up = u_ref[:, r * 128 : (r + 1) * 128]
            grad = rs_ref[pl.ds(r, count, stride=stride), :] * (1.0 - up * up)
            cols_ref[:count, r * 128 : (r + 1) * 128] = grad.astype(BF)
        grad = cols_ref[:count, :wide]
        part_ref[base : base + count, :] = dot_nt(grad, w_ref[:, column : column + wide])
        grad_ref[:, column : column + wide] = dot_tn(mid_ref[base : base + count, :], grad).astype(BF)
        base += count
        column += wide
    for slot, ref in enumerate((keep_ref, give_ref)):
        for at in range(2):
            ref[:, at * 128 : (at + 1) * 128] = part_ref[:, lane_at(t, XOR[2 * slot + at])]


def up_backward(place, res, ua, ub, mid, weight, tall):
    small = mid.shape[0]
    width = res.shape[3]
    out = [
        shape_of(small, 2 * width),
        shape_of(small, 2 * width),
        shape_of(D, weight.shape[1], kind=BF),
    ]
    return pl.pallas_call(
        up_back_kernel,
        in_specs=[scalars()] + [whole(v) for v in (res, ua, ub, mid, weight)],
        out_specs=[whole(v) for v in out],
        out_shape=out,
        scratch_shapes=[
            pltpu.VMEM((tall, width), F32),
            pltpu.VMEM((max(ua.shape[0], ub.shape[0]), max(ua.shape[1], ub.shape[1])), BF),
            pltpu.VMEM((small, D), F32),
        ],
        compiler_params=PARAMS,
        cost_estimate=cost(4 * small * D * weight.shape[1] // 2, res, ua, ub, mid, weight, *out),
    )(place, res, ua, ub, mid, weight)


def down_weight_kernel(place_ref, grad_ref, *refs):
    t = place_ref[1]
    several = grad_ref.shape[0]

    @pl.when(pl.program_id(0) == 0)
    def _():
        for out_ref in refs[8:]:
            out_ref[...] = jnp.zeros_like(out_ref)

    base = 0
    for blocks, out_ref in ((refs[:4], refs[8]), (refs[4:8], refs[9])):
        taps = out_ref.shape[0] // D
        count = blocks[0].shape[1] // taps
        for g in range(several):
            grad = grad_ref[g, base : base + count, :]
            for j in range(taps):
                at = slice(j * count, (j + 1) * count)
                x = jnp.concatenate([v[g, at, :] for v in blocks], axis=1)
                part = dot_tn(x, grad)
                for i, k in enumerate(XOR):
                    to = pl.ds(pl.multiple_of(j * D + (t ^ k) * 128, 128), 128)
                    out_ref[to, :] = out_ref[to, :] + part[i * 128 : (i + 1) * 128]
        base += count


def down_weight_grad(place, grad_all, blocks_a, blocks_b, counts):
    groups, small, width = grad_all.shape
    several = 4
    out = [
        shape_of(blocks[0].shape[1] // size * D, width)
        for blocks, size in zip((blocks_a, blocks_b), counts)
    ]
    block = lambda v: pl.BlockSpec((several,) + v.shape[1:], lambda i: (i, 0, 0))
    return pl.pallas_call(
        down_weight_kernel,
        grid=(groups // several,),
        in_specs=[scalars()] + [block(v) for v in (grad_all, *blocks_a, *blocks_b)],
        out_specs=[whole(v) for v in out],
        out_shape=out,
        compiler_params=PARAMS,
        cost_estimate=cost(8 * blocks_a[0].size * 4 * width // 2, grad_all, *blocks_a, *blocks_b),
    )(place, grad_all, *blocks_a, *blocks_b)


def down_input_kernel(count, place_ref, index_ref, grad_ref, *refs):
    parts, (keep_ref, give_ref, gx_ref, wa_ref, wb_ref) = refs[: 2 * count], refs[2 * count :]
    t = place_ref[1]
    rows = keep_ref.shape[0]
    assemble(wa_ref, index_ref, parts[:count])
    assemble(wb_ref, index_ref, [v.at[: wb_ref.shape[0] // count] for v in parts[count:]])
    base = 0
    for stride, weight in ((SA, wa_ref), (SB, wb_ref)):
        count = -(-rows // stride // 16) * 16
        grad = grad_ref[base : base + count, :]
        for r in range(stride):
            at = pl.ds(r, count, stride=stride)
            part = dot_nt(grad, weight[r * D : (r + 1) * D, :])
            for j in range(4):
                lane = slice(j * 128, (j + 1) * 128)
                if base:
                    gx_ref[j, at, :] = gx_ref[j, at, :] + part[:, lane]
                else:
                    gx_ref[j, at, :] = part[:, lane]
        base += count
    for slot, ref in enumerate((keep_ref, give_ref)):
        for i in range(2):
            ref[:, i * 128 : (i + 1) * 128] = gx_ref[t ^ XOR[2 * slot + i], :rows, :].astype(BF)


def down_input_grad(place, index, grad, parts, rows, tall):
    width = grad.shape[1]
    out = [shape_of(rows, 2 * width, kind=BF)] * 2
    return pl.pallas_call(
        partial(down_input_kernel, len(parts) // 2),
        in_specs=[scalars()] * 2 + [whole(v) for v in (grad, *parts)],
        out_specs=[whole(v) for v in out],
        out_shape=out,
        scratch_shapes=[
            pltpu.VMEM((4, tall, 128), F32),
            pltpu.VMEM((SA * D, width), BF),
            pltpu.VMEM((SB * D, width), BF),
        ],
        compiler_params=PARAMS,
        cost_estimate=cost(4 * rows * D * width, grad, *parts, *out),
    )(place, index, grad, *parts)


def body(
    signal,
    horizon,
    down_a,
    iso_a,
    up_a,
    down_b,
    iso_b,
    up_b,
    merge_w,
    ff_in,
    ff_out,
    norm_gain,
    norm_bias,
    first_gain,
    first_bias,
    last_gain,
    last_bias,
    cotangent,
):
    row_count, col_count = signal.shape
    part_rows = row_count // 4
    counts = (row_count // SA, -(-row_count // SB // 16) * 16)
    small = counts[0] + counts[1]
    tall = max(counts[0] * SA, counts[1] * SB)
    spans = ((counts[0], MA), (counts[1], MB))
    t = lax.axis_index("tensor")
    group = lax.axis_index("dp")
    place = jnp.stack([group, t]).astype(jnp.int32)

    x_blocks = four(signal)
    parts_a, index = ring_list(down_a)
    parts_b, _ = ring_list(jnp.concatenate([down_b, merge_w], axis=0))
    parts = parts_a + parts_b
    act, low, x_full, x_send_a, x_send_b = down_forward(
        place, index, x_blocks, parts, counts, small, tall
    )

    vec_own = jnp.stack(
        [norm_gain, norm_bias, first_gain, first_bias, last_gain, last_bias, last_bias, last_bias]
    )
    ff_own = jnp.concatenate([ff_in, ff_out], axis=0)
    vec_own, ff_own = after((vec_own, ff_own), x_blocks[1])
    vec = jnp.concatenate(natural_order(four(vec_own)), axis=1)
    ff_blocks = four(ff_own)
    up_held = jnp.concatenate(
        [up_a.reshape(up_a.shape[0], -1), up_b.reshape(up_b.shape[0], -1)], axis=1
    )
    (up_held,) = after((up_held,), *parts)
    w_up = lax.all_gather(up_held, "dp", axis=0, tiled=True)
    (cot_held,) = after((cotangent,), ff_blocks[1])
    cot_rows = lax.all_to_all(
        cot_held.reshape(4, part_rows, col_count), "tensor", 0, 0, tiled=True
    )
    taps_a, offset_a, reach_a = tap_plan(iso_a.shape[0], MA)
    taps_b, offset_b, reach_b = tap_plan(iso_b.shape[0], MB)
    reach = jnp.stack([reach_a, reach_b]).astype(jnp.int32)
    wide_a = tap_columns(iso_a, taps_a, offset_a)
    wide_b = tap_columns(iso_b, taps_b, offset_b)

    pair_all = ring_gather(jnp.concatenate([low, swap(low, 2)], axis=1))
    far_all = swap(pair_all, 1)
    merge_own = jnp.zeros((len(parts_b),) + merge_w.shape, BF)
    for i, part in enumerate(parts_b):
        merge_own = lax.dynamic_update_index_in_dim(
            merge_own, part[down_b.shape[0] :], index[i], 0
        )
    (merge_own,) = after((merge_own.reshape(2 * D, col_count),), pair_all)
    merge_blocks = four(merge_own)
    iso_pre = exchange_sum(iso_forward(reach, pair_all, far_all, wide_a, wide_b, spans))
    send, up_act_a, up_act_b, middle, normed, inv_std, iso_own = up_forward(
        place, four(iso_pre), pair_all, far_all, vec, w_up, counts, part_rows, tall
    )
    (x_send_a,) = after((x_send_a,), iso_pre)
    x_pos_a = lax.all_to_all(x_send_a, "dp", 0, 0, tiled=True)
    up_rows = lax.all_to_all(send, "tensor", 0, 0, tiled=True)
    x_pos_a, x_send_b = after((x_pos_a, x_send_b), up_rows)
    x_pos_a = four(x_pos_a)
    x_pos_b = lax.all_to_all(x_send_b, "dp", 0, 0, tiled=True)
    last, res_send, keep_w, give_w, sums = rows_step(
        place, horizon, up_rows, x_full, cot_rows, vec, ff_blocks, merge_blocks
    )
    res = lax.all_to_all(res_send, "tensor", 0, 0, tiled=True)
    keep_w, give_w = after((keep_w, give_w), res)
    sum_w = (keep_w.astype(F32) + swap(give_w, 1).astype(F32)).astype(BF)
    sum_w = lax.psum_scatter(sum_w, "dp", scatter_dimension=0, tiled=True)

    keep, give, grad_up = up_backward(place, res, up_act_a, up_act_b, middle, w_up, tall)
    sum_up = lax.psum_scatter(grad_up, "dp", scatter_dimension=0, tiled=True)
    keep = keep + swap(give, 1)
    crossed = swap(keep.astype(BF), 2).astype(F32)
    keep = keep + jnp.concatenate([crossed[:, col_count:], crossed[:, :col_count]], axis=1)
    grad_middle = jnp.concatenate([keep, swap(keep, 1)], axis=1)
    last, sums, x_pos_b = after((last, sums, x_pos_b), grad_middle)
    x_pos_b = four(x_pos_b)
    series_out = lax.all_to_all(last, "tensor", 0, 0, tiled=True).reshape(row_count, col_count)
    x_gain = jnp.concatenate(xor_order(lanes(vec[:1])), axis=1)
    grad_inner, gain_mid, bias_mid = norm_backward(grad_middle, x_gain, (normed, inv_std[:, :1]))
    grad_inner = grad_inner[:, :col_count]
    grad_ipre_all = ring_gather((grad_inner * (1.0 - iso_own * iso_own)).astype(BF))
    grad_wide_a, grad_wide_b, back = iso_backward(
        reach, grad_ipre_all, pair_all, far_all, wide_a, wide_b, spans
    )
    half = 2 * col_count
    kept = back[..., :half].astype(F32) + swap(back[..., half:], 1).astype(F32)
    kept = kept[..., :col_count] + swap(kept[..., col_count:].astype(BF), 2).astype(F32)
    grad_down = exchange_sum(kept)
    grad_dpre = ((grad_down + grad_inner) * (1.0 - act * act)).astype(BF)
    keep_x, give_x = down_input_grad(place, index, grad_dpre, parts, row_count, tall)
    grad_dpre_all = ring_gather(grad_dpre)
    grad_pos_a, grad_pos_b = down_weight_grad(place, grad_dpre_all, x_pos_a, x_pos_b, counts)
    count = lax.axis_size("dp")
    sum_down = []
    for grad, held, stride in ((grad_pos_a, down_a, SA), (grad_pos_b, down_b, SB)):
        rows_held = held.shape[0]
        starts = jnp.array(positions(rows_held, stride, count)[1], jnp.int32)
        offset = group * rows_held - starts[group] * D
        sum_down.append(lax.dynamic_slice_in_dim(grad, offset, rows_held, 0))
    sum_down_a, sum_down_b = sum_down
    keep_x = keep_x.astype(F32) + swap(give_x, 1).astype(F32)
    grad_input = keep_x[:, :col_count] + swap(keep_x[:, col_count:].astype(BF), 2).astype(F32)
    res = res.astype(F32)
    grad_input = grad_input + (res[:, 0] + res[:, 1]).reshape(row_count, col_count)

    grad_iso_a = tap_rows(grad_wide_a, iso_a.shape[0], offset_a)
    grad_iso_b = tap_rows(grad_wide_b, iso_b.shape[0], offset_b)
    (sum_w,) = after((sum_w,), back)
    wide = D + col_count
    sum_w = sum_w[:, :wide].astype(F32) + swap(sum_w[:, wide:], 2).astype(F32)
    sum_merge = sum_w[:, D:]
    ff_total = lax.all_gather(sum_w[:, :D].astype(BF), "dp", axis=0, tiled=True)
    sum_up, ff_total = after((sum_up, ff_total), give_x)
    ff_total = ff_total.astype(F32)
    sum_up = sum_up.astype(F32)
    sum_up_a = sum_up[:, : SA * col_count].reshape(up_a.shape)
    sum_up_b = sum_up[:, SA * col_count :].reshape(up_b.shape)
    sums = total_over(sums, "tensor", 4)
    own = jnp.stack([gain_mid[:col_count], bias_mid[:col_count]])
    own = jnp.pad(own, ((0, 6), (0, 0)))
    sums = total_over(own_lanes(sums) + own, "dp", lax.axis_size("dp"))
    return (
        series_out,
        grad_input,
        sum_down_a,
        grad_iso_a,
        sum_up_a,
        sum_down_b,
        grad_iso_b,
        sum_up_b,
        sum_merge,
        ff_total[:D],
        ff_total[D:],
        sums[0],
        sums[1],
        sums[2],
        sums[3],
        sums[4],
        sums[5],
    )


def solution(mesh):
    in_specs = (
        P("dp", "tensor"),
        P("dp"),
        P("dp", "tensor"),
        P("dp", "tensor"),
        P("dp", None, "tensor"),
        P("dp", "tensor"),
        P("dp", "tensor"),
        P("dp", None, "tensor"),
        P("dp", "tensor"),
        P(None, "tensor"),
        P("tensor", None),
        P("tensor"),
        P("tensor"),
        P("tensor"),
        P("tensor"),
        P("tensor"),
        P("tensor"),
        P("dp", "tensor"),
    )
    out_specs = (
        P("dp", "tensor"),
        P("dp", "tensor"),
        P("dp", "tensor"),
        P("dp", "tensor"),
        P("dp", None, "tensor"),
        P("dp", "tensor"),
        P("dp", "tensor"),
        P("dp", None, "tensor"),
        P("dp", "tensor"),
        P(None, "tensor"),
        P("tensor", None),
        P("tensor"),
        P("tensor"),
        P("tensor"),
        P("tensor"),
        P("tensor"),
        P("tensor"),
    )
    return jax.shard_map(body, mesh=mesh, in_specs=in_specs, out_specs=out_specs, check_vma=False)
```

time: 975 us -> 616 us (0.63)
  local copies, waits for them, and re-layouts: 257 us -> 51.5 us
  matrix products: 150 us -> 0 us
  other arithmetic: 151 us -> 37.9 us
  Pallas kernels: 0 us -> 97.7 us
  blocking collectives: 53.8 us -> 25.7 us
  starting transfers between devices: 89.1 us -> 111 us
  between operations: 35.3 us -> 49.8 us
    dot_general x27 -> x0, matrix products: 150 us -> none  [the longest x9 65 us: matmul(): return jnp.dot(left, right, preferred_element_type=F32)]
    pallas_call x0 -> x8, Pallas kernels: none -> 97.7 us  [the longest x1 28.2 us: rows_step(): pl.pallas_call(rows_kernel, grid_spec=pltpu.PrefetchScalarGridSpec(num_sc...]
    psum x1 -> x0, blocking collectives: 53.8 us -> none  [body(): sums = own_lanes(lax.psum(sums, ('dp', 'tensor')))]
    ppermute x18 -> x9, waiting for transfers between devices: 52.4 us -> 3.21 us  [ring_gather(): behind = lax.ppermute(behind, 'dp', down)]
    convert_element_type x27 -> x4, other arithmetic: 49.9 us -> 8.83 us  [the longest x1 3.85 us: body(): sum_w = (keep_w.astype(F32) + swap(give_w, 1).astype(F32)).astype(BF)]
    scatter-add x15 -> x0, other arithmetic: 39.3 us -> none  [iso_backward(): total = total.at[j:j + span_len].add(spread[:, :, j * D:(j + 1) * D])]
    ppermute x56 -> x32, waiting for transfers between devices: 81.5 us -> 43.4 us  [swap(): return lax.ppermute(value, 'tensor', [(i, i ^ mask) for i in range(4)])]
    all_to_all x2, waiting for transfers between devices: 16.2 us -> 49 us  [exchange_sum(): got = lax.all_to_all(blocks.astype(BF), 'dp', 0, 0, tiled=True)]
  transfers between devices with their start and end apart: 108 -> 83, of which waited for: 41 -> 37; matrix products, arithmetic and copies ran while one was open for 50% -> 11% of each run, Pallas kernels for 0% -> 10%
where the time goes in v2:
time: 616 us; the launch traced here: 605 us
  waiting for transfers between devices  231 us (38%)
  starting transfers between devices  111 us (18%)
  Pallas kernels  97.7 us (16%)
  local copies, waits for them, and re-layouts  51.5 us (8%)
  between operations  49.8 us (8%)
  other arithmetic  37.9 us (6%)
  blocking collectives  25.7 us (4%)
    ppermute x12, waiting for transfers between devices, ring_gather(): ahead = lax.ppermute(ahead, 'dp', up)  69.4 us
    all_to_all x2, waiting for transfers between devices, exchange_sum(): got = lax.all_to_all(blocks.astype(BF), 'dp', 0, 0, tiled=True)  49 us
    ppermute x32, waiting for transfers between devices, swap(): return lax.ppermute(value, 'tensor', [(i, i ^ mask) for i in range(4)])  43.4 us
    pallas_call x1, Pallas kernels, rows_step(): pl.pallas_call(rows_kernel, grid_spec=pltpu.PrefetchScalarGridSpec(num_sc...  28.2 us
    all_to_all x1, waiting for transfers between devices, body(): x_pos_b = lax.all_to_all(x_send_b, 'dp', 0, 0, tiled=True)  26.8 us
    all_to_all x1, blocking collectives, body(): res = lax.all_to_all(res_send, 'tensor', 0, 0, tiled=True)  25.7 us
    ppermute x12, starting transfers between devices, ring_gather(): ahead = lax.ppermute(ahead, 'dp', up)  24.5 us
    unnamed x219, local copies, waits for them, and re-layouts  19.3 us
  transfers between devices with their start and end apart: 83, of which 37 were waited for; matrix products, arithmetic and copies ran while one was open for 11% of the time, Pallas kernels for 10%

profile of v2, /device:TPU:0, one launch (start us, length us, event | category | flops | bytes accessed | tf_op | source)
XLA Modules:
  0.0 605.1 jit_solution(17701945765328942812)
XLA Ops:
  56.0 5.8 collective-permute-done.9.refs_11_.refs_7_
  62.7 11.1 %shard_map.400 = (f32[480,128]{1,0:T(8,128)}, bf16[480,128]{1,0:T(8,128)(2,1)}, bf16[3264,512]{1,0:T(8,128)(2,1)}, bf16[8,544,128]{2,1,0:T(8,128)(2,1)}, bf16[8,416,128]{2,1,0:T(8,128)(2,1)}) custom-call(s32[2]{0:T(128)} %pad_add_fusion.place_ref, s32[8]{0:T(128)} %gather_fusion, bf16[3264,128]{1,0:T(8,128)(2,1)} %refs_0_.2, ...), custom_call_target="tpu_custom_call" | custom-call | flops 855638016 | bytes 12951552 | tf_op jit(solution)/shard_map/pallas_call | solution.py:390
  102.4 5.4 collective-permute-done.20
  110.2 10.8 %collective-permute-done.22 = bf16[480,256]{1,0:T(8,128)(2,1)S(1)} collective-permute-done((bf16[480,256]{1,0:T(8,128)(2,1)S(1)}, bf16[480,256]{1,0:T(8,128)(2,1)S(1)}, u32[]{:S(2)}, u32[]{:S(2)}) %collective-permute-start.22) | collective-permute-done | bytes 245792 | tf_op jit(solution)/shard_map/ppermute | solution.py:81
  121.0 6.0 collective-permute-start.24
  127.2 5.9 collective-permute-done.24
  139.0 8.0 %shard_map.401 = bf16[8,480,128]{2,1,0:T(8,128)(2,1)} custom-call(s32[2]{0:T(128)S(1)} %pad_add_fusion.1.reach_ref, bf16[8,480,256]{2,1,0:T(8,128)(2,1)} %copy-done.7, bf16[8,480,256]{2,1,0:T(8,128)(2,1)} %copy-done.17, bf16[512,1152]{1,0:T(8,128)(2,1)S(1)} %maximum_dynamic-update-slice_fusion.w_a_ref, ...), custom_call_target="tpu_custom_call" | custom-call | flops 4311744512 | bytes 4915200 | tf_op jit(solution)/shard_map/pallas_call | solution.py:256
  147.1 6.2 %all-to-all-start = ((bf16[8,480,128]{2,1,0:T(8,128)(2,1)}), bf16[8,480,128]{2,1,0:T(8,128)(2,1)S(1)}, u32[]{:S(2)}, u32[]{:S(2)}) async-start(bf16[8,480,128]{2,1,0:T(8,128)(2,1)} %shard_map.401), calls=%async_computation | async-start | bytes 1966080 | tf_op jit(solution)/shard_map/all_to_all | solution.py:121
  175.3 18.5 %all-to-all-done = bf16[8,480,128]{2,1,0:T(8,128)(2,1)S(1)} async-done(((bf16[8,480,128]{2,1,0:T(8,128)(2,1)}), bf16[8,480,128]{2,1,0:T(8,128)(2,1)S(1)}, u32[]{:S(2)}, u32[]{:S(2)}) %all-to-all-start) | async-done | bytes 983072 | tf_op jit(solution)/shard_map/all_to_all | solution.py:121
  205.0 7.3 %shard_map.402 = (bf16[4,2,816,128]{3,2,1,0:T(8,128)(2,1)}, f32[272,1536]{1,0:T(8,128)}, f32[208,2048]{1,0:T(8,128)}, bf16[480,512]{1,0:T(8,128)(2,1)}, f32[480,...) custom-call(s32[2]{0:T(128)} %pad_add_fusion.place_ref, f32[480,128]{1,0:T(8,128)} %convert_reduce_fusion.1.own_ref, ...), custom_call_target="tpu_custom_call" | custom-call | flops 880803840 | bytes 10682368 | tf_op jit(solution)/shard_map/pallas_call | solution.py:450
  213.7 4.4 all-to-all-start.1
  224.0 20.7 %collective-permute-done.35.refs_5_ = bf16[1024,128]{1,0:T(8,128)(2,1)S(1)} collective-permute-done((bf16[1024,128]{1,0:T(8,128)(2,1)S(1)}, bf16[1024,128]{1,0:T(8,128)(2,1)S(1)}, u32[]{:S(2)}, u32[]{:S(2)}) %collective-permute-start.35) | collective-permute-done | bytes 262176 | tf_op jit(solution)/shard_map/ppermute | solution.py:41
  246.9 28.2 %shard_map.403 = (bf16[4,816,128]{2,1,0:T(8,128)(2,1)}, bf16[4,2,816,128]{3,2,1,0:T(8,128)(2,1)}, bf16[1024,1280]{1,0:T(8,128)(2,1)}, bf16[1024,1280]{1,0:T(8,128)(2,1)}, f32[8,512]{1,0:T(8,128)}) custom-call(s32[2]{0:T(128)} %pad_add_fusion.place_ref, s32[4]{0:T(128)} %horizon_ref.1, bf16[4,2,816,128]{3,2,1,0:T(8,128)(2,1)} %all-to-all-done.1.up_ref, ...), custom_call_target="tpu_custom_call" | custom-call | flops 12834570240 | bytes 13008896 | tf_op jit(solution)/shard_map/pallas_call | solution.py:561
  275.1 25.7 %all_to_all.40.res_ref = bf16[4,2,816,128]{3,2,1,0:T(8,128)(2,1)} all-to-all(bf16[4,2,816,128]{3,2,1,0:T(8,128)(2,1)} %get-tuple-element.74), channel_id=1, replica_groups=mesh['dp'=8,'tensor'=4] {'tensor'}, dimensions={0} | all-to-all | bytes 3342336 | tf_op jit(solution)/shard_map/all_to_all | solution.py:810
  300.8 9.4 %shard_map.404 = (f32[480,256]{1,0:T(8,128)}, f32[480,256]{1,0:T(8,128)}, bf16[512,3584]{1,0:T(8,128)(2,1)}) custom-call(s32[2]{0:T(128)} %pad_add_fusion.place_ref, bf16[4,2,816,128]{3,2,1,0:T(8,128)(2,1)} %all_to_all.40.res_ref, f32[272,1536]{1,0:T(8,128)} %get-tuple-element.75.ua_ref, f32[208,2048]{1,0:T(8,128)} %get-tuple-element.76.ub_ref, ...), custom_call_target="tpu_custom_call" | custom-call | flops 1761607680 | bytes 13860864 | tf_op jit(solution)/shard_map/pallas_call | solution.py:626
  318.5 4.2 collective-permute-done.39
  328.6 4.3 all-to-all-start.3
  336.9 32.1 %collective-permute-done.43 = bf16[480,128]{1,0:T(8,128)(2,1)S(1)} collective-permute-done((bf16[480,128]{1,0:T(8,128)(2,1)S(1)}, bf16[480,128]{1,0:T(8,128)(2,1)S(1)}, u32[]{:S(2)}, u32[]{:S(2)}) %collective-permute-start.43) | collective-permute-done | bytes 122912 | tf_op jit(solution)/shard_map/ppermute | solution.py:81
  369.0 7.5 %collective-permute-start.45 = (bf16[480,128]{1,0:T(8,128)(2,1)S(1)}, bf16[480,128]{1,0:T(8,128)(2,1)S(1)}, u32[]{:S(2)}, u32[]{:S(2)}) collective-permute-start(bf16[480,128]{1,0:T(8,128)(2,1)S(1)} %collective-permute-done.43), channel_id=1, source_target_pairs={{0,8},{8,16},{16,24},{24,28},{28,20},{20,12},{12,4},{4,0},{1,9},{9... | collective-permute-start | bytes 368648 | tf_op jit(solution)/shard_map/ppermute | solution.py:81
  382.2 4.4 collective-permute-done.47
  386.7 16.8 %shard_map.405 = (f32[9,512,128]{2,1,0:T(8,128)}, f32[8,512,128]{2,1,0:T(8,128)}, bf16[8,480,512]{2,1,0:T(8,128)(2,1)}) custom-call(s32[2]{0:T(128)S(1)} %pad_add_fusion.1.reach_ref, bf16[8,480,128]{2,1,0:T(8,128)(2,1)S(1)} %bitcast_dynamic-update-slice_fusion.16.grad_ref, bf16[8,480,256]{2,1,0:T(8,128)(2,1)} %copy-done.7, bf16[8,480,256]{2,1,0:T(8,128)(2,1)} %copy-done.17, ...), custom_call_target="tpu_custom_call" | custom-call | flops 8623489024 | bytes 7864320 | tf_op jit(solution)/shard_map/pallas_call | solution.py:284
  405.3 4.5 all-to-all-start.4
  416.4 26.8 %all-to-all-done.4.refs_4_ = bf16[8,416,128]{2,1,0:T(8,128)(2,1)} async-done(((bf16[8,416,128]{2,1,0:T(8,128)(2,1)}), bf16[8,416,128]{2,1,0:T(8,128)(2,1)}, u32[]{:S(2)}, u32[]{:S(2)}) %all-to-all-start.4) | async-done | bytes 852000 | tf_op jit(solution)/shard_map/all_to_all | solution.py:806
  443.2 4.2 all-to-all-start.6
  449.5 10.4 %collective-permute-done.68 = f32[8,512]{1,0:T(8,128)S(1)} collective-permute-done((f32[8,512]{1,0:T(8,128)S(1)}, f32[8,512]{1,0:T(8,128)S(1)}, u32[]{:S(2)}, u32[]{:S(2)}) %collective-permute-start.68) | collective-permute-done | bytes 16416 | tf_op jit(solution)/shard_map/ppermute | solution.py:308
  459.9 4.2 collective-permute-start.69
  473.2 5.8 all-to-all-start.7
  486.6 30.5 %all-to-all-done.7 = bf16[8,480,128]{2,1,0:T(8,128)(2,1)} async-done(((bf16[8,480,128]{2,1,0:T(8,128)(2,1)}), bf16[8,480,128]{2,1,0:T(8,128)(2,1)}, u32[]{:S(2)}, u32[]{:S(2)}) %all-to-all-start.7) | async-done | bytes 983072 | tf_op jit(solution)/shard_map/all_to_all | solution.py:121
  520.6 10.3 %shard_map.406 = (bf16[3264,256]{1,0:T(8,128)(2,1)}, bf16[3264,256]{1,0:T(8,128)(2,1)}) custom-call(s32[2]{0:T(128)} %pad_add_fusion.place_ref, s32[8]{0:T(128)} %gather_fusion, bf16[480,128]{1,0:T(8,128)(2,1)} %get-tuple-element.142.grad_ref, bf16[768,128]{1,0:T(8,128)(2,1)} %refs_0_.3, bf16[768,128]{1,0:T(8,128)(2,1)} %copy-done.36, ...), custom_call_target="tpu_custom_call" | custom-call | flops 855638016 | bytes 7397376 | tf_op jit(solution)/shard_map/pallas_call | solution.py:713
  564.8 6.6 %shard_map.407 = (f32[1024,128]{1,0:T(8,128)}, f32[1024,128]{1,0:T(8,128)}) custom-call(s32[2]{0:T(128)} %pad_add_fusion.place_ref, bf16[8,480,128]{2,1,0:T(8,128)(2,1)} %copy-done.10, bf16[8,544,128]{2,1,0:T(8,128)(2,1)} %all-to-all-done.3.refs_0_, bf16[8,544,128]{2,1,0:T(8,128)(2,1)} %collective-permute-done.59.refs_1_, bf16[8,544,128]{2,1,0:T(8,128)(2,1)} %copy-done.26, ...), custom_call_target="tpu_custom_call" | custom-call | flops 1140850688 | bytes 8847360 | tf_op jit(solution)/shard_map/pallas_call | solution.py:674
  573.7 7.2 %collective-permute-done.51 = bf16[3264,128]{1,0:T(8,128)(2,1)} collective-permute-done((bf16[3264,128]{1,0:T(8,128)(2,1)}, bf16[3264,128]{1,0:T(8,128)(2,1)}, u32[]{:S(2)}, u32[]{:S(2)}) %collective-permute-start.51) | collective-permute-done | bytes 835616 | tf_op jit(solution)/shard_map/ppermute | solution.py:41
  583.6 7.9 %all-gather.5.cloned.1.call-done = bf16[1024,512]{1,0:T(8,128)(2,1)} async-done(((bf16[128,512]{1,0:T(8,128)(2,1)}), bf16[1024,512]{1,0:T(8,128)(2,1)}) %all-gather.5.cloned.1.call-update) | async-done | bytes 1048592 | tf_op jit(solution)/shard_map/all_gather | solution.py:858
  (488 shorter events, 194.5 us)
Async XLA Ops:
  7.2 197.8 %all-gather.3.cloned.1.call-start = ((), (), s32[]{:S(2)}) async-start(), calls=%async_computation.10 | async-start | bytes 4128768 | tf_op jit(solution)/shard_map/all_gather | solution.py:777
  9.1 16.0 %collective-permute-start.10 = (bf16[1152,128]{1,0:T(8,128)(2,1)S(1)}, bf16[1152,128]{1,0:T(8,128)(2,1)S(1)}, u32[]{:S(2)}, u32[]{:S(2)}) collective-permute-start(bf16[1152,128]{1,0:T(8,128)(2,1)S(1)} %constant_dynamic-update-slice_fusion.refs_12_.refs_8_), channel_id=1, source_target_pairs={{0,8},{8,16},{16,24},{24,28},{28,20},{20,12},{12,4},{4,0},{1,9},{9... | collective-permute-start | bytes 884744 | tf_op jit(solution)/shard_map/ppermute | solution.py:101
  12.1 15.7 %collective-permute-start.11 = (bf16[1152,128]{1,0:T(8,128)(2,1)S(1)}, bf16[1152,128]{1,0:T(8,128)(2,1)S(1)}, u32[]{:S(2)}, u32[]{:S(2)}) collective-permute-start(bf16[1152,128]{1,0:T(8,128)(2,1)S(1)} %constant_dynamic-update-slice_fusion.refs_12_.refs_8_), channel_id=1, source_target_pairs={{8,0},{16,8},{24,16},{28,24},{20,28},{12,20},{4,12},{0,4},{9,1},{1... | collective-permute-start | bytes 884744 | tf_op jit(solution)/shard_map/ppermute | solution.py:105
  14.1 19.8 %collective-permute-start = (bf16[3264,128]{1,0:T(8,128)(2,1)}, bf16[3264,128]{1,0:T(8,128)(2,1)}, u32[]{:S(2)}, u32[]{:S(2)}) collective-permute-start(bf16[3264,128]{1,0:T(8,128)(2,1)} %refs_0_.2), channel_id=1, source_target_pairs={{0,2},{1,3},{2,0},{3,1},{4,6},{5,7},{6,4},{7,5},{8,10},{9,11},{10,... | collective-permute-start | bytes 2506760 | tf_op jit(solution)/shard_map/ppermute | solution.py:41
  27.8 34.0 %collective-permute-start.1 = (bf16[3264,128]{1,0:T(8,128)(2,1)}, bf16[3264,128]{1,0:T(8,128)(2,1)}, u32[]{:S(2)}, u32[]{:S(2)}) collective-permute-start(bf16[3264,128]{1,0:T(8,128)(2,1)} %refs_0_.2), channel_id=1, source_target_pairs={{0,1},{1,0},{2,3},{3,2},{4,5},{5,4},{6,7},{7,6},{8,9},{9,8},{10,11... | collective-permute-start | bytes 2506760 | tf_op jit(solution)/shard_map/ppermute | solution.py:41
  34.0 27.8 %collective-permute-start.2 = (bf16[3264,128]{1,0:T(8,128)(2,1)}, bf16[3264,128]{1,0:T(8,128)(2,1)}, u32[]{:S(2)}, u32[]{:S(2)}) collective-permute-start(bf16[3264,128]{1,0:T(8,128)(2,1)} %collective-permute-done.refs_1_), channel_id=1, source_target_pairs={{0,1},{1,0},{2,3},{3,2},{4,5},{5,4},{6,7},{7,6},{8,9},{9,8},{10,11... | collective-permute-start | bytes 2506760 | tf_op jit(solution)/shard_map/ppermute | solution.py:41
  43.6 18.1 %collective-permute-start.15 = (bf16[1152,128]{1,0:T(8,128)(2,1)S(1)}, bf16[1152,128]{1,0:T(8,128)(2,1)S(1)}, u32[]{:S(2)}, u32[]{:S(2)}) collective-permute-start(bf16[1152,128]{1,0:T(8,128)(2,1)S(1)} %collective-permute-done.13.refs_16_.refs_12_), channel_id=1, source_target_pairs={{8,0},{16,8},{24,16},{28,24},{20,28},{12,20},{4,12},{0,4},{9,1},{1... | collective-permute-start | bytes 884744 | tf_op jit(solution)/shard_map/ppermute | solution.py:105
  79.0 21.2 %collective-permute-start.18 = (bf16[480,256]{1,0:T(8,128)(2,1)S(1)}, bf16[480,256]{1,0:T(8,128)(2,1)S(1)}, u32[]{:S(2)}, u32[]{:S(2)}) collective-permute-start(bf16[480,256]{1,0:T(8,128)(2,1)S(1)} %constant_dynamic-update-slice_fusion.2), channel_id=1, source_target_pairs={{0,8},{8,16},{16,24},{24,28},{28,20},{20,12},{12,4},{4,0},{1,9},{9... | collective-permute-start | bytes 737288 | tf_op jit(solution)/shard_map/ppermute | solution.py:81
  80.5 21.2 %collective-permute-start.19 = (bf16[480,256]{1,0:T(8,128)(2,1)S(1)}, bf16[480,256]{1,0:T(8,128)(2,1)S(1)}, u32[]{:S(2)}, u32[]{:S(2)}) collective-permute-start(bf16[480,256]{1,0:T(8,128)(2,1)S(1)} %constant_dynamic-update-slice_fusion.2), channel_id=1, source_target_pairs={{8,0},{16,8},{24,16},{28,24},{20,28},{12,20},{4,12},{0,4},{9,1},{1... | collective-permute-start | bytes 737288 | tf_op jit(solution)/shard_map/ppermute | solution.py:84
  109.7 17.3 %collective-permute-start.23 = (bf16[480,256]{1,0:T(8,128)(2,1)S(1)}, bf16[480,256]{1,0:T(8,128)(2,1)S(1)}, u32[]{:S(2)}, u32[]{:S(2)}) collective-permute-start(bf16[480,256]{1,0:T(8,128)(2,1)S(1)} %collective-permute-done.21), channel_id=1, source_target_pairs={{8,0},{16,8},{24,16},{28,24},{20,28},{12,20},{4,12},{0,4},{9,1},{1... | collective-permute-start | bytes 737288 | tf_op jit(solution)/shard_map/ppermute | solution.py:84
  147.1 46.8 %all-to-all-start = ((bf16[8,480,128]{2,1,0:T(8,128)(2,1)}), bf16[8,480,128]{2,1,0:T(8,128)(2,1)S(1)}, u32[]{:S(2)}, u32[]{:S(2)}) async-start(bf16[8,480,128]{2,1,0:T(8,128)(2,1)} %shard_map.401), calls=%async_computation | async-start | bytes 1966080 | tf_op jit(solution)/shard_map/all_to_all | solution.py:121
  155.6 42.4 %collective-permute-start.32 = (bf16[1024,512]{1,0:T(8,128)(2,1)}, bf16[1024,512]{1,0:T(8,128)(2,1)}, u32[]{:S(2)}, u32[]{:S(2)}) collective-permute-start(bf16[1024,512]{1,0:T(8,128)(2,1)} %pad_maximum_fusion.2.refs_0_), channel_id=1, source_target_pairs={{0,2},{1,3},{2,0},{3,1},{4,6},{5,7},{6,4},{7,5},{8,10},{9,11},{10,... | collective-permute-start | bytes 3145736 | tf_op jit(solution)/shard_map/ppermute | solution.py:41
  174.8 22.7 %collective-permute-start.30 = (f32[8,128]{1,0:T(8,128)S(1)}, f32[8,128]{1,0:T(8,128)S(1)}, u32[]{:S(2)}, u32[]{:S(2)}) collective-permute-start(f32[8,128]{1,0:T(8,128)S(1)} %stack.62), channel_id=1, source_target_pairs={{0,2},{1,3},{2,0},{3,1},{4,6},{5,7},{6,4},{7,5},{8,10},{9,11},{10,... | collective-permute-start | bytes 12296 | tf_op jit(solution)/shard_map/ppermute | solution.py:41
  213.7 33.2 %all-to-all-start.1 = ((bf16[4,2,816,128]{3,2,1,0:T(8,128)(2,1)}), bf16[4,2,816,128]{3,2,1,0:T(8,128)(2,1)}, u32[]{:S(2)}, u32[]{:S(2)}) async-start(bf16[4,2,816,128]{3,2,1,0:T(8,128)(2,1)} %get-tuple-element.63), calls=%async_computation.1 | async-start | bytes 3342336 | tf_op jit(solution)/shard_map/all_to_all | solution.py:803
  218.0 325.0 %reduce-scatter.5.cloned.1.call-start = ((), (), s32[]{:S(2)}) async-start(), calls=%async_computation.12 | async-start | bytes 2949120 | tf_op jit(solution)/shard_map/reduce_scatter | solution.py:813
  219.3 25.5 %collective-permute-start.33 = (bf16[1024,512]{1,0:T(8,128)(2,1)}, bf16[1024,512]{1,0:T(8,128)(2,1)S(1)}, u32[]{:S(2)}, u32[]{:S(2)}) collective-permute-start(bf16[1024,512]{1,0:T(8,128)(2,1)} %pad_maximum_fusion.2.refs_0_), channel_id=1, source_target_pairs={{0,1},{1,0},{2,3},{3,2},{4,5},{5,4},{6,7},{7,6},{8,9},{9,8},{10,11... | collective-permute-start | bytes 3145736 | tf_op jit(solution)/shard_map/ppermute | solution.py:41
  219.7 25.1 %collective-permute-start.34 = (bf16[1024,512]{1,0:T(8,128)(2,1)}, bf16[1024,512]{1,0:T(8,128)(2,1)S(1)}, u32[]{:S(2)}, u32[]{:S(2)}) collective-permute-start(bf16[1024,512]{1,0:T(8,128)(2,1)} %collective-permute-done.32.refs_1_), channel_id=1, source_target_pairs={{0,1},{1,0},{2,3},{3,2},{4,5},{5,4},{6,7},{7,6},{8,9},{9,8},{10,11... | collective-permute-start | bytes 3145736 | tf_op jit(solution)/shard_map/ppermute | solution.py:41
  222.1 22.7 %collective-permute-start.35 = (bf16[1024,128]{1,0:T(8,128)(2,1)S(1)}, bf16[1024,128]{1,0:T(8,128)(2,1)S(1)}, u32[]{:S(2)}, u32[]{:S(2)}) collective-permute-start(bf16[1024,128]{1,0:T(8,128)(2,1)S(1)} %bitcast.299), channel_id=1, source_target_pairs={{0,2},{1,3},{2,0},{3,1},{4,6},{5,7},{6,4},{7,5},{8,10},{9,11},{10,... | collective-permute-start | bytes 786440 | tf_op jit(solution)/shard_map/ppermute | solution.py:41
  224.0 20.8 %collective-permute-start.36 = (bf16[1024,128]{1,0:T(8,128)(2,1)S(1)}, bf16[1024,128]{1,0:T(8,128)(2,1)S(1)}, u32[]{:S(2)}, u32[]{:S(2)}) collective-permute-start(bf16[1024,128]{1,0:T(8,128)(2,1)S(1)} %bitcast.300), channel_id=1, source_target_pairs={{0,1},{1,0},{2,3},{3,2},{4,5},{5,4},{6,7},{7,6},{8,9},{9,8},{10,11... | collective-permute-start | bytes 786440 | tf_op jit(solution)/shard_map/ppermute | solution.py:41
  328.6 76.7 %all-to-all-start.3 = ((bf16[8,544,128]{2,1,0:T(8,128)(2,1)}), bf16[8,544,128]{2,1,0:T(8,128)(2,1)}, u32[]{:S(2)}, u32[]{:S(2)}) async-start(bf16[8,544,128]{2,1,0:T(8,128)(2,1)} %get-tuple-element.71), calls=%async_computation.3 | async-start | bytes 2228224 | tf_op jit(solution)/shard_map/all_to_all | solution.py:802
  332.9 250.7 %reduce-scatter.3.cloned.1.call-start = ((), (), s32[]{:S(2)}) async-start(), calls=%async_computation.11 | async-start | bytes 4128768 | tf_op jit(solution)/shard_map/reduce_scatter | solution.py:816
  333.1 35.9 %collective-permute-start.43 = (bf16[480,128]{1,0:T(8,128)(2,1)S(1)}, bf16[480,128]{1,0:T(8,128)(2,1)S(1)}, u32[]{:S(2)}, u32[]{:S(2)}) collective-permute-start(bf16[480,128]{1,0:T(8,128)(2,1)S(1)} %collective-permute-done.41), channel_id=1, source_target_pairs={{0,8},{8,16},{16,24},{24,28},{28,20},{20,12},{12,4},{4,0},{1,9},{9... | collective-permute-start | bytes 368648 | tf_op jit(solution)/shard_map/ppermute | solution.py:81
  336.8 39.7 %collective-permute-start.44 = (bf16[480,128]{1,0:T(8,128)(2,1)S(1)}, bf16[480,128]{1,0:T(8,128)(2,1)S(1)}, u32[]{:S(2)}, u32[]{:S(2)}) collective-permute-start(bf16[480,128]{1,0:T(8,128)(2,1)S(1)} %collective-permute-done.42), channel_id=1, source_target_pairs={{8,0},{16,8},{24,16},{28,24},{20,28},{12,20},{4,12},{0,4},{9,1},{1... | collective-permute-start | bytes 368648 | tf_op jit(solution)/shard_map/ppermute | solution.py:84
  405.3 37.9 %all-to-all-start.4 = ((bf16[8,416,128]{2,1,0:T(8,128)(2,1)}), bf16[8,416,128]{2,1,0:T(8,128)(2,1)}, u32[]{:S(2)}, u32[]{:S(2)}) async-start(bf16[8,416,128]{2,1,0:T(8,128)(2,1)} %get-tuple-element.73), calls=%async_computation.4 | async-start | bytes 1703936 | tf_op jit(solution)/shard_map/all_to_all | solution.py:806
  415.3 55.5 %collective-permute-start.49 = (bf16[8,480,128]{2,1,0:T(8,128)(2,1)}, bf16[8,480,128]{2,1,0:T(8,128)(2,1)}, u32[]{:S(2)}, u32[]{:S(2)}) collective-permute-start(bf16[8,480,128]{2,1,0:T(8,128)(2,1)} %slice.1034), channel_id=1, source_target_pairs={{0,2},{1,3},{2,0},{3,1},{4,6},{5,7},{6,4},{7,5},{8,10},{9,11},{10,... | collective-permute-start | bytes 2949128 | tf_op jit(solution)/shard_map/ppermute | solution.py:41
  443.2 30.0 %all-to-all-start.6 = ((bf16[4,816,128]{2,1,0:T(8,128)(2,1)}), bf16[4,816,128]{2,1,0:T(8,128)(2,1)}, u32[]{:S(2)}, u32[]{:S(2)}) async-start(bf16[4,816,128]{2,1,0:T(8,128)(2,1)} %get-tuple-element.80), calls=%async_computation.6 | async-start | bytes 1671168 | tf_op jit(solution)/shard_map/all_to_all | solution.py:823
  467.0 85.5 %collective-permute-start.59 = (bf16[8,544,128]{2,1,0:T(8,128)(2,1)}, bf16[8,544,128]{2,1,0:T(8,128)(2,1)}, u32[]{:S(2)}, u32[]{:S(2)}) collective-permute-start(bf16[8,544,128]{2,1,0:T(8,128)(2,1)} %all-to-all-done.3.refs_0_), channel_id=1, source_target_pairs={{0,2},{1,3},{2,0},{3,1},{4,6},{5,7},{6,4},{7,5},{8,10},{9,11},{10,... | collective-permute-start | bytes 3342344 | tf_op jit(solution)/shard_map/ppermute | solution.py:41
  473.2 43.8 %all-to-all-start.7 = ((bf16[8,480,128]{2,1,0:T(8,128)(2,1)}), bf16[8,480,128]{2,1,0:T(8,128)(2,1)}, u32[]{:S(2)}, u32[]{:S(2)}) async-start(bf16[8,480,128]{2,1,0:T(8,128)(2,1)} %fusion), calls=%async_computation.7 | async-start | bytes 1966080 | tf_op jit(solution)/shard_map/all_to_all | solution.py:121
  479.0 112.5 %all-gather.5.cloned.1.call-start = ((), (), s32[]{:S(2)}) async-start(), calls=%async_computation.13 | async-start | bytes 1179648 | tf_op jit(solution)/shard_map/all_gather | solution.py:858
  480.7 71.9 %collective-permute-start.62 = (bf16[8,416,128]{2,1,0:T(8,128)(2,1)}, bf16[8,416,128]{2,1,0:T(8,128)(2,1)}, u32[]{:S(2)}, u32[]{:S(2)}) collective-permute-start(bf16[8,416,128]{2,1,0:T(8,128)(2,1)} %all-to-all-done.4.refs_4_), channel_id=1, source_target_pairs={{0,2},{1,3},{2,0},{3,1},{4,6},{5,7},{6,4},{7,5},{8,10},{9,11},{10,... | collective-permute-start | bytes 2555912 | tf_op jit(solution)/shard_map/ppermute | solution.py:41
  530.9 23.4 %collective-permute-start.50 = (bf16[3264,256]{1,0:T(8,128)(2,1)}, bf16[3264,256]{1,0:T(8,128)(2,1)}, u32[]{:S(2)}, u32[]{:S(2)}) collective-permute-start(bf16[3264,256]{1,0:T(8,128)(2,1)} %get-tuple-element.87), channel_id=1, source_target_pairs={{0,1},{1,0},{2,3},{3,2},{4,5},{5,4},{6,7},{7,6},{8,9},{9,8},{10,11... | collective-permute-start | bytes 5013512 | tf_op jit(solution)/shard_map/ppermute | solution.py:41
  560.3 20.5 %collective-permute-start.51 = (bf16[3264,128]{1,0:T(8,128)(2,1)}, bf16[3264,128]{1,0:T(8,128)(2,1)}, u32[]{:S(2)}, u32[]{:S(2)}) collective-permute-start(bf16[3264,128]{1,0:T(8,128)(2,1)} %slice.1035), channel_id=1, source_target_pairs={{0,2},{1,3},{2,0},{3,1},{4,6},{5,7},{6,4},{7,5},{8,10},{9,11},{10,... | collective-permute-start | bytes 2506760 | tf_op jit(solution)/shard_map/ppermute | solution.py:41
  (157 other events, 1929.8 us)
Sparse Core Ops, SparseCore 0:
  100.1 93.9 all-gather.2
  318.6 90.6 reduce-scatter.4
  412.9 104.8 reduce-scatter.2
  552.7 38.7 all-gather.4

commit v3 on v2

v3 whole, which is shorter than its diff:
```python
from functools import partial

import jax
import jax.numpy as jnp
import numpy as np
from jax import lax
from jax.experimental import pallas as pl
from jax.experimental.pallas import tpu as pltpu
from jax.sharding import PartitionSpec as P

D = 512
SA = 12
SB = 16
IN_LEN = 96
L = 816
MA = 68
MB = 51


EPS = 1e-05
BF = jnp.bfloat16
F32 = jnp.float32


XOR = (0, 2, 1, 3)
PARAMS = pltpu.CompilerParams(vmem_limit_bytes=56 << 20)


def dot(left, right):
    return jnp.dot(left, right, preferred_element_type=F32)


def dot_tn(left, right):
    return lax.dot_general(left, right, (((0,), (0,)), ((), ())), preferred_element_type=F32)


def dot_nt(left, right):
    return lax.dot_general(left, right, (((1,), (1,)), ((), ())), preferred_element_type=F32)


def swap(value, mask):
    return lax.ppermute(value, "tensor", [(i, i ^ mask) for i in range(4)])


def by_xor(blocks):
    t = lax.axis_index("tensor")
    low = (t % 2) == 0
    high = (t // 2) == 0
    mid = [jnp.where(low, blocks[k], blocks[k ^ 1]) for k in range(4)]
    return [jnp.where(high, mid[k], mid[k ^ 2]) for k in range(4)]


def lanes(value):
    width = value.shape[1] // 4
    return [value[:, i * width : (i + 1) * width] for i in range(4)]


def own_lanes(value):
    width = value.shape[1] // 4
    return lax.dynamic_slice_in_dim(value, lax.axis_index("tensor") * width, width, 1)


def lane_at(t, k, width=128):
    return pl.ds(pl.multiple_of((t ^ k) * width, width), width)


def ring_order(count):
    return list(range(0, count, 2)) + list(range(1, count, 2))[::-1]


def ring_places(count):
    order = ring_order(count)
    steps = [0]
    for step in range(1, count // 2 + 1):
        steps += [-step, step] if step <= (count - 1) // 2 else [-step]
    places = [[order[(order.index(i) + k) % count] for k in steps] for i in range(count)]
    return np.array(places, np.int32)


def own_row(table):
    start = (lax.axis_index("dp"), jnp.int32(0))
    size = (1, table.shape[1])
    return lax.dynamic_slice(jnp.asarray(table), start, size, allow_negative_indices=False)[0]


def rows_from(value, start, count):
    return lax.dynamic_slice_in_dim(value, start, count, 0, allow_negative_indices=False)


def ring_list(value, halves=False, beside=()):
    beside = list(beside)
    held = []
    count = lax.axis_size("dp")
    order = ring_order(count)
    up = [(order[i], order[(i + 1) % count]) for i in range(count)]
    down = [(b, a) for a, b in up]
    ahead = behind = value
    blocks = [value]
    for step in range(1, count // 2 + 1):
        if step > 2 and beside:
            ahead, *moved = together(ahead, *beside.pop(0)(held))
            held += moved
        if step > (count - 1) // 2 and halves:
            half = value.shape[0] // 2
            first = lax.ppermute(ahead[:half], "dp", up)
            second = lax.ppermute(behind[half:], "dp", down)
            blocks.append(jnp.concatenate([first, second], axis=0))
            continue
        ahead = lax.ppermute(ahead, "dp", up)
        blocks.append(ahead)
        if step <= (count - 1) // 2:
            behind = lax.ppermute(behind, "dp", down)
            blocks.append(behind)
    return (blocks, held) if held else blocks


def ring_stack(value):
    blocks = ring_list(value)
    result = jnp.zeros((len(blocks),) + value.shape, value.dtype)
    for i, block in enumerate(blocks):
        result = lax.dynamic_update_slice(result, block[None], (i,) + (0,) * value.ndim)
    return result


def four(value):
    across = swap(value, 2)
    return [value, across, swap(value, 1), swap(across, 1)]


def exchange(blocks):
    return [blocks[0]] + [swap(v, k) for v, k in zip(blocks[1:], XOR[1:])]


def own_sum(blocks):
    far = blocks[1].astype(F32) + swap(blocks[3], 1).astype(F32)
    near = blocks[0].astype(F32) + swap(blocks[2], 1).astype(F32)
    return near + swap(far.astype(BF), 2).astype(F32)


def after(values, *events):
    return lax.optimization_barrier(tuple(values) + events)[: len(values)]


def together(*values):
    return lax.optimization_barrier(values)


def exchange_sum(blocks):
    got = lax.all_to_all(blocks.astype(BF), "dp", 0, 0, tiled=True)
    return jnp.sum(got.astype(F32), axis=0)


def scatter_sum(value):
    return lax.psum_scatter(value.astype(BF), "dp", scatter_dimension=0, tiled=True).astype(F32)


def norm_forward(operand, gain_vec, bias_vec):
    row_mean = jnp.mean(operand, axis=1, keepdims=True)
    row_square = jnp.mean(operand * operand, axis=1, keepdims=True)
    inv_std = lax.rsqrt(row_square - row_mean * row_mean + EPS)
    normed = (operand - row_mean) * inv_std
    return (normed * gain_vec + bias_vec, (normed, inv_std))


def norm_backward(upstream, gain_vec, stored):
    normed, inv_std = stored
    scaled = upstream * gain_vec
    first_mean = jnp.mean(scaled, axis=1, keepdims=True)
    second_mean = jnp.mean(scaled * normed, axis=1, keepdims=True)
    result = inv_std * (scaled - first_mean - normed * second_mean)
    return (result, jnp.sum(upstream * normed, axis=0), jnp.sum(upstream, axis=0))


def tap_plan(rows_held, span_len, count):
    taps = max(-(-(i * rows_held % D + rows_held) // D) for i in range(count))
    first = [min(i * rows_held // D, span_len - taps) for i in range(count)]
    offset = [i * rows_held - f * D for i, f in enumerate(first)]
    return taps, offset, [span_len - taps - f for f in first]


def xor_order(blocks):
    moved = by_xor(blocks)
    return [moved[0], moved[2], moved[1], moved[3]]


def natural_order(blocks):
    return by_xor([blocks[0], blocks[2], blocks[1], blocks[3]])


def taps_kernel(place_ref, plan_ref, iso_a_ref, iso_b_ref, wide_a_ref, wide_b_ref, tall_ref):
    t = place_ref[1]
    for i, (held_ref, wide_ref) in enumerate(((iso_a_ref, wide_a_ref), (iso_b_ref, wide_b_ref))):
        rows = held_ref.shape[0]
        tall_ref[...] = jnp.zeros_like(tall_ref)
        at = pl.ds(pl.multiple_of(plan_ref[2 + i], 8), rows)
        tall_ref[at, :] = held_ref[...].astype(F32)
        for j in range(wide_ref.shape[1] // 128):
            for slot, k in enumerate(XOR):
                at = pl.ds(pl.multiple_of(j * D + (t ^ k) * 128, 128), 128)
                wide_ref[slot * 128 : (slot + 1) * 128, j * 128 : (j + 1) * 128] = tall_ref[
                    at, :
                ].astype(BF)


def tap_columns(place, plan, iso_a, iso_b, taps):
    width = iso_a.shape[1]
    out = [shape_of(D, n * width, kind=BF) for n in taps]
    return pl.pallas_call(
        taps_kernel,
        in_specs=[scalars()] * 2 + [whole(iso_a), whole(iso_b)],
        out_specs=[whole(v) for v in out],
        out_shape=out,
        scratch_shapes=[pltpu.VMEM((max(taps) * D, width), F32)],
        compiler_params=PARAMS,
        cost_estimate=cost(0, iso_a, iso_b, *out),
    )(place, plan, iso_a, iso_b)


def step_of(rows, span):
    step = lax.broadcasted_iota(jnp.int32, (rows, 128), 0)
    for at in range(span, rows, span):
        step = step - jnp.where(step >= span, span, 0)
    return step


def iso_forward_kernel(spans, reach_ref, index_ref, pair_ref, mate_ref, w_a_ref, w_b_ref, out_ref):
    base = 0
    for scale, w_ref in enumerate((w_a_ref, w_b_ref)):
        rows, span = spans[scale]
        step = step_of(rows, span)
        reach = reach_ref[scale]
        width = out_ref.shape[2]
        taps = w_ref.shape[1] // width
        for g in range(pair_ref.shape[0]):
            to = index_ref[pl.program_id(0) * pair_ref.shape[0] + g]
            x = jnp.concatenate(
                [pair_ref[g, base : base + rows, :], mate_ref[g, base : base + rows, :]], axis=1
            )
            z = jnp.dot(x, w_ref[...], preferred_element_type=F32)
            total = z[:, :width]
            for j in range(1, taps):
                total = jnp.where(step >= 1, pltpu.roll(total, 1, 0), 0.0)
                total = total + z[:, j * width : (j + 1) * width]
            total = jnp.where(step >= reach, pltpu.roll(total, reach, 0), 0.0)
            out_ref[to, base : base + rows, :] = total.astype(BF)
        base += rows


def iso_backward_kernel(
    spans, place_ref, plan_ref, index_ref, grad_ref, pair_ref, mate_ref, w_a_ref, w_b_ref, *refs
):
    ga_ref, gb_ref, backs, (cols_ref, sum_a_ref, sum_b_ref) = refs[0], refs[1], refs[2:6], refs[6:]
    t = place_ref[1]
    base = 0
    for scale, (w_ref, gw_ref) in enumerate(((w_a_ref, sum_a_ref), (w_b_ref, sum_b_ref))):
        rows, span = spans[scale]
        step = step_of(rows, span)
        reach = plan_ref[scale]
        width = grad_ref.shape[2]
        taps = w_ref.shape[1] // width
        count = grad_ref.shape[0]
        for g in range(count):
            part = grad_ref[g, base : base + rows, :].astype(F32)
            turn = jnp.where(reach > 0, rows - reach, 0)
            part = jnp.where(step + reach < span, pltpu.roll(part, turn, 0), 0.0)
            for j in range(taps - 1, -1, -1):
                cols_ref[g * rows : (g + 1) * rows, j * width : (j + 1) * width] = part.astype(BF)
                if j:
                    part = jnp.where(step + 1 < span, pltpu.roll(part, rows - 1, 0), 0.0)
            back = dot_nt(cols_ref[g * rows : (g + 1) * rows, : taps * width], w_ref[...])
            back = back.astype(BF)
            to = index_ref[pl.program_id(0) * count + g] if backs[0].shape[0] > 1 else 0
            for i, back_ref in enumerate(backs):
                back_ref[to, base : base + rows, :] = back[:, i * 128 : (i + 1) * 128]
        for half, x_ref in enumerate((pair_ref, mate_ref)):
            x = jnp.concatenate([x_ref[g, base : base + rows, :] for g in range(count)], axis=0)
            grad = dot_tn(x, cols_ref[: count * rows, : taps * width])
            for j in range(taps):
                for i in range(2):
                    k = XOR[2 * half + i]
                    at = pl.ds(pl.multiple_of(j * D + (t ^ k) * 128, 128), 128)
                    new = grad[i * 128 : (i + 1) * 128, j * width : (j + 1) * width]

                    @pl.when(pl.program_id(0) == 0)
                    def _():
                        gw_ref[at, :] = new

                    @pl.when(pl.program_id(0) > 0)
                    def _():
                        gw_ref[at, :] = gw_ref[at, :] + new

        base += rows

    @pl.when(pl.program_id(0) == pl.num_programs(0) - 1)
    def _():
        for i, (out_ref, sum_ref) in enumerate(((ga_ref, sum_a_ref), (gb_ref, sum_b_ref))):
            at = pl.ds(pl.multiple_of(plan_ref[2 + i], 8), out_ref.shape[0])
            out_ref[...] = sum_ref[at, :]


def iso_forward(reach, index, pair_all, mate_all, wide_a, wide_b, spans):
    groups, rows, half = pair_all.shape
    width = half // 2
    several = 4
    whole = lambda array: pl.BlockSpec(array.shape, lambda i: (0,) * len(array.shape))
    block = lambda width: pl.BlockSpec((several, rows, width), lambda i: (i, 0, 0))
    flops = 2 * groups * sum(r * D * w.shape[1] for (r, _), w in zip(spans, (wide_a, wide_b)))
    return pl.pallas_call(
        partial(iso_forward_kernel, spans),
        grid=(groups // several,),
        in_specs=[
            pl.BlockSpec(memory_space=pltpu.SMEM),
            pl.BlockSpec(memory_space=pltpu.SMEM),
            block(half),
            block(half),
            whole(wide_a),
            whole(wide_b),
        ],
        out_specs=pl.BlockSpec((groups, rows, width), lambda i: (0, 0, 0)),
        out_shape=jax.ShapeDtypeStruct((groups, rows, width), BF),
        compiler_params=pltpu.CompilerParams(vmem_limit_bytes=50 << 20),
        cost_estimate=pl.CostEstimate(
            flops=flops, bytes_accessed=2 * groups * rows * (D + width), transcendentals=0
        ),
    )(reach, index, pair_all, mate_all, wide_a, wide_b)


def iso_backward(place, plan, index, grad_all, pair_all, mate_all, wide_a, wide_b, spans, held):
    groups, rows, half = pair_all.shape
    width = half // 2
    several = 4 if groups <= 8 else 1
    block = lambda width: pl.BlockSpec((several, rows, width), lambda i, *_: (i, 0, 0))
    taps = [w.shape[1] // width for w in (wide_a, wide_b)]
    out = [shape_of(n, width) for n in held] + [shape_of(groups, rows, width, kind=BF)] * 4
    flops = 4 * groups * sum(r * D * w.shape[1] for (r, _), w in zip(spans, (wide_a, wide_b)))
    if several > 1:
        back = whole(out[2])
    else:
        back = pl.BlockSpec((1, rows, width), lambda i, place, plan, index: (index[i], 0, 0))
    specs = pltpu.PrefetchScalarGridSpec(
        num_scalar_prefetch=3,
        grid=(groups // several,),
        in_specs=[block(width), block(half), block(half), whole(wide_a), whole(wide_b)],
        out_specs=[whole(out[0]), whole(out[1])] + [back] * 4,
        scratch_shapes=[
            pltpu.VMEM((several * max(r for r, _ in spans), max(taps) * width), BF),
            pltpu.VMEM((taps[0] * D, width), F32),
            pltpu.VMEM((taps[1] * D, width), F32),
        ],
    )
    return pl.pallas_call(
        partial(iso_backward_kernel, spans),
        grid_spec=specs,
        out_shape=out,
        compiler_params=PARAMS,
        cost_estimate=cost(flops, grad_all, pair_all, mate_all, wide_a, wide_b, *out),
    )(place, plan, index, grad_all, pair_all, mate_all, wide_a, wide_b)


def whole(array):
    return pl.BlockSpec(array.shape, lambda *_: (0,) * len(array.shape))


def scalars():
    return pl.BlockSpec(memory_space=pltpu.SMEM)


def cost(flops, *arrays):
    size = sum(a.size * a.dtype.itemsize for a in arrays)
    return pl.CostEstimate(flops=int(flops), bytes_accessed=int(size), transcendentals=0)


def shape_of(*dims, kind=F32):
    return jax.ShapeDtypeStruct(dims, kind)


def assemble(wa_ref, wb_ref, index_ref, refs):
    rows_a, rows_b = wa_ref.shape[0] // len(refs), wb_ref.shape[0] // len(refs)
    for i, ref in enumerate(refs):
        at = pl.ds(pl.multiple_of(index_ref[i] * rows_a, rows_a), rows_a)
        wa_ref[at, :] = ref[:rows_a, :]
        at = pl.ds(pl.multiple_of(index_ref[i] * rows_b, rows_b), rows_b)
        wb_ref[at, :] = ref[rows_a : rows_a + rows_b, :]


def strided(ref, start, count, stride):
    parts = [ref[j, pl.ds(start, count, stride=stride), :] for j in range(ref.shape[0])]
    return jnp.concatenate(parts, axis=1).astype(BF)


def positions(rows_held, stride, count):
    taps = max(-(-(i * rows_held % D + rows_held) // D) for i in range(count))
    return taps, [min(i * rows_held // D, stride - taps) for i in range(count)]


def down_kernel(count, place_ref, index_ref, *refs):
    blocks, parts, refs = refs[:4], refs[4 : 4 + count], refs[4 + count :]
    act_ref, low_ref, full_ref, send_ref, vec_ref, xs_ref, wa_ref, wb_ref = refs
    t = place_ref[1]
    rows = full_ref.shape[0]
    for k, part in zip(XOR, blocks):
        value = part[:rows, :]
        vec = part[rows:, :].astype(F32)
        vec_ref[:, lane_at(t, k)] = vec[:8] + vec[8:16] + vec[16:24]
        xs_ref[t ^ k, :rows, :] = value.astype(F32)
        full_ref[:, lane_at(t, k)] = value
    xs_ref[:, rows:, :] = jnp.zeros((4, xs_ref.shape[1] - rows, 128), F32)
    assemble(wa_ref, wb_ref, index_ref, parts)
    base = 0
    for stride, weight in ((SA, wa_ref), (SB, wb_ref)):
        size = -(-rows // stride // 16) * 16
        taps, starts = positions(weight.shape[0] // count, stride, count)
        for i, start in enumerate(starts):
            for j in range(taps):
                part = xs_ref[t, pl.ds(start + j, size, stride=stride), :]
                send_ref[i, base + j * size : base + (j + 1) * size, :] = part.astype(BF)
        base += taps * size
    base = 0
    for stride, weight in ((SA, wa_ref), (SB, wb_ref)):
        count = -(-rows // stride // 16) * 16
        total = jnp.zeros((count, weight.shape[1]), F32)
        for r in range(stride):
            window = strided(xs_ref, r, count, stride)
            total = total + dot(window, weight[r * D : (r + 1) * D, :])
        total = jnp.tanh(total)
        act_ref[base : base + count, :] = total
        low_ref[base : base + count, :] = total.astype(BF)
        base += count


def down_forward(place, index, blocks, parts, counts, small, tall):
    rows, width = blocks[0].shape
    rows = rows - 32
    count = len(parts)
    taps_a, _ = positions(SA * D // count, SA, count)
    taps_b, _ = positions(SB * D // count, SB, count)
    out = [
        shape_of(small, width),
        shape_of(small, width, kind=BF),
        shape_of(rows, D, kind=BF),
        shape_of(count, taps_a * counts[0] + taps_b * counts[1], width, kind=BF),
        shape_of(8, D),
    ]
    return pl.pallas_call(
        partial(down_kernel, len(parts)),
        in_specs=[scalars()] * 2 + [whole(v) for v in (*blocks, *parts)],
        out_specs=[whole(v) for v in out],
        out_shape=out,
        scratch_shapes=[
            pltpu.VMEM((4, tall, 128), F32),
            pltpu.VMEM((SA * D, width), BF),
            pltpu.VMEM((SB * D, width), BF),
        ],
        compiler_params=PARAMS,
        cost_estimate=cost(4 * rows * D * width, *blocks, *parts, *out),
    )(place, index, *blocks, *parts)


def up_kernel(
    place_ref, own_ref, across_ref, mate_ref, last_ref, pair_ref, far_ref, vec_ref, wa_ref, wb_ref,
    *refs,
):
    sends, (ua_ref, ub_ref, mid_ref, normed_ref, inv_ref, act_ref, ups_ref) = refs[:4], refs[4:]
    t = place_ref[1]
    act = jnp.tanh(
        jnp.concatenate([own_ref[...], across_ref[...], mate_ref[...], last_ref[...]], axis=1)
    )
    down = jnp.concatenate([pair_ref[0], far_ref[0]], axis=1).astype(F32)
    gain = jnp.concatenate([vec_ref[0:1, lane_at(t, k)] for k in XOR], axis=1)
    bias = jnp.concatenate([vec_ref[1:2, lane_at(t, k)] for k in XOR], axis=1)
    middle, (normed, inv_std) = norm_forward(act + down, gain, bias)
    middle = middle.astype(BF)
    for at, k in enumerate(XOR):
        mid_ref[:, lane_at(t, k)] = middle[:, at * 128 : (at + 1) * 128]
    normed_ref[...] = normed
    inv_ref[...] = jnp.broadcast_to(inv_std, inv_ref.shape)
    act_ref[...] = act[:, :128]
    part_rows = sends[0].shape[1]
    base = 0
    for scale, (stride, u_ref, w_ref) in enumerate(((SA, ua_ref, wa_ref), (SB, ub_ref, wb_ref))):
        count = u_ref.shape[0]
        up = jnp.tanh(dot(mid_ref[base : base + count, :], w_ref[...]))
        u_ref[...] = up
        for r in range(stride):
            ups_ref[pl.ds(r, count, stride=stride), :] = up[:, r * 128 : (r + 1) * 128]
        for k, send_ref in zip(XOR, sends):
            at = pl.ds(pl.multiple_of((t ^ k) * part_rows, part_rows), part_rows)
            send_ref[scale] = ups_ref[at, :].astype(BF)
        base += count


def up_forward(place, blocks, pair_all, far_all, vec, weights, counts, part_rows, tall):
    small, width = blocks[0].shape
    out = [
        *[shape_of(2, part_rows, width, kind=BF)] * 4,
        shape_of(counts[0], SA * width),
        shape_of(counts[1], SB * width),
        shape_of(small, D, kind=BF),
        shape_of(small, D),
        shape_of(small, width),
        shape_of(small, width),
    ]
    group = pl.BlockSpec((1,) + pair_all.shape[1:], lambda *_: (0, 0, 0))
    return pl.pallas_call(
        up_kernel,
        grid_spec=pltpu.PrefetchScalarGridSpec(
            num_scalar_prefetch=1,
            grid=(1,),
            in_specs=[whole(v) for v in blocks] + [group, group, whole(vec)]
            + [whole(v) for v in weights],
            out_specs=[whole(v) for v in out],
            scratch_shapes=[pltpu.VMEM((tall, width), F32)],
        ),
        out_shape=out,
        compiler_params=PARAMS,
        cost_estimate=cost(small * D * (SA + SB) * width, *weights, *out),
    )(place, *blocks, pair_all, far_all, vec, *weights)


def rows_kernel(
    place_ref, horizon_ref, index_ref, x_ref, cot_ref, vec_ref, *refs
):
    ups, weights, merges, out_ref, sends = refs[:4], refs[4:8], refs[8:12], refs[12], refs[13:17]
    keep_ref, give_ref, sums_ref, wm_ref, slope_ref, turn_ref = refs[17:23]
    hid_ref, hpre_ref, first_ref, feed_ref, pair_ref, merged_ref = refs[23:]
    t = place_ref[1]
    step = pl.program_id(0)
    tile = x_ref.shape[0]
    at = pl.ds(pl.multiple_of(step * tile, tile), tile)
    @pl.when(step == 0)
    def _():
        for k, merge in zip(XOR, merges):
            count, held = merge.shape[:2]
            for i in range(count):
                rows = pl.ds(pl.multiple_of(index_ref[i] * held, held), held)
                wm_ref[rows, lane_at(t, k)] = merge[i]

    vec = [vec_ref[i : i + 1, :] for i in range(6)]
    x = x_ref[...].astype(F32)
    stored = []
    for scale in range(2):
        for k, up_ref in zip(XOR, ups):
            turn_ref[:, lane_at(t, k)] = up_ref[scale].astype(F32)
        branch, kept = norm_forward(turn_ref[...] + x, vec[0], vec[1])
        stored.append(kept)
        pair_ref[at, scale * D : (scale + 1) * D] = branch.astype(BF)
    merged = dot(pair_ref[at, :], wm_ref[...])
    first, first_kept = norm_forward(merged, vec[2], vec[3])
    first_ref[at, :] = first.astype(BF)
    feed = jnp.zeros((tile, D), F32)
    for k in range(4):
        pre = dot(first_ref[at, :], weights[k][:D, :])
        chance = 0.5 * (1.0 + lax.erf(pre * (0.5**0.5)))
        slope_ref[:, k * D : (k + 1) * D] = chance + pre * (
            jnp.exp(-0.5 * pre * pre) * 0.3989422804014327
        )
        hid_ref[at, k * D : (k + 1) * D] = (pre * chance).astype(BF)
        feed = feed + dot(hid_ref[at, k * D : (k + 1) * D], weights[k][D:, :])
    last, last_kept = norm_forward(merged + feed, vec[4], vec[5])
    time = step * tile + lax.broadcasted_iota(jnp.int32, (tile, 128), 0)
    mask = (time < IN_LEN + horizon_ref[t]).astype(F32)[:, :1]
    last = (last * mask).astype(BF)
    for j in range(4):
        out_ref[j] = last[:, j * 128 : (j + 1) * 128]
    upstream = jnp.concatenate([cot_ref[j] for j in range(4)], axis=1).astype(F32) * mask
    grad_sum, last_gain, last_bias = norm_backward(upstream, vec[4], last_kept)
    feed_ref[at, :] = grad_sum.astype(BF)
    grad_first = jnp.zeros((tile, D), F32)
    for k in range(4):
        grad_hidden = dot_nt(feed_ref[at, :], weights[k][D:, :])
        hpre_ref[at, k * D : (k + 1) * D] = (
            grad_hidden * slope_ref[:, k * D : (k + 1) * D]
        ).astype(BF)
        grad_first = grad_first + dot_nt(hpre_ref[at, k * D : (k + 1) * D], weights[k][:D, :])
    grad_merged, first_gain, first_bias = norm_backward(grad_first, vec[2], first_kept)
    merged_ref[at, :] = (grad_merged + grad_sum).astype(BF)
    gains = jnp.zeros((D,), F32)
    biases = jnp.zeros((D,), F32)
    for scale in range(2):
        grad_branch = dot_nt(merged_ref[at, :], wm_ref[scale * D : (scale + 1) * D, :])
        grad, gain, bias = norm_backward(grad_branch, vec[0], stored[scale])
        gains, biases = gains + gain, biases + bias
        turn_ref[...] = grad
        for k, send_ref in zip(XOR, sends):
            send_ref[scale] = turn_ref[:, lane_at(t, k)].astype(BF)
    sums = (gains, biases, first_gain, first_bias, last_gain, last_bias)
    sums = jnp.concatenate([v[None, :] for v in sums] + [jnp.zeros((2, D), F32)], axis=0)
    sums_ref[...] = jnp.where(step == 0, sums, sums_ref[...] + sums)

    @pl.when(step == pl.num_programs(0) - 1)
    def _():
        wide = keep_ref.shape[1] // 2
        for i, (k, ref) in enumerate(zip(XOR, (keep_ref, keep_ref, give_ref, give_ref))):
            block = slice(i * D, (i + 1) * D)
            to = i % 2 * wide
            ref[:D, to : to + D] = dot_tn(first_ref[...], hpre_ref[:, block]).astype(BF)
            ref[D:, to : to + D] = dot_tn(hid_ref[:, block], feed_ref[...]).astype(BF)
            ref[:, to + D : to + wide] = dot_tn(
                pair_ref[...], merged_ref[:, lane_at(t, k)]
            ).astype(BF)


def rows_step(place, horizon, index, up_rows, x_full, cot_rows, vec, weights, merges):
    part_rows, width = cot_rows.shape[1:]
    steps = 3
    tile = part_rows // steps
    tall, wide = weights[0].shape[0], weights[0].shape[1] + width
    out = [
        shape_of(4, part_rows, width, kind=BF),
        *[shape_of(2, part_rows, width, kind=BF)] * 4,
        shape_of(tall, 2 * wide, kind=BF),
        shape_of(tall, 2 * wide, kind=BF),
        shape_of(8, D),
    ]
    one_way = pl.BlockSpec((4, tile, width), lambda i, place: (0, i, 0))
    two_way = pl.BlockSpec((2, tile, width), lambda i, place: (0, i, 0))
    once = lambda v: pl.BlockSpec(
        v.shape, lambda *_: (0,) * len(v.shape), pipeline_mode=pl.Buffered(1)
    )
    return pl.pallas_call(
        rows_kernel,
        grid_spec=pltpu.PrefetchScalarGridSpec(
            num_scalar_prefetch=1,
            grid=(steps,),
            in_specs=[
                scalars(),
                scalars(),
                pl.BlockSpec((tile, D), lambda i, place: (place[1] * steps + i, 0)),
                one_way,
                whole(vec),
                *[two_way] * 4,
                *[once(v) for v in weights + merges],
            ],
            out_specs=[one_way, *[two_way] * 4, *[whole(v) for v in out[5:]]],
            scratch_shapes=[
                pltpu.VMEM((2 * D, D), BF),
                pltpu.VMEM((tile, 4 * D), F32),
                pltpu.VMEM((tile, D), F32),
                pltpu.VMEM((part_rows, 4 * D), BF),
                pltpu.VMEM((part_rows, 4 * D), BF),
                pltpu.VMEM((part_rows, D), BF),
                pltpu.VMEM((part_rows, D), BF),
                pltpu.VMEM((part_rows, 2 * D), BF),
                pltpu.VMEM((part_rows, D), BF),
            ],
        ),
        out_shape=out,
        compiler_params=PARAMS,
        cost_estimate=cost(6 * part_rows * D * 10 * D, *weights, *merges, *out),
    )(place, horizon, index, x_full, cot_rows, vec, *up_rows, *weights, *merges)


def up_back_kernel(place_ref, *refs):
    held, (ua_ref, ub_ref, mid_ref, wa_ref, wb_ref) = refs[:4], refs[4:9]
    sums_ref, outs = refs[9], refs[10:14]
    grad_ref, kept_ref, rs_ref, cols_ref, part_ref = refs[14:]
    t = place_ref[1]
    part_rows = held[0].shape[1]
    rows = 4 * part_rows
    rs_ref[rows:, :] = jnp.zeros((rs_ref.shape[0] - rows, 128), F32)
    base = column = 0
    for scale, (stride, u_ref, w_ref) in enumerate(((SA, ua_ref, wa_ref), (SB, ub_ref, wb_ref))):
        count, wide = u_ref.shape
        for k, held_ref in zip(XOR, held):
            at = pl.ds(pl.multiple_of((t ^ k) * part_rows, part_rows), part_rows)
            value = held_ref[scale].astype(F32)
            rs_ref[at, :] = value
            kept_ref[at, :] = kept_ref[at, :] + value if scale else value
        for r in range(stride):
            up = u_ref[:, r * 128 : (r + 1) * 128]
            grad = rs_ref[pl.ds(r, count, stride=stride), :] * (1.0 - up * up)
            cols_ref[:count, r * 128 : (r + 1) * 128] = grad.astype(BF)
        grad = cols_ref[:count, :wide]
        part_ref[base : base + count, :] = dot_nt(grad, w_ref[...])
        grad_ref[:, column : column + wide] = dot_tn(mid_ref[base : base + count, :], grad).astype(BF)
        base += count
        column += wide
    part_ref[base:, :] = sums_ref[...]
    for k, out_ref in zip(XOR, outs):
        out_ref[...] = part_ref[:, lane_at(t, k)]


def up_backward(place, res, ua, ub, mid, weights, sums, tall):
    small = mid.shape[0]
    extra = small + sums.shape[0]
    _, part_rows, width = res[0].shape
    out = [
        *[shape_of(extra, width)] * 4,
        shape_of(D, ua.shape[1] + ub.shape[1], kind=BF),
        shape_of(4 * part_rows, width),
    ]
    return pl.pallas_call(
        up_back_kernel,
        in_specs=[scalars()] + [whole(v) for v in (*res, ua, ub, mid, *weights, sums)],
        out_specs=[whole(v) for v in out],
        out_shape=out,
        scratch_shapes=[
            pltpu.VMEM((tall, width), F32),
            pltpu.VMEM((max(ua.shape[0], ub.shape[0]), max(ua.shape[1], ub.shape[1])), BF),
            pltpu.VMEM((extra, D), F32),
        ],
        compiler_params=PARAMS,
        cost_estimate=cost(2 * small * D * out[4].shape[1], *res, ua, ub, mid, *weights, *out),
    )(place, *res, ua, ub, mid, *weights, sums)


def down_weight_kernel(counts, place_ref, plan_ref, index_ref, grad_ref, *refs):
    t = place_ref[1]
    several = grad_ref.shape[0]

    @pl.when(pl.program_id(0) == 0)
    def _():
        for sum_ref in refs[7:9]:
            sum_ref[...] = jnp.zeros_like(sum_ref)

    blocks = refs[:4]
    base = first = 0
    for count, out_ref in zip(counts, refs[7:9]):
        taps = out_ref.shape[0] // D
        for g in range(several):
            grad = grad_ref[g, base : base + count, :]
            for j in range(taps):
                at = slice(first + j * count, first + (j + 1) * count)
                x = jnp.concatenate([v[g, at, :] for v in blocks], axis=1)
                part = dot_tn(x, grad)
                for i, k in enumerate(XOR):
                    to = pl.ds(pl.multiple_of(j * D + (t ^ k) * 128, 128), 128)
                    out_ref[to, :] = out_ref[to, :] + part[i * 128 : (i + 1) * 128]
        base += count
        first += taps * count
    held_ref = refs[-1]
    held_ref[index_ref[pl.program_id(0)]] = grad_ref[0, base:, :].astype(F32)

    @pl.when(pl.program_id(0) == pl.num_programs(0) - 1)
    def _():
        for i in range(2):
            out_ref, sum_ref = refs[4 + i], refs[7 + i]
            at = pl.ds(pl.multiple_of(plan_ref[4 + i], 8), out_ref.shape[0])
            out_ref[...] = sum_ref[at, :]
        total = held_ref[0]
        for i in range(1, held_ref.shape[0]):
            total = total + held_ref[i]
        refs[6][...] = total


def down_weight_grad(place, plan, index, grad_all, blocks, counts, taps, held):
    groups, small, width = grad_all.shape
    sums = [pltpu.VMEM((n * D, width), F32) for n in taps]
    rest = small - sum(counts)
    sums.append(pltpu.VMEM((groups, rest, width), F32))
    out = [shape_of(n, width) for n in held] + [shape_of(rest, width)]
    block = lambda v: pl.BlockSpec((1,) + v.shape[1:], lambda i, place, plan, index: (index[i], 0, 0))
    return pl.pallas_call(
        partial(down_weight_kernel, counts),
        grid_spec=pltpu.PrefetchScalarGridSpec(
            num_scalar_prefetch=3,
            grid=(groups,),
            in_specs=[pl.BlockSpec((1, small, width), lambda i, *_: (i, 0, 0))]
            + [block(v) for v in blocks],
            out_specs=[whole(v) for v in out],
            scratch_shapes=sums,
        ),
        out_shape=out,
        compiler_params=PARAMS,
        cost_estimate=cost(8 * blocks[0].size * 4 * width // 2, grad_all, *blocks),
    )(place, plan, index, grad_all, *blocks)


def down_input_kernel(count, place_ref, index_ref, grad_ref, *refs):
    parts, refs = refs[:count], refs[count:]
    outs, (gx_ref, wa_ref, wb_ref) = refs[:4], refs[4:]
    t = place_ref[1]
    rows = outs[0].shape[0]
    assemble(wa_ref, wb_ref, index_ref, parts)
    base = 0
    for stride, weight in ((SA, wa_ref), (SB, wb_ref)):
        count = -(-rows // stride // 16) * 16
        grad = grad_ref[base : base + count, :]
        for r in range(stride):
            at = pl.ds(r, count, stride=stride)
            part = dot_nt(grad, weight[r * D : (r + 1) * D, :])
            for j in range(4):
                lane = slice(j * 128, (j + 1) * 128)
                if base:
                    gx_ref[j, at, :] = gx_ref[j, at, :] + part[:, lane]
                else:
                    gx_ref[j, at, :] = part[:, lane]
        base += count
    for k, out_ref in zip(XOR, outs):
        out_ref[...] = gx_ref[t ^ k, :rows, :].astype(BF)


def down_input_grad(place, index, grad, parts, rows, tall):
    width = grad.shape[1]
    out = [shape_of(rows, width, kind=BF)] * 4
    return pl.pallas_call(
        partial(down_input_kernel, len(parts)),
        in_specs=[scalars()] * 2 + [whole(v) for v in (grad, *parts)],
        out_specs=[whole(v) for v in out],
        out_shape=out,
        scratch_shapes=[
            pltpu.VMEM((4, tall, 128), F32),
            pltpu.VMEM((SA * D, width), BF),
            pltpu.VMEM((SB * D, width), BF),
        ],
        compiler_params=PARAMS,
        cost_estimate=cost(4 * rows * D * width, grad, *parts, *out),
    )(place, index, grad, *parts)


def body(
    signal,
    horizon,
    down_a,
    iso_a,
    up_a,
    down_b,
    iso_b,
    up_b,
    merge_w,
    ff_in,
    ff_out,
    norm_gain,
    norm_bias,
    first_gain,
    first_bias,
    last_gain,
    last_bias,
    cotangent,
):
    row_count, col_count = signal.shape
    part_rows = row_count // 4
    counts = (row_count // SA, -(-row_count // SB // 16) * 16)
    small = counts[0] + counts[1]
    tall = max(counts[0] * SA, counts[1] * SB)
    spans = ((counts[0], MA), (counts[1], MB))
    t = lax.axis_index("tensor")
    group = lax.axis_index("dp")
    place = jnp.stack([group, t]).astype(jnp.int32)
    count = lax.axis_size("dp")
    index = own_row(ring_places(count))
    taps_a, *taps_plan_a = tap_plan(iso_a.shape[0], MA, count)
    taps_b, *taps_plan_b = tap_plan(iso_b.shape[0], MB, count)
    down_offsets = [
        [i * v.shape[0] - first * D for i, first in enumerate(positions(v.shape[0], stride, count)[1])]
        for v, stride in ((down_a, SA), (down_b, SB))
    ]
    table = [taps_plan_a[1], taps_plan_b[1], taps_plan_a[0], taps_plan_b[0], *down_offsets]
    plan = own_row(np.array(table, np.int32).T)

    vec_own = jnp.stack(
        [norm_gain, norm_bias, first_gain, first_bias, last_gain, last_bias, last_bias, last_bias]
    )
    split = [lax.reduce_precision(vec_own, 8, 7)]
    split.append(lax.reduce_precision(vec_own - split[0], 8, 7))
    split.append(vec_own - split[0] - split[1])
    split.append(jnp.zeros_like(vec_own))
    x_own = jnp.concatenate([signal] + [v.astype(BF) for v in split], axis=0)
    parts, x_blocks = ring_list(
        jnp.concatenate([down_a, down_b, merge_w], axis=0),
        halves=True,
        beside=(
            lambda _: [swap(x_own, 2)],
            lambda held: [swap(x_own, 1), swap(held[0], 1)],
        ),
    )
    x_blocks = [x_own] + x_blocks

    ff_own, x_blocks[1] = together(jnp.concatenate([ff_in, ff_out], axis=0), x_blocks[1])
    ff_blocks = four(ff_own)
    up_held_a, up_held_b, parts[-1] = together(
        up_a.reshape(up_a.shape[0], -1), up_b.reshape(up_b.shape[0], -1), parts[-1]
    )
    w_up_a = lax.all_gather(up_held_a, "dp", axis=0, tiled=True)
    w_up_b = lax.all_gather(up_held_b, "dp", axis=0, tiled=True)
    act, low, x_full, x_send, vec = down_forward(
        place, index, x_blocks, parts, counts, small, tall
    )
    iso_held = after((iso_a, iso_b), low)
    wide_a, wide_b = tap_columns(place, plan, *iso_held, (taps_a, taps_b))

    low_across = swap(low, 2)
    (cot_held,) = after((cotangent,), low_across)
    cot_rows = lax.all_to_all(
        cot_held.reshape(4, part_rows, col_count), "tensor", 0, 0, tiled=True
    )
    pair_all = ring_stack(jnp.concatenate([low, low_across], axis=1))
    (pair_all,) = after((pair_all,), cot_rows, w_up_a, ff_blocks[1])
    far_all = swap(pair_all, 1)
    merge_own = jnp.stack([v[down_a.shape[0] + down_b.shape[0] :] for v in parts])
    (merge_own,) = after((merge_own,), pair_all)
    merge_blocks = four(merge_own)
    iso_part = iso_forward(plan, index, pair_all, far_all, wide_a, wide_b, spans)
    iso_part, w_up_b = together(iso_part, w_up_b)
    iso_pre = exchange_sum(iso_part)
    *send, up_act_a, up_act_b, middle, normed, inv_std, iso_own = up_forward(
        place, four(iso_pre), pair_all, far_all, vec, (w_up_a, w_up_b), counts, part_rows, tall
    )
    (x_send,) = after((x_send,), iso_pre)
    x_pos = lax.all_to_all(x_send, "dp", 0, 0, tiled=True)
    up_rows = exchange(send)
    (x_full,) = after((x_full,), x_pos)
    last, *out = rows_step(
        place, horizon, index, up_rows, x_full, cot_rows, vec, ff_blocks, merge_blocks
    )
    res_send, (keep_w, give_w, sums) = out[:4], out[4:]
    res = exchange(res_send)
    (keep_w,) = after((keep_w,), res_send[1])
    sum_w = (keep_w.astype(F32) + swap(give_w, 1).astype(F32)).astype(BF)
    sum_w = lax.psum_scatter(sum_w, "dp", scatter_dimension=0, tiled=True)

    *mid_parts, grad_up, resid = up_backward(
        place, res, up_act_a, up_act_b, middle, (w_up_a, w_up_b), sums, tall
    )
    sum_up = lax.psum_scatter(grad_up, "dp", scatter_dimension=0, tiled=True)
    near = mid_parts[0] + swap(mid_parts[2], 1)
    far = mid_parts[1] + swap(mid_parts[3], 1)
    crossed = swap(jnp.concatenate([far, near], axis=1).astype(BF), 2).astype(F32)
    keep = jnp.concatenate([near, far], axis=1) + crossed
    grad_middle = jnp.concatenate([keep, swap(keep, 1)], axis=1)
    last, x_pos, grad_middle = together(last, x_pos, grad_middle)
    sums = grad_middle[small:, :col_count]
    grad_middle = grad_middle[:small]
    series_out = lax.all_to_all(last, "tensor", 0, 0, tiled=True)
    x_pos = four(x_pos)
    x_gain = jnp.concatenate(xor_order(lanes(vec[:1])), axis=1)
    grad_inner, gain_mid, bias_mid = norm_backward(grad_middle, x_gain, (normed, inv_std[:, :1]))
    grad_inner = grad_inner[:, :col_count]
    grad_ipre_all = ring_stack((grad_inner * (1.0 - iso_own * iso_own)).astype(BF))
    grad_iso_a, grad_iso_b, *back = iso_backward(
        place, plan, index, grad_ipre_all, pair_all, far_all, wide_a, wide_b, spans,
        (iso_a.shape[0], iso_b.shape[0]),
    )
    series_out, *back = together(series_out, *back)
    series_out = series_out.reshape(row_count, col_count)
    own_back = own_sum(back)
    sum_w, own_back = together(sum_w, own_back)
    wide = D + col_count
    sum_w = sum_w[:, :wide].astype(F32) + swap(sum_w[:, wide:], 2).astype(F32)
    sum_merge = sum_w[:, D:]
    grad_down = exchange_sum(own_back)
    grad_dpre = ((grad_down + grad_inner) * (1.0 - act * act)).astype(BF)
    x_parts = down_input_grad(place, index, grad_dpre, parts, row_count, tall)
    sums = sums + jnp.pad(
        jnp.stack([gain_mid[:col_count], bias_mid[:col_count]]), ((0, 6), (0, 0))
    )
    sums = jnp.pad(sums, ((0, 8), (0, 0))).astype(BF)
    grad_dpre_all = ring_stack(jnp.concatenate([grad_dpre, sums], axis=0))
    ff_total = lax.all_gather(sum_w[:, :D].astype(BF), "dp", axis=0, tiled=True)
    grad_dpre_all, ff_total = together(grad_dpre_all, ff_total)
    sum_down_a, sum_down_b, sums = down_weight_grad(
        place, plan, index, grad_dpre_all, x_pos, counts,
        [positions(v.shape[0], n, count)[0] for v, n in ((down_a, SA), (down_b, SB))],
        (down_a.shape[0], down_b.shape[0]),
    )
    grad_input = own_sum(x_parts) + resid

    ff_total = ff_total.astype(F32)
    sum_up = sum_up.astype(F32)
    sum_up_a = sum_up[:, : SA * col_count].reshape(up_a.shape)
    sum_up_b = sum_up[:, SA * col_count :].reshape(up_b.shape)
    return (
        series_out,
        grad_input,
        sum_down_a,
        grad_iso_a,
        sum_up_a,
        sum_down_b,
        grad_iso_b,
        sum_up_b,
        sum_merge,
        ff_total[:D],
        ff_total[D:],
        sums[0],
        sums[1],
        sums[2],
        sums[3],
        sums[4],
        sums[5],
    )


def solution(mesh):
    in_specs = (
        P("dp", "tensor"),
        P("dp"),
        P("dp", "tensor"),
        P("dp", "tensor"),
        P("dp", None, "tensor"),
        P("dp", "tensor"),
        P("dp", "tensor"),
        P("dp", None, "tensor"),
        P("dp", "tensor"),
        P(None, "tensor"),
        P("tensor", None),
        P("tensor"),
        P("tensor"),
        P("tensor"),
        P("tensor"),
        P("tensor"),
        P("tensor"),
        P("dp", "tensor"),
    )
    out_specs = (
        P("dp", "tensor"),
        P("dp", "tensor"),
        P("dp", "tensor"),
        P("dp", "tensor"),
        P("dp", None, "tensor"),
        P("dp", "tensor"),
        P("dp", "tensor"),
        P("dp", None, "tensor"),
        P("dp", "tensor"),
        P(None, "tensor"),
        P("tensor", None),
        P("tensor"),
        P("tensor"),
        P("tensor"),
        P("tensor"),
        P("tensor"),
        P("tensor"),
    )
    return jax.shard_map(body, mesh=mesh, in_specs=in_specs, out_specs=out_specs, check_vma=False)
```

time: 616 us -> 549 us (0.89)
  starting transfers between devices: 111 us -> 69.5 us
  between operations: 49.8 us -> 15.3 us
  waiting for transfers between devices: 231 us -> 252 us
  Pallas kernels: 97.7 us -> 112 us
  other arithmetic: 37.9 us -> 24.6 us
  local copies, waits for them, and re-layouts: 51.5 us -> 38.9 us
    ppermute x26 -> x2, waiting for transfers between devices: 84.6 us -> 5.04 us  [the longest x1 2.98 us: ring_list(): second = lax.ppermute(behind[half:], 'dp', down)]
    ppermute x32 -> x35, waiting for transfers between devices: 43.4 us -> 114 us  [swap(): return lax.ppermute(value, 'tensor', [(i, i ^ mask) for i in range(4)])]
    all_to_all x2 -> x1, waiting for transfers between devices: 49 us -> 0.01 us  [exchange_sum(): got = lax.all_to_all(blocks.astype(BF), 'dp', 0, 0, tiled=True)]
    ppermute x6 -> x12, waiting for transfers between devices: 2.56 us -> 42.2 us  [ring_list(): behind = lax.ppermute(behind, 'dp', down)]
    ppermute x26 -> x2, starting transfers between devices: 40.8 us -> 2.03 us  [the longest x1 1.29 us: ring_list(): second = lax.ppermute(behind[half:], 'dp', down)]
    ppermute x8 -> x15, waiting for transfers between devices: 15.5 us -> 43.5 us  [ring_list(): ahead = lax.ppermute(ahead, 'dp', up)]
    all_gather x1 -> x2, waiting for transfers between devices: 0.01 us -> 26.5 us  [the longest x1 26.5 us: body(): w_up_b = lax.all_gather(up_held_b, 'dp', axis=0, tiled=True)]
    pallas_call x4 -> x5, Pallas kernels: 44.8 us -> 58.3 us  [the longest x1 22.8 us: iso_backward(): pl.pallas_call(partial(iso_backward_kernel, spans), grid_spec=specs, out_...]
  transfers between devices with their start and end apart: 83 -> 73, of which waited for: 37 -> 35; matrix products, arithmetic and copies ran while one was open for 11% -> 7% of each run, Pallas kernels for 10% -> 15%
where the time goes in v3:
time: 549 us; the launch traced here: 540 us
  waiting for transfers between devices  252 us (46%)
  Pallas kernels  112 us (20%)
  starting transfers between devices  69.5 us (13%)
  local copies, waits for them, and re-layouts  38.9 us (7%)
  blocking collectives  27.3 us (5%)
  other arithmetic  24.6 us (4%)
  between operations  15.3 us (3%)
    ppermute x35, waiting for transfers between devices, swap(): return lax.ppermute(value, 'tensor', [(i, i ^ mask) for i in range(4)])  114 us
    ppermute x15, waiting for transfers between devices, ring_list(): ahead = lax.ppermute(ahead, 'dp', up)  43.5 us
    ppermute x12, waiting for transfers between devices, ring_list(): behind = lax.ppermute(behind, 'dp', down)  42.2 us
    pallas_call x1, Pallas kernels, rows_step(): pl.pallas_call(rows_kernel, grid_spec=pltpu.PrefetchScalarGridSpec(num_sc...  29 us
    all_to_all x1, blocking collectives, exchange_sum(): got = lax.all_to_all(blocks.astype(BF), 'dp', 0, 0, tiled=True)  27.3 us
    all_gather x1, waiting for transfers between devices, body(): w_up_b = lax.all_gather(up_held_b, 'dp', axis=0, tiled=True)  26.5 us
    unnamed x132, local copies, waits for them, and re-layouts  25.5 us
    pallas_call x1, Pallas kernels, iso_backward(): pl.pallas_call(partial(iso_backward_kernel, spans), grid_spec=specs, out_...  22.8 us
  transfers between devices with their start and end apart: 73, of which 35 were waited for; matrix products, arithmetic and copies ran while one was open for 7% of the time, Pallas kernels for 15%

profile of v3, /device:TPU:0, one launch (start us, length us, event | category | flops | bytes accessed | tf_op | source)
XLA Modules:
  0.0 540.0 jit_solution(4997355324447786823)
XLA Ops:
  16.4 7.8 %collective-permute-done.refs_5_.refs_1_ = bf16[1920,128]{1,0:T(8,128)(2,1)S(1)} collective-permute-done((bf16[1920,128]{1,0:T(8,128)(2,1)S(1)}, bf16[1920,128]{1,0:T(8,128)(2,1)S(1)}, u32[]{:S(2)}, u32[]{:S(2)}) %collective-permute-start) | collective-permute-done | bytes 491552 | tf_op jit(solution)/shard_map/ppermute | solution.py:109
  28.9 5.9 %collective-permute-done.2.refs_1_ = bf16[3296,128]{1,0:T(8,128)(2,1)S(1)} collective-permute-done((bf16[3296,128]{1,0:T(8,128)(2,1)S(1)}, bf16[3296,128]{1,0:T(8,128)(2,1)S(1)}, u32[]{:S(2)}, u32[]{:S(2)}) %collective-permute-start.2) | collective-permute-done | bytes 843808 | tf_op jit(solution)/shard_map/ppermute | solution.py:42
  43.6 6.8 %collective-permute-done.8.refs_10_.refs_6_ = bf16[1920,128]{1,0:T(8,128)(2,1)S(1)} collective-permute-done((bf16[1920,128]{1,0:T(8,128)(2,1)S(1)}, bf16[1920,128]{1,0:T(8,128)(2,1)S(1)}, u32[]{:S(2)}, u32[]{:S(2)}) %collective-permute-start.8) | collective-permute-done | bytes 491552 | tf_op jit(solution)/shard_map/ppermute | solution.py:112
  65.8 11.8 %shard_map.323 = (f32[480,128]{1,0:T(8,128)}, bf16[480,128]{1,0:T(8,128)(2,1)}, bf16[3264,512]{1,0:T(8,128)(2,1)}, bf16[8,960,128]{2,1,0:T(8,128)(2,1)}, f32[8,512]{1,0:T(8,128)}) custom-call(s32[2]{0:T(128)} %pad_add_fusion.place_ref, s32[8]{0:T(128)} %fusion.7.index_ref, bf16[3296,128]{1,0:T(8,128)(2,1)} %copy-done.10, bf16[3296,128]{1,0:T(8,128)(2,1)} %copy-done.27, ...), custom_call_target="tpu_custom_call" | custom-call | flops 855638016 | bytes 13000704 | tf_op jit(solution)/shard_map/pallas_call | solution.py:444
  93.0 14.1 %collective-permute-done.15 = bf16[480,256]{1,0:T(8,128)(2,1)S(1)} collective-permute-done((bf16[480,256]{1,0:T(8,128)(2,1)}, bf16[480,256]{1,0:T(8,128)(2,1)S(1)}, u32[]{:S(2)}, u32[]{:S(2)}) %collective-permute-start.15) | collective-permute-done | bytes 245792 | tf_op jit(solution)/shard_map/ppermute | solution.py:112
  109.2 6.3 %collective-permute-done.16 = bf16[480,256]{1,0:T(8,128)(2,1)S(1)} collective-permute-done((bf16[480,256]{1,0:T(8,128)(2,1)S(1)}, bf16[480,256]{1,0:T(8,128)(2,1)S(1)}, u32[]{:S(2)}, u32[]{:S(2)}) %collective-permute-start.16) | collective-permute-done | bytes 245792 | tf_op jit(solution)/shard_map/ppermute | solution.py:109
  117.1 6.0 %collective-permute-done.18 = bf16[480,256]{1,0:T(8,128)(2,1)S(1)} collective-permute-done((bf16[480,256]{1,0:T(8,128)(2,1)S(1)}, bf16[480,256]{1,0:T(8,128)(2,1)S(1)}, u32[]{:S(2)}, u32[]{:S(2)}) %collective-permute-start.18) | collective-permute-done | bytes 245792 | tf_op jit(solution)/shard_map/ppermute | solution.py:109
  132.5 7.2 %shard_map.325 = bf16[8,480,128]{2,1,0:T(8,128)(2,1)S(1)} custom-call(s32[6]{0:T(128)S(1)} %copy-done.3, s32[8]{0:T(128)S(1)} %copy-done.2, bf16[8,480,256]{2,1,0:T(8,128)(2,1)} %copy-done.7, bf16[8,480,256]{2,1,0:T(8,128)(2,1)} %copy-done.21, bf16[512,1152]{1,0:T(8,128)(2,1)S(1)} %copy-done.4, bf16[512,1024]{1,0:T(8,128)(2,1)S(1)} %copy-done.5), custom_call_target="tpu_custom_call" | custom-call | flops 4311744512 | bytes 4915200 | tf_op jit(solution)/shard_map/pallas_call | solution.py:308
  139.8 26.5 %all-gather.6.cloned.1.call-done.wb_ref.refs_8_ = bf16[512,2048]{1,0:T(8,128)(2,1)} async-done(((bf16[64,2048]{1,0:T(8,128)(2,1)}), bf16[512,2048]{1,0:T(8,128)(2,1)}) %all-gather.6.cloned.1.call-update) | async-done | bytes 2097168 | tf_op jit(solution)/shard_map/all_gather | solution.py:875
  166.2 27.3 %all_to_all.25 = bf16[8,480,128]{2,1,0:T(8,128)(2,1)S(1)} all-to-all(bf16[8,480,128]{2,1,0:T(8,128)(2,1)S(1)} %shard_map.325), channel_id=1, replica_groups=mesh['dp'=8,'tensor'=4] {'dp'}, dimensions={0} | all-to-all | bytes 1966080 | tf_op jit(solution)/shard_map/all_to_all | solution.py:149
  204.1 4.9 collective-permute-done.21.across_ref
  212.0 7.9 %shard_map.326 = (bf16[2,816,128]{2,1,0:T(8,128)(2,1)}, bf16[2,816,128]{2,1,0:T(8,128)(2,1)}, bf16[2,816,128]{2,1,0:T(8,128)(2,1)}, bf16[2,816,128]{2,1,0:T(8,12...) custom-call(s32[2]{0:T(128)} %pad_add_fusion.place_ref, ...), custom_call_target="tpu_custom_call" | custom-call | flops 880803840 | bytes 10682368 | tf_op jit(solution)/shard_map/pallas_call | solution.py:504
  223.1 19.4 %all-to-all-done.2.refs_0_ = bf16[8,960,128]{2,1,0:T(8,128)(2,1)S(1)} async-done(((bf16[8,960,128]{2,1,0:T(8,128)(2,1)}), bf16[8,960,128]{2,1,0:T(8,128)(2,1)S(1)}, u32[]{:S(2)}, u32[]{:S(2)}) %all-to-all-start.2) | async-done | bytes 1966112 | tf_op jit(solution)/shard_map/all_to_all | solution.py:900
  243.5 29.0 %shard_map.327 = (bf16[4,816,128]{2,1,0:T(8,128)(2,1)}, bf16[2,816,128]{2,1,0:T(8,128)(2,1)}, bf16[2,816,128]{2,1,0:T(8,128)(2,1)}, bf16[2,816,128]{2,1,0:T(8,12...) custom-call(s32[2]{0:T(128)} %pad_add_fusion.place_ref, ...), custom_call_target="tpu_custom_call" | custom-call | flops 12834570240 | bytes 13008896 | tf_op jit(solution)/shard_map/pallas_call | solution.py:620
  272.6 5.1 collective-permute-done.46
  284.9 9.4 %collective-permute-done.34.refs_3_ = bf16[2,816,128]{2,1,0:T(8,128)(2,1)S(1)} collective-permute-done((bf16[2,816,128]{2,1,0:T(8,128)(2,1)S(1)}, bf16[2,816,128]{2,1,0:T(8,128)(2,1)S(1)}, u32[]{:S(2)}, u32[]{:S(2)}) %collective-permute-start.34) | collective-permute-done | bytes 417824 | tf_op jit(solution)/shard_map/ppermute | solution.py:42
  294.4 9.4 %collective-permute-done.32.refs_1_ = bf16[2,816,128]{2,1,0:T(8,128)(2,1)S(1)} collective-permute-done((bf16[2,816,128]{2,1,0:T(8,128)(2,1)S(1)}, bf16[2,816,128]{2,1,0:T(8,128)(2,1)S(1)}, u32[]{:S(2)}, u32[]{:S(2)}) %collective-permute-start.32) | collective-permute-done | bytes 417824 | tf_op jit(solution)/shard_map/ppermute | solution.py:42
  304.5 9.9 %shard_map.328 = (f32[488,128]{1,0:T(8,128)}, f32[488,128]{1,0:T(8,128)}, f32[488,128]{1,0:T(8,128)}, f32[488,128]{1,0:T(8,128)}, bf16[512,3584]{1,0:T(8,128)(2,1)}, /*index=5*/f32[3264,128]{1,0:T(8,128)}) custom-call(s32[2]{0:T(128)} %pad_add_fusion.place_ref, bf16[2,816,128]{2,1,0:T(8,128)(2,1)} %get-tuple-element.123.refs_0_, ...), custom_call_target="tpu_custom_call" | custom-call | flops 1761607680 | bytes 15548416 | tf_op jit(solution)/shard_map/pallas_call | solution.py:692
  319.8 6.6 %collective-permute-done.37 = bf16[488,256]{1,0:T(8,128)(2,1)S(1)} collective-permute-done((bf16[488,256]{1,0:T(8,128)(2,1)S(1)}, bf16[488,256]{1,0:T(8,128)(2,1)S(1)}, u32[]{:S(2)}, u32[]{:S(2)}) %collective-permute-start.37) | collective-permute-done | bytes 249888 | tf_op jit(solution)/shard_map/ppermute | solution.py:42
  333.3 4.3 all-to-all-start.3
  339.9 6.6 %collective-permute-done.42 = bf16[480,128]{1,0:T(8,128)(2,1)S(1)} collective-permute-done((bf16[480,128]{1,0:T(8,128)(2,1)S(1)}, bf16[480,128]{1,0:T(8,128)(2,1)S(1)}, u32[]{:S(2)}, u32[]{:S(2)}) %collective-permute-start.42) | collective-permute-done | bytes 122912 | tf_op jit(solution)/shard_map/ppermute | solution.py:112
  354.8 4.6 collective-permute-done.45
  360.4 22.8 %shard_map.329 = (f32[4352,128]{1,0:T(8,128)}, f32[3264,128]{1,0:T(8,128)}, bf16[8,480,128]{2,1,0:T(8,128)(2,1)}, bf16[8,480,128]{2,1,0:T(8,128)(2,1)}, bf16[8,4...) custom-call(s32[2]{0:T(128)} %pad_add_fusion.place_ref, s32[6]{0:T(128)} %fusion.8.plan_ref.reach_ref, ...), custom_call_target="tpu_custom_call" | custom-call | flops 8623489024 | bytes 14974976 | tf_op jit(solution)/shard_map/pallas_call | solution.py:351
  389.6 22.6 %collective-permute-done.49 = bf16[8,480,128]{2,1,0:T(8,128)(2,1)S(1)} collective-permute-done((bf16[8,480,128]{2,1,0:T(8,128)(2,1)S(1)}, bf16[8,480,128]{2,1,0:T(8,128)(2,1)S(1)}, u32[]{:S(2)}, u32[]{:S(2)}) %collective-permute-start.49) | collective-permute-done | bytes 983072 | tf_op jit(solution)/shard_map/ppermute | solution.py:42
  413.5 4.2 all-to-all-start.4
  417.9 35.7 %collective-permute-done.61.refs_1_ = bf16[8,960,128]{2,1,0:T(8,128)(2,1)} collective-permute-done((bf16[8,960,128]{2,1,0:T(8,128)(2,1)S(1)}, bf16[8,960,128]{2,1,0:T(8,128)(2,1)}, u32[]{:S(2)}, u32[]{:S(2)}) %collective-permute-start.61) | collective-permute-done | bytes 1966112 | tf_op jit(solution)/shard_map/ppermute | solution.py:42
  467.8 10.0 %shard_map.330 = (bf16[3264,128]{1,0:T(8,128)(2,1)}, bf16[3264,128]{1,0:T(8,128)(2,1)}, bf16[3264,128]{1,0:T(8,128)(2,1)}, bf16[3264,128]{1,0:T(8,128)(2,1)}) custom-call(s32[2]{0:T(128)} %pad_add_fusion.place_ref, s32[8]{0:T(128)} %fusion.7.index_ref, bf16[480,128]{1,0:T(8,128)(2,1)} %copy-done.23, bf16[1920,128]{1,0:T(8,128)(2,1)} %copy-done.13, ...), custom_call_target="tpu_custom_call" | custom-call | flops 855638016 | bytes 7397376 | tf_op jit(solution)/shard_map/pallas_call | solution.py:796
  479.9 5.1 collective-permute-done.55
  491.3 6.3 %collective-permute-done.57 = bf16[496,128]{1,0:T(8,128)(2,1)S(1)} collective-permute-done((bf16[496,128]{1,0:T(8,128)(2,1)S(1)}, bf16[496,128]{1,0:T(8,128)(2,1)S(1)}, u32[]{:S(2)}, u32[]{:S(2)}) %collective-permute-start.57) | collective-permute-done | bytes 127008 | tf_op jit(solution)/shard_map/ppermute | solution.py:109
  498.6 5.4 collective-permute-done.58
  510.0 10.1 %shard_map.331 = (f32[768,128]{1,0:T(8,128)}, f32[1024,128]{1,0:T(8,128)}, f32[16,128]{1,0:T(8,128)}) custom-call(s32[2]{0:T(128)} %pad_add_fusion.place_ref, s32[6]{0:T(128)} %fusion.8.plan_ref.reach_ref, s32[8]{0:T(128)} %fusion.7.index_ref, bf16[8,496,128]{2,1,0:T(8,128)(2,1)} %copy-done.9, bf16[8,960,128]{2,1,0:T(8,128)(2,1)} %copy-done.6, ...), custom_call_target="tpu_custom_call" | custom-call | flops 2013265920 | bytes 8880128 | tf_op jit(solution)/shard_map/pallas_call | solution.py:753
  523.1 4.8 collective-permute-done.52
  (330 shorter events, 161.0 us)
Async XLA Ops:
  7.3 115.8 %all-gather.4.cloned.1.call-start = ((), (), s32[]{:S(2)}) async-start(), calls=%async_computation.7 | async-start | bytes 1769472 | tf_op jit(solution)/shard_map/all_gather | solution.py:874
  10.1 14.2 %collective-permute-start = (bf16[1920,128]{1,0:T(8,128)(2,1)S(1)}, bf16[1920,128]{1,0:T(8,128)(2,1)S(1)}, u32[]{:S(2)}, u32[]{:S(2)}) collective-permute-start(bf16[1920,128]{1,0:T(8,128)(2,1)S(1)} %constant_dynamic-update-slice_fusion.5.refs_4_.refs_0_), channel_id=1, source_target_pairs={{0,8},{8,16},{16,24},{24,28},{28,20},{20,12},{12,4},{4,0},{1,9},{9... | collective-permute-start | bytes 1474568 | tf_op jit(solution)/shard_map/ppermute | solution.py:109
  14.4 20.3 %collective-permute-start.2 = (bf16[3296,128]{1,0:T(8,128)(2,1)S(1)}, bf16[3296,128]{1,0:T(8,128)(2,1)S(1)}, u32[]{:S(2)}, u32[]{:S(2)}) collective-permute-start(bf16[3296,128]{1,0:T(8,128)(2,1)S(1)} %constant_dynamic-update-slice_fusion.refs_0_), channel_id=1, source_target_pairs={{0,2},{1,3},{2,0},{3,1},{4,6},{5,7},{6,4},{7,5},{8,10},{9,11},{10,... | collective-permute-start | bytes 2531336 | tf_op jit(solution)/shard_map/ppermute | solution.py:42
  28.8 23.6 %collective-permute-start.4 = (bf16[3296,128]{1,0:T(8,128)(2,1)S(1)}, bf16[3296,128]{1,0:T(8,128)(2,1)S(1)}, u32[]{:S(2)}, u32[]{:S(2)}) collective-permute-start(bf16[3296,128]{1,0:T(8,128)(2,1)S(1)} %constant_dynamic-update-slice_fusion.refs_0_), channel_id=1, source_target_pairs={{0,1},{1,0},{2,3},{3,2},{4,5},{5,4},{6,7},{7,6},{8,9},{9,8},{10,11... | collective-permute-start | bytes 2531336 | tf_op jit(solution)/shard_map/ppermute | solution.py:42
  36.7 15.8 %collective-permute-start.5 = (bf16[3296,128]{1,0:T(8,128)(2,1)S(1)}, bf16[3296,128]{1,0:T(8,128)(2,1)S(1)}, u32[]{:S(2)}, u32[]{:S(2)}) collective-permute-start(bf16[3296,128]{1,0:T(8,128)(2,1)S(1)} %collective-permute-done.2.refs_1_), channel_id=1, source_target_pairs={{0,1},{1,0},{2,3},{3,2},{4,5},{5,4},{6,7},{7,6},{8,9},{9,8},{10,11... | collective-permute-start | bytes 2531336 | tf_op jit(solution)/shard_map/ppermute | solution.py:42
  61.7 104.6 %all-gather.6.cloned.1.call-start = ((), (), s32[]{:S(2)}) async-start(), calls=%async_computation.8 | async-start | bytes 2359296 | tf_op jit(solution)/shard_map/all_gather | solution.py:875
  84.8 38.3 %collective-permute-start.19 = (bf16[1024,512]{1,0:T(8,128)(2,1)}, bf16[1024,512]{1,0:T(8,128)(2,1)}, u32[]{:S(2)}, u32[]{:S(2)}) collective-permute-start(bf16[1024,512]{1,0:T(8,128)(2,1)} %pad_maximum_fusion.refs_4_), channel_id=1, source_target_pairs={{0,2},{1,3},{2,0},{3,1},{4,6},{5,7},{6,4},{7,5},{8,10},{9,11},{10,... | collective-permute-start | bytes 3145736 | tf_op jit(solution)/shard_map/ppermute | solution.py:42
  86.3 36.8 %all-to-all-start = ((bf16[4,816,128]{2,1,0:T(8,128)(2,1)}), bf16[4,816,128]{2,1,0:T(8,128)(2,1)S(1)}, u32[]{:S(2)}, u32[]{:S(2)}) async-start(bf16[4,816,128]{2,1,0:T(8,128)(2,1)} %bitcast.123), calls=%async_computation | async-start | bytes 1671168 | tf_op jit(solution)/shard_map/all_to_all | solution.py:884
  89.9 17.2 %collective-permute-start.15 = (bf16[480,256]{1,0:T(8,128)(2,1)}, bf16[480,256]{1,0:T(8,128)(2,1)S(1)}, u32[]{:S(2)}, u32[]{:S(2)}) collective-permute-start(bf16[480,256]{1,0:T(8,128)(2,1)} %collective-permute-done.13), channel_id=1, source_target_pairs={{8,0},{16,8},{24,16},{28,24},{20,28},{12,20},{4,12},{0,4},{9,1},{1... | collective-permute-start | bytes 737288 | tf_op jit(solution)/shard_map/ppermute | solution.py:112
  91.6 15.5 %collective-permute-start.14 = (bf16[480,256]{1,0:T(8,128)(2,1)S(1)}, bf16[480,256]{1,0:T(8,128)(2,1)S(1)}, u32[]{:S(2)}, u32[]{:S(2)}) collective-permute-start(bf16[480,256]{1,0:T(8,128)(2,1)S(1)} %collective-permute-done.12), channel_id=1, source_target_pairs={{0,8},{8,16},{16,24},{24,28},{28,20},{20,12},{12,4},{4,0},{1,9},{9... | collective-permute-start | bytes 737288 | tf_op jit(solution)/shard_map/ppermute | solution.py:109
  193.7 48.8 %all-to-all-start.2 = ((bf16[8,960,128]{2,1,0:T(8,128)(2,1)}), bf16[8,960,128]{2,1,0:T(8,128)(2,1)S(1)}, u32[]{:S(2)}, u32[]{:S(2)}) async-start(bf16[8,960,128]{2,1,0:T(8,128)(2,1)} %get-tuple-element.113), calls=%async_computation.2 | async-start | bytes 3932160 | tf_op jit(solution)/shard_map/all_to_all | solution.py:900
  197.4 216.1 %reduce-scatter.3.cloned.1.call-start = ((), (), s32[]{:S(2)}) async-start(), calls=%async_computation.9 | async-start | bytes 2949120 | tf_op jit(solution)/shard_map/reduce_scatter | solution.py:910
  199.0 21.5 %collective-permute-start.27 = (bf16[1024,512]{1,0:T(8,128)(2,1)}, bf16[1024,512]{1,0:T(8,128)(2,1)S(1)}, u32[]{:S(2)}, u32[]{:S(2)}) collective-permute-start(bf16[1024,512]{1,0:T(8,128)(2,1)} %pad_maximum_fusion.refs_4_), channel_id=1, source_target_pairs={{0,1},{1,0},{2,3},{3,2},{4,5},{5,4},{6,7},{7,6},{8,9},{9,8},{10,11... | collective-permute-start | bytes 3145736 | tf_op jit(solution)/shard_map/ppermute | solution.py:42
  199.8 22.3 %collective-permute-start.28 = (bf16[1024,512]{1,0:T(8,128)(2,1)}, bf16[1024,512]{1,0:T(8,128)(2,1)S(1)}, u32[]{:S(2)}, u32[]{:S(2)}) collective-permute-start(bf16[1024,512]{1,0:T(8,128)(2,1)} %collective-permute-done.19.refs_5_), channel_id=1, source_target_pairs={{0,1},{1,0},{2,3},{3,2},{4,5},{5,4},{6,7},{7,6},{8,9},{9,8},{10,11... | collective-permute-start | bytes 3145736 | tf_op jit(solution)/shard_map/ppermute | solution.py:42
  219.8 22.7 %collective-permute-start.24 = (bf16[2,816,128]{2,1,0:T(8,128)(2,1)}, bf16[2,816,128]{2,1,0:T(8,128)(2,1)S(1)}, u32[]{:S(2)}, u32[]{:S(2)}) collective-permute-start(bf16[2,816,128]{2,1,0:T(8,128)(2,1)} %get-tuple-element.118), channel_id=1, source_target_pairs={{0,2},{1,3},{2,0},{3,1},{4,6},{5,7},{6,4},{7,5},{8,10},{9,11},{10,... | collective-permute-start | bytes 1253384 | tf_op jit(solution)/shard_map/ppermute | solution.py:42
  220.6 22.0 %collective-permute-start.25 = (bf16[2,816,128]{2,1,0:T(8,128)(2,1)}, bf16[2,816,128]{2,1,0:T(8,128)(2,1)S(1)}, u32[]{:S(2)}, u32[]{:S(2)}) collective-permute-start(bf16[2,816,128]{2,1,0:T(8,128)(2,1)} %get-tuple-element.119), channel_id=1, source_target_pairs={{0,1},{1,0},{2,3},{3,2},{4,5},{5,4},{6,7},{7,6},{8,9},{9,8},{10,11... | collective-permute-start | bytes 1253384 | tf_op jit(solution)/shard_map/ppermute | solution.py:42
  220.6 22.0 %collective-permute-start.26 = (bf16[2,816,128]{2,1,0:T(8,128)(2,1)}, bf16[2,816,128]{2,1,0:T(8,128)(2,1)}, u32[]{:S(2)}, u32[]{:S(2)}) collective-permute-start(bf16[2,816,128]{2,1,0:T(8,128)(2,1)} %get-tuple-element.120), channel_id=1, source_target_pairs={{0,3},{1,2},{2,1},{3,0},{4,7},{5,6},{6,5},{7,4},{8,11},{9,10},{10,... | collective-permute-start | bytes 1253384 | tf_op jit(solution)/shard_map/ppermute | solution.py:42
  222.1 20.4 %collective-permute-start.30 = (bf16[8,128,128]{2,1,0:T(8,128)(2,1)S(1)}, bf16[8,128,128]{2,1,0:T(8,128)(2,1)}, u32[]{:S(2)}, u32[]{:S(2)}) collective-permute-start(bf16[8,128,128]{2,1,0:T(8,128)(2,1)S(1)} %constant_dynamic-update-slice_fusion.10.refs_8_), channel_id=1, source_target_pairs={{0,1},{1,0},{2,3},{3,2},{4,5},{5,4},{6,7},{7,6},{8,9},{9,8},{10,11... | collective-permute-start | bytes 786440 | tf_op jit(solution)/shard_map/ppermute | solution.py:42
  223.0 19.5 %collective-permute-start.31 = (bf16[8,128,128]{2,1,0:T(8,128)(2,1)}, bf16[8,128,128]{2,1,0:T(8,128)(2,1)}, u32[]{:S(2)}, u32[]{:S(2)}) collective-permute-start(bf16[8,128,128]{2,1,0:T(8,128)(2,1)} %collective-permute-done.29.refs_9_), channel_id=1, source_target_pairs={{0,1},{1,0},{2,3},{3,2},{4,5},{5,4},{6,7},{7,6},{8,9},{9,8},{10,11... | collective-permute-start | bytes 786440 | tf_op jit(solution)/shard_map/ppermute | solution.py:42
  281.8 173.6 %reduce-scatter.5.cloned.1.call-start = ((), (), s32[]{:S(2)}) async-start(), calls=%async_computation.11 | async-start | bytes 4128768 | tf_op jit(solution)/shard_map/reduce_scatter | solution.py:915
  284.3 19.5 %collective-permute-start.32 = (bf16[2,816,128]{2,1,0:T(8,128)(2,1)S(1)}, bf16[2,816,128]{2,1,0:T(8,128)(2,1)S(1)}, u32[]{:S(2)}, u32[]{:S(2)}) collective-permute-start(bf16[2,816,128]{2,1,0:T(8,128)(2,1)S(1)} %copy-done.55), channel_id=1, source_target_pairs={{0,2},{1,3},{2,0},{3,1},{4,6},{5,7},{6,4},{7,5},{8,10},{9,11},{10,... | collective-permute-start | bytes 1253384 | tf_op jit(solution)/shard_map/ppermute | solution.py:42
  333.3 49.9 %all-to-all-start.3 = ((bf16[4,816,128]{2,1,0:T(8,128)(2,1)}), bf16[4,816,128]{2,1,0:T(8,128)(2,1)}, u32[]{:S(2)}, u32[]{:S(2)}) async-start(bf16[4,816,128]{2,1,0:T(8,128)(2,1)} %get-tuple-element.135), calls=%async_computation.3 | async-start | bytes 1671168 | tf_op jit(solution)/shard_map/all_to_all | solution.py:924
  387.5 24.7 %collective-permute-start.49 = (bf16[8,480,128]{2,1,0:T(8,128)(2,1)S(1)}, bf16[8,480,128]{2,1,0:T(8,128)(2,1)S(1)}, u32[]{:S(2)}, u32[]{:S(2)}) collective-permute-start(bf16[8,480,128]{2,1,0:T(8,128)(2,1)S(1)} %add_convert_fusion.1), channel_id=1, source_target_pairs={{0,2},{1,3},{2,0},{3,1},{4,6},{5,7},{6,4},{7,5},{8,10},{9,11},{10,... | collective-permute-start | bytes 2949128 | tf_op jit(solution)/shard_map/ppermute | solution.py:42
  388.7 64.9 %collective-permute-start.61 = (bf16[8,960,128]{2,1,0:T(8,128)(2,1)S(1)}, bf16[8,960,128]{2,1,0:T(8,128)(2,1)}, u32[]{:S(2)}, u32[]{:S(2)}) collective-permute-start(bf16[8,960,128]{2,1,0:T(8,128)(2,1)S(1)} %all-to-all-done.2.refs_0_), channel_id=1, source_target_pairs={{0,2},{1,3},{2,0},{3,1},{4,6},{5,7},{6,4},{7,5},{8,10},{9,11},{10,... | collective-permute-start | bytes 5898248 | tf_op jit(solution)/shard_map/ppermute | solution.py:42
  413.5 45.9 %all-to-all-start.4 = ((bf16[8,480,128]{2,1,0:T(8,128)(2,1)}), bf16[8,480,128]{2,1,0:T(8,128)(2,1)}, u32[]{:S(2)}, u32[]{:S(2)}) async-start(bf16[8,480,128]{2,1,0:T(8,128)(2,1)} %convert_add_fusion), calls=%async_computation.5 | async-start | bytes 1966080 | tf_op jit(solution)/shard_map/all_to_all | solution.py:149
  417.8 91.3 %all-gather.8.cloned.1.call-start = ((), (), s32[]{:S(2)}) async-start(), calls=%async_computation.10 | async-start | bytes 1179648 | tf_op jit(solution)/shard_map/all_gather | solution.py:949
  417.8 91.3 %collective-permute-start.62 = (bf16[8,960,128]{2,1,0:T(8,128)(2,1)S(1)}, bf16[8,960,128]{2,1,0:T(8,128)(2,1)}, u32[]{:S(2)}, u32[]{:S(2)}) collective-permute-start(bf16[8,960,128]{2,1,0:T(8,128)(2,1)S(1)} %all-to-all-done.2.refs_0_), channel_id=1, source_target_pairs={{0,1},{1,0},{2,3},{3,2},{4,5},{5,4},{6,7},{7,6},{8,9},{9,8},{10,11... | collective-permute-start | bytes 5898248 | tf_op jit(solution)/shard_map/ppermute | solution.py:42
  453.6 55.5 %collective-permute-start.63 = (bf16[8,960,128]{2,1,0:T(8,128)(2,1)}, bf16[8,960,128]{2,1,0:T(8,128)(2,1)}, u32[]{:S(2)}, u32[]{:S(2)}) collective-permute-start(bf16[8,960,128]{2,1,0:T(8,128)(2,1)} %collective-permute-done.61.refs_1_), channel_id=1, source_target_pairs={{0,1},{1,0},{2,3},{3,2},{4,5},{5,4},{6,7},{7,6},{8,9},{9,8},{10,11... | collective-permute-start | bytes 5898248 | tf_op jit(solution)/shard_map/ppermute | solution.py:42
  462.1 15.8 %collective-permute-start.53 = (bf16[496,128]{1,0:T(8,128)(2,1)S(1)}, bf16[496,128]{1,0:T(8,128)(2,1)}, u32[]{:S(2)}, u32[]{:S(2)}) collective-permute-start(bf16[496,128]{1,0:T(8,128)(2,1)S(1)} %get-tuple-element.214), channel_id=1, source_target_pairs={{0,8},{8,16},{16,24},{24,28},{28,20},{20,12},{12,4},{4,0},{1,9},{9... | collective-permute-start | bytes 380936 | tf_op jit(solution)/shard_map/ppermute | solution.py:109
  477.8 45.3 %collective-permute-start.50 = (bf16[3264,128]{1,0:T(8,128)(2,1)}, bf16[3264,128]{1,0:T(8,128)(2,1)}, u32[]{:S(2)}, u32[]{:S(2)}) collective-permute-start(bf16[3264,128]{1,0:T(8,128)(2,1)} %get-tuple-element.155), channel_id=1, source_target_pairs={{0,1},{1,0},{2,3},{3,2},{4,5},{5,4},{6,7},{7,6},{8,9},{9,8},{10,11... | collective-permute-start | bytes 2506760 | tf_op jit(solution)/shard_map/ppermute | solution.py:42
  478.0 28.4 %collective-permute-start.51 = (bf16[3264,128]{1,0:T(8,128)(2,1)}, bf16[3264,128]{1,0:T(8,128)(2,1)S(1)}, u32[]{:S(2)}, u32[]{:S(2)}) collective-permute-start(bf16[3264,128]{1,0:T(8,128)(2,1)} %get-tuple-element.157), channel_id=1, source_target_pairs={{0,1},{1,0},{2,3},{3,2},{4,5},{5,4},{6,7},{7,6},{8,9},{9,8},{10,11... | collective-permute-start | bytes 2506760 | tf_op jit(solution)/shard_map/ppermute | solution.py:42
  507.5 20.4 %collective-permute-start.52 = (bf16[3264,128]{1,0:T(8,128)(2,1)}, bf16[3264,128]{1,0:T(8,128)(2,1)}, u32[]{:S(2)}, u32[]{:S(2)}) collective-permute-start(bf16[3264,128]{1,0:T(8,128)(2,1)} %add_convert_fusion.2), channel_id=1, source_target_pairs={{0,2},{1,3},{2,0},{3,1},{4,6},{5,7},{6,4},{7,5},{8,10},{9,11},{10,... | collective-permute-start | bytes 2506760 | tf_op jit(solution)/shard_map/ppermute | solution.py:42
  (99 other events, 1089.6 us)
Sparse Core Ops, SparseCore 0:
  61.8 49.1 all-gather.3
  113.7 52.5 all-gather.5
  281.9 72.8 reduce-scatter.2
  358.3 97.0 reduce-scatter.4
  466.0 39.9 all-gather.7

commit v4 on v3

--- a/solution.py
+++ b/solution.py
@@ -891,21 +891,20 @@
     (merge_own,) = after((merge_own,), pair_all)
     merge_blocks = four(merge_own)
     iso_part = iso_forward(plan, index, pair_all, far_all, wide_a, wide_b, spans)
-    iso_part, w_up_b = together(iso_part, w_up_b)
-    iso_pre = exchange_sum(iso_part)
+    iso_pre, w_up_b = together(exchange_sum(iso_part), w_up_b)
     *send, up_act_a, up_act_b, middle, normed, inv_std, iso_own = up_forward(
         place, four(iso_pre), pair_all, far_all, vec, (w_up_a, w_up_b), counts, part_rows, tall
     )
     (x_send,) = after((x_send,), iso_pre)
     x_pos = lax.all_to_all(x_send, "dp", 0, 0, tiled=True)
     up_rows = exchange(send)
-    (x_full,) = after((x_full,), x_pos)
     last, *out = rows_step(
         place, horizon, index, up_rows, x_full, cot_rows, vec, ff_blocks, merge_blocks
     )
     res_send, (keep_w, give_w, sums) = out[:4], out[4:]
+    x_pos, *res_send = together(x_pos, *res_send)
     res = exchange(res_send)
-    (keep_w,) = after((keep_w,), res_send[1])
+    give_w, res[2] = together(give_w, res[2])
     sum_w = (keep_w.astype(F32) + swap(give_w, 1).astype(F32)).astype(BF)
     sum_w = lax.psum_scatter(sum_w, "dp", scatter_dimension=0, tiled=True)
 

time: 549 us -> 541 us (0.985)
  waiting for transfers between devices: 252 us -> 223 us
  blocking collectives: 27.3 us -> 46.6 us
  starting transfers between devices: 69.5 us -> 76.9 us
  local copies, waits for them, and re-layouts: 38.9 us -> 32.9 us
    all_gather x1, waiting for transfers between devices: 26.5 us -> 0.75 us  [body(): w_up_b = lax.all_gather(up_held_b, 'dp', axis=0, tiled=True)]
    all_to_all x1, waiting for transfers between devices: 19.4 us -> 0.01 us  [body(): x_pos = lax.all_to_all(x_send, 'dp', 0, 0, tiled=True)]
    all_to_all x1, blocking collectives: 27.3 us -> 46.6 us  [exchange_sum(): got = lax.all_to_all(blocks.astype(BF), 'dp', 0, 0, tiled=True)]
    ppermute x35, waiting for transfers between devices: 114 us -> 132 us  [swap(): return lax.ppermute(value, 'tensor', [(i, i ^ mask) for i in range(4)])]
    unnamed x132 -> x136, local copies, waits for them, and re-layouts: 25.5 us -> 22.2 us
  transfers between devices with their start and end apart: 73 -> 73, of which waited for: 35 -> 38; matrix products, arithmetic and copies ran while one was open for 7% -> 7% of each run, Pallas kernels for 15% -> 21%
where the time goes in v4:
time: 541 us; the launch traced here: 531 us
  waiting for transfers between devices  223 us (41%)
  Pallas kernels  112 us (21%)
  starting transfers between devices  76.9 us (14%)
  blocking collectives  46.6 us (9%)
  local copies, waits for them, and re-layouts  32.9 us (6%)
  other arithmetic  24.3 us (4%)
  between operations  15.3 us (3%)
    ppermute x35, waiting for transfers between devices, swap(): return lax.ppermute(value, 'tensor', [(i, i ^ mask) for i in range(4)])  132 us
    all_to_all x1, blocking collectives, exchange_sum(): got = lax.all_to_all(blocks.astype(BF), 'dp', 0, 0, tiled=True)  46.6 us
    ppermute x12, waiting for transfers between devices, ring_list(): behind = lax.ppermute(behind, 'dp', down)  42.7 us
    ppermute x15, waiting for transfers between devices, ring_list(): ahead = lax.ppermute(ahead, 'dp', up)  41.1 us
    pallas_call x1, Pallas kernels, rows_step(): pl.pallas_call(rows_kernel, grid_spec=pltpu.PrefetchScalarGridSpec(num_sc...  29.1 us
    ppermute x15, starting transfers between devices, ring_list(): ahead = lax.ppermute(ahead, 'dp', up)  22.9 us
    pallas_call x1, Pallas kernels, iso_backward(): pl.pallas_call(partial(iso_backward_kernel, spans), grid_spec=specs, out_...  22.8 us
    ppermute x35, starting transfers between devices, swap(): return lax.ppermute(value, 'tensor', [(i, i ^ mask) for i in range(4)])  22.4 us
  transfers between devices with their start and end apart: 73, of which 38 were waited for; matrix products, arithmetic and copies ran while one was open for 7% of the time, Pallas kernels for 21%

profile of v4, /device:TPU:0, one launch (start us, length us, event | category | flops | bytes accessed | tf_op | source)
XLA Modules:
  0.0 531.3 jit_solution(14010949859705187679)
XLA Ops:
  16.5 7.8 %collective-permute-done.refs_5_.refs_1_ = bf16[1920,128]{1,0:T(8,128)(2,1)S(1)} collective-permute-done((bf16[1920,128]{1,0:T(8,128)(2,1)S(1)}, bf16[1920,128]{1,0:T(8,128)(2,1)S(1)}, u32[]{:S(2)}, u32[]{:S(2)}) %collective-permute-start) | collective-permute-done | bytes 491552 | tf_op jit(solution)/shard_map/ppermute | solution.py:109
  28.9 5.9 %collective-permute-done.2.refs_1_ = bf16[3296,128]{1,0:T(8,128)(2,1)S(1)} collective-permute-done((bf16[3296,128]{1,0:T(8,128)(2,1)S(1)}, bf16[3296,128]{1,0:T(8,128)(2,1)S(1)}, u32[]{:S(2)}, u32[]{:S(2)}) %collective-permute-start.2) | collective-permute-done | bytes 843808 | tf_op jit(solution)/shard_map/ppermute | solution.py:42
  42.8 8.5 %collective-permute-done.8.refs_10_.refs_6_ = bf16[1920,128]{1,0:T(8,128)(2,1)S(1)} collective-permute-done((bf16[1920,128]{1,0:T(8,128)(2,1)S(1)}, bf16[1920,128]{1,0:T(8,128)(2,1)S(1)}, u32[]{:S(2)}, u32[]{:S(2)}) %collective-permute-start.8) | collective-permute-done | bytes 491552 | tf_op jit(solution)/shard_map/ppermute | solution.py:112
  65.2 11.8 %shard_map.323 = (f32[480,128]{1,0:T(8,128)}, bf16[480,128]{1,0:T(8,128)(2,1)}, bf16[3264,512]{1,0:T(8,128)(2,1)}, bf16[8,960,128]{2,1,0:T(8,128)(2,1)}, f32[8,512]{1,0:T(8,128)}) custom-call(s32[2]{0:T(128)} %pad_add_fusion.place_ref, s32[8]{0:T(128)} %fusion.7.index_ref, bf16[3296,128]{1,0:T(8,128)(2,1)} %copy-done.10, bf16[3296,128]{1,0:T(8,128)(2,1)} %copy-done.25, ...), custom_call_target="tpu_custom_call" | custom-call | flops 855638016 | bytes 13000704 | tf_op jit(solution)/shard_map/pallas_call | solution.py:444
  94.0 12.8 %collective-permute-done.15 = bf16[480,256]{1,0:T(8,128)(2,1)S(1)} collective-permute-done((bf16[480,256]{1,0:T(8,128)(2,1)S(1)}, bf16[480,256]{1,0:T(8,128)(2,1)S(1)}, u32[]{:S(2)}, u32[]{:S(2)}) %collective-permute-start.15) | collective-permute-done | bytes 245792 | tf_op jit(solution)/shard_map/ppermute | solution.py:112
  108.9 6.2 %collective-permute-done.16 = bf16[480,256]{1,0:T(8,128)(2,1)S(1)} collective-permute-done((bf16[480,256]{1,0:T(8,128)(2,1)S(1)}, bf16[480,256]{1,0:T(8,128)(2,1)S(1)}, u32[]{:S(2)}, u32[]{:S(2)}) %collective-permute-start.16) | collective-permute-done | bytes 245792 | tf_op jit(solution)/shard_map/ppermute | solution.py:109
  116.6 5.9 %collective-permute-done.18 = bf16[480,256]{1,0:T(8,128)(2,1)S(1)} collective-permute-done((bf16[480,256]{1,0:T(8,128)(2,1)S(1)}, bf16[480,256]{1,0:T(8,128)(2,1)S(1)}, u32[]{:S(2)}, u32[]{:S(2)}) %collective-permute-start.18) | collective-permute-done | bytes 245792 | tf_op jit(solution)/shard_map/ppermute | solution.py:109
  130.7 7.3 %shard_map.325 = bf16[8,480,128]{2,1,0:T(8,128)(2,1)S(1)} custom-call(s32[6]{0:T(128)S(1)} %copy-done.3, s32[8]{0:T(128)S(1)} %copy-done.2, bf16[8,480,256]{2,1,0:T(8,128)(2,1)} %copy-done.7, bf16[8,480,256]{2,1,0:T(8,128)(2,1)} %collective-permute-done.20.mate_ref.far_ref, bf16[512,1152]{1,0:T(8,128)(2,1)S(1)} %copy-done.4, bf16[512,1024]{1,0:T(8,128)(2,1)S(1)} %copy-done.5), custom_call_target="tpu_custom_call" | custom-call | flops 4311744512 | bytes 4915200 | tf_op jit(solution)/shard_map/pallas_call | solution.py:308
  138.0 46.6 %all_to_all.25 = bf16[8,480,128]{2,1,0:T(8,128)(2,1)S(1)} all-to-all(bf16[8,480,128]{2,1,0:T(8,128)(2,1)S(1)} %shard_map.325), channel_id=1, replica_groups=mesh['dp'=8,'tensor'=4] {'dp'}, dimensions={0} | all-to-all | bytes 1966080 | tf_op jit(solution)/shard_map/all_to_all | solution.py:149
  195.8 5.0 collective-permute-done.21.across_ref
  203.7 7.9 %shard_map.326 = (bf16[2,816,128]{2,1,0:T(8,128)(2,1)}, bf16[2,816,128]{2,1,0:T(8,128)(2,1)}, bf16[2,816,128]{2,1,0:T(8,128)(2,1)}, bf16[2,816,128]{2,1,0:T(8,12...) custom-call(s32[2]{0:T(128)} %pad_add_fusion.place_ref, ...), custom_call_target="tpu_custom_call" | custom-call | flops 880803840 | bytes 10682368 | tf_op jit(solution)/shard_map/pallas_call | solution.py:504
  215.7 8.6 %collective-permute-done.24.refs_1_ = bf16[2,816,128]{2,1,0:T(8,128)(2,1)S(1)} collective-permute-done((bf16[2,816,128]{2,1,0:T(8,128)(2,1)}, bf16[2,816,128]{2,1,0:T(8,128)(2,1)S(1)}, u32[]{:S(2)}, u32[]{:S(2)}) %collective-permute-start.24) | collective-permute-done | bytes 417824 | tf_op jit(solution)/shard_map/ppermute | solution.py:42
  224.3 7.5 %collective-permute-done.26.refs_3_ = bf16[2,816,128]{2,1,0:T(8,128)(2,1)S(1)} collective-permute-done((bf16[2,816,128]{2,1,0:T(8,128)(2,1)}, bf16[2,816,128]{2,1,0:T(8,128)(2,1)S(1)}, u32[]{:S(2)}, u32[]{:S(2)}) %collective-permute-start.26) | collective-permute-done | bytes 417824 | tf_op jit(solution)/shard_map/ppermute | solution.py:42
  232.6 29.1 %shard_map.327 = (bf16[4,816,128]{2,1,0:T(8,128)(2,1)}, bf16[2,816,128]{2,1,0:T(8,128)(2,1)}, bf16[2,816,128]{2,1,0:T(8,128)(2,1)}, bf16[2,816,128]{2,1,0:T(8,12...) custom-call(s32[2]{0:T(128)} %pad_add_fusion.place_ref, ...), custom_call_target="tpu_custom_call" | custom-call | flops 12834570240 | bytes 13008896 | tf_op jit(solution)/shard_map/pallas_call | solution.py:620
  264.6 4.7 collective-permute-done.46
  276.0 10.7 %collective-permute-done.32.refs_1_ = bf16[2,816,128]{2,1,0:T(8,128)(2,1)S(1)} collective-permute-done((bf16[2,816,128]{2,1,0:T(8,128)(2,1)S(1)}, bf16[2,816,128]{2,1,0:T(8,128)(2,1)S(1)}, u32[]{:S(2)}, u32[]{:S(2)}) %collective-permute-start.32) | collective-permute-done | bytes 417824 | tf_op jit(solution)/shard_map/ppermute | solution.py:42
  286.8 7.8 %collective-permute-done.34.refs_3_ = bf16[2,816,128]{2,1,0:T(8,128)(2,1)S(1)} collective-permute-done((bf16[2,816,128]{2,1,0:T(8,128)(2,1)S(1)}, bf16[2,816,128]{2,1,0:T(8,128)(2,1)S(1)}, u32[]{:S(2)}, u32[]{:S(2)}) %collective-permute-start.34) | collective-permute-done | bytes 417824 | tf_op jit(solution)/shard_map/ppermute | solution.py:42
  295.4 10.1 %shard_map.328 = (f32[488,128]{1,0:T(8,128)}, f32[488,128]{1,0:T(8,128)}, f32[488,128]{1,0:T(8,128)}, f32[488,128]{1,0:T(8,128)}, bf16[512,3584]{1,0:T(8,128)(2,1)}, /*index=5*/f32[3264,128]{1,0:T(8,128)}) custom-call(s32[2]{0:T(128)} %pad_add_fusion.place_ref, bf16[2,816,128]{2,1,0:T(8,128)(2,1)} %get-tuple-element.132.refs_0_, ...), custom_call_target="tpu_custom_call" | custom-call | flops 1761607680 | bytes 15548416 | tf_op jit(solution)/shard_map/pallas_call | solution.py:692
  310.3 7.6 %collective-permute-done.37 = bf16[488,256]{1,0:T(8,128)(2,1)S(1)} collective-permute-done((bf16[488,256]{1,0:T(8,128)(2,1)S(1)}, bf16[488,256]{1,0:T(8,128)(2,1)S(1)}, u32[]{:S(2)}, u32[]{:S(2)}) %collective-permute-start.37) | collective-permute-done | bytes 249888 | tf_op jit(solution)/shard_map/ppermute | solution.py:42
  324.7 4.2 all-to-all-start.3
  331.1 8.1 %collective-permute-done.42 = bf16[480,128]{1,0:T(8,128)(2,1)S(1)} collective-permute-done((bf16[480,128]{1,0:T(8,128)(2,1)S(1)}, bf16[480,128]{1,0:T(8,128)(2,1)S(1)}, u32[]{:S(2)}, u32[]{:S(2)}) %collective-permute-start.42) | collective-permute-done | bytes 122912 | tf_op jit(solution)/shard_map/ppermute | solution.py:112
  341.3 4.4 collective-permute-done.43
  347.8 4.6 collective-permute-done.45
  353.3 22.8 %shard_map.329 = (f32[4352,128]{1,0:T(8,128)}, f32[3264,128]{1,0:T(8,128)}, bf16[8,480,128]{2,1,0:T(8,128)(2,1)}, bf16[8,480,128]{2,1,0:T(8,128)(2,1)}, bf16[8,4...) custom-call(s32[2]{0:T(128)} %pad_add_fusion.place_ref, s32[6]{0:T(128)} %fusion.8.plan_ref.reach_ref, ...), custom_call_target="tpu_custom_call" | custom-call | flops 8623489024 | bytes 14974976 | tf_op jit(solution)/shard_map/pallas_call | solution.py:351
  382.5 22.6 %collective-permute-done.49 = bf16[8,480,128]{2,1,0:T(8,128)(2,1)S(1)} collective-permute-done((bf16[8,480,128]{2,1,0:T(8,128)(2,1)S(1)}, bf16[8,480,128]{2,1,0:T(8,128)(2,1)S(1)}, u32[]{:S(2)}, u32[]{:S(2)}) %collective-permute-start.49) | collective-permute-done | bytes 983072 | tf_op jit(solution)/shard_map/ppermute | solution.py:42
  406.4 4.2 all-to-all-start.4
  410.9 35.7 %collective-permute-done.61.refs_1_ = bf16[8,960,128]{2,1,0:T(8,128)(2,1)} collective-permute-done((bf16[8,960,128]{2,1,0:T(8,128)(2,1)S(1)}, bf16[8,960,128]{2,1,0:T(8,128)(2,1)}, u32[]{:S(2)}, u32[]{:S(2)}) %collective-permute-start.61) | collective-permute-done | bytes 1966112 | tf_op jit(solution)/shard_map/ppermute | solution.py:42
  460.6 10.0 %shard_map.330 = (bf16[3264,128]{1,0:T(8,128)(2,1)}, bf16[3264,128]{1,0:T(8,128)(2,1)}, bf16[3264,128]{1,0:T(8,128)(2,1)}, bf16[3264,128]{1,0:T(8,128)(2,1)}) custom-call(s32[2]{0:T(128)} %pad_add_fusion.place_ref, s32[8]{0:T(128)} %fusion.7.index_ref, bf16[480,128]{1,0:T(8,128)(2,1)} %copy-done.21, bf16[1920,128]{1,0:T(8,128)(2,1)} %copy-done.13, ...), custom_call_target="tpu_custom_call" | custom-call | flops 855638016 | bytes 7397376 | tf_op jit(solution)/shard_map/pallas_call | solution.py:796
  472.2 4.6 collective-permute-done.55
  483.8 5.7 %collective-permute-done.57 = bf16[496,128]{1,0:T(8,128)(2,1)S(1)} collective-permute-done((bf16[496,128]{1,0:T(8,128)(2,1)S(1)}, bf16[496,128]{1,0:T(8,128)(2,1)S(1)}, u32[]{:S(2)}, u32[]{:S(2)}) %collective-permute-start.57) | collective-permute-done | bytes 127008 | tf_op jit(solution)/shard_map/ppermute | solution.py:109
  491.5 5.1 collective-permute-done.58
  502.8 10.1 %shard_map.331 = (f32[768,128]{1,0:T(8,128)}, f32[1024,128]{1,0:T(8,128)}, f32[16,128]{1,0:T(8,128)}) custom-call(s32[2]{0:T(128)} %pad_add_fusion.place_ref, s32[6]{0:T(128)} %fusion.8.plan_ref.reach_ref, s32[8]{0:T(128)} %fusion.7.index_ref, bf16[8,496,128]{2,1,0:T(8,128)(2,1)} %copy-done.9, bf16[8,960,128]{2,1,0:T(8,128)(2,1)} %copy-done.6, ...), custom_call_target="tpu_custom_call" | custom-call | flops 2013265920 | bytes 8880128 | tf_op jit(solution)/shard_map/pallas_call | solution.py:753
  (334 shorter events, 162.3 us)
Async XLA Ops:
  7.3 115.3 %all-gather.4.cloned.1.call-start = ((), (), s32[]{:S(2)}) async-start(), calls=%async_computation.7 | async-start | bytes 1769472 | tf_op jit(solution)/shard_map/all_gather | solution.py:874
  10.1 14.2 %collective-permute-start = (bf16[1920,128]{1,0:T(8,128)(2,1)S(1)}, bf16[1920,128]{1,0:T(8,128)(2,1)S(1)}, u32[]{:S(2)}, u32[]{:S(2)}) collective-permute-start(bf16[1920,128]{1,0:T(8,128)(2,1)S(1)} %constant_dynamic-update-slice_fusion.5.refs_4_.refs_0_), channel_id=1, source_target_pairs={{0,8},{8,16},{16,24},{24,28},{28,20},{20,12},{12,4},{4,0},{1,9},{9... | collective-permute-start | bytes 1474568 | tf_op jit(solution)/shard_map/ppermute | solution.py:109
  14.5 20.3 %collective-permute-start.2 = (bf16[3296,128]{1,0:T(8,128)(2,1)S(1)}, bf16[3296,128]{1,0:T(8,128)(2,1)S(1)}, u32[]{:S(2)}, u32[]{:S(2)}) collective-permute-start(bf16[3296,128]{1,0:T(8,128)(2,1)S(1)} %constant_dynamic-update-slice_fusion.refs_0_), channel_id=1, source_target_pairs={{0,2},{1,3},{2,0},{3,1},{4,6},{5,7},{6,4},{7,5},{8,10},{9,11},{10,... | collective-permute-start | bytes 2531336 | tf_op jit(solution)/shard_map/ppermute | solution.py:42
  16.1 12.4 %collective-permute-start.6 = (bf16[1920,128]{1,0:T(8,128)(2,1)S(1)}, bf16[1920,128]{1,0:T(8,128)(2,1)S(1)}, u32[]{:S(2)}, u32[]{:S(2)}) collective-permute-start(bf16[1920,128]{1,0:T(8,128)(2,1)S(1)} %constant_dynamic-update-slice_fusion.5.refs_4_.refs_0_), channel_id=1, source_target_pairs={{8,0},{16,8},{24,16},{28,24},{20,28},{12,20},{4,12},{0,4},{9,1},{1... | collective-permute-start | bytes 1474568 | tf_op jit(solution)/shard_map/ppermute | solution.py:112
  24.3 12.4 %collective-permute-start.1 = (bf16[1920,128]{1,0:T(8,128)(2,1)S(1)}, bf16[1920,128]{1,0:T(8,128)(2,1)S(1)}, u32[]{:S(2)}, u32[]{:S(2)}) collective-permute-start(bf16[1920,128]{1,0:T(8,128)(2,1)S(1)} %collective-permute-done.refs_5_.refs_1_), channel_id=1, source_target_pairs={{0,8},{8,16},{16,24},{24,28},{28,20},{20,12},{12,4},{4,0},{1,9},{9... | collective-permute-start | bytes 1474568 | tf_op jit(solution)/shard_map/ppermute | solution.py:109
  28.9 23.0 %collective-permute-start.4 = (bf16[3296,128]{1,0:T(8,128)(2,1)S(1)}, bf16[3296,128]{1,0:T(8,128)(2,1)S(1)}, u32[]{:S(2)}, u32[]{:S(2)}) collective-permute-start(bf16[3296,128]{1,0:T(8,128)(2,1)S(1)} %constant_dynamic-update-slice_fusion.refs_0_), channel_id=1, source_target_pairs={{0,1},{1,0},{2,3},{3,2},{4,5},{5,4},{6,7},{7,6},{8,9},{9,8},{10,11... | collective-permute-start | bytes 2531336 | tf_op jit(solution)/shard_map/ppermute | solution.py:42
  36.7 15.2 %collective-permute-start.5 = (bf16[3296,128]{1,0:T(8,128)(2,1)S(1)}, bf16[3296,128]{1,0:T(8,128)(2,1)S(1)}, u32[]{:S(2)}, u32[]{:S(2)}) collective-permute-start(bf16[3296,128]{1,0:T(8,128)(2,1)S(1)} %collective-permute-done.2.refs_1_), channel_id=1, source_target_pairs={{0,1},{1,0},{2,3},{3,2},{4,5},{5,4},{6,7},{7,6},{8,9},{9,8},{10,11... | collective-permute-start | bytes 2531336 | tf_op jit(solution)/shard_map/ppermute | solution.py:42
  84.5 38.1 %collective-permute-start.19 = (bf16[1024,512]{1,0:T(8,128)(2,1)}, bf16[1024,512]{1,0:T(8,128)(2,1)}, u32[]{:S(2)}, u32[]{:S(2)}) collective-permute-start(bf16[1024,512]{1,0:T(8,128)(2,1)} %pad_maximum_fusion.refs_4_), channel_id=1, source_target_pairs={{0,2},{1,3},{2,0},{3,1},{4,6},{5,7},{6,4},{7,5},{8,10},{9,11},{10,... | collective-permute-start | bytes 3145736 | tf_op jit(solution)/shard_map/ppermute | solution.py:42
  85.7 36.9 %all-to-all-start = ((bf16[4,816,128]{2,1,0:T(8,128)(2,1)}), bf16[4,816,128]{2,1,0:T(8,128)(2,1)S(1)}, u32[]{:S(2)}, u32[]{:S(2)}) async-start(bf16[4,816,128]{2,1,0:T(8,128)(2,1)} %bitcast.123), calls=%async_computation | async-start | bytes 1671168 | tf_op jit(solution)/shard_map/all_to_all | solution.py:884
  89.2 96.3 %all-gather.6.cloned.1.call-start = ((), (), s32[]{:S(2)}) async-start(), calls=%async_computation.8 | async-start | bytes 2359296 | tf_op jit(solution)/shard_map/all_gather | solution.py:875
  89.4 17.5 %collective-permute-start.15 = (bf16[480,256]{1,0:T(8,128)(2,1)S(1)}, bf16[480,256]{1,0:T(8,128)(2,1)S(1)}, u32[]{:S(2)}, u32[]{:S(2)}) collective-permute-start(bf16[480,256]{1,0:T(8,128)(2,1)S(1)} %collective-permute-done.13), channel_id=1, source_target_pairs={{8,0},{16,8},{24,16},{28,24},{20,28},{12,20},{4,12},{0,4},{9,1},{1... | collective-permute-start | bytes 737288 | tf_op jit(solution)/shard_map/ppermute | solution.py:112
  91.0 15.8 %collective-permute-start.14 = (bf16[480,256]{1,0:T(8,128)(2,1)S(1)}, bf16[480,256]{1,0:T(8,128)(2,1)S(1)}, u32[]{:S(2)}, u32[]{:S(2)}) collective-permute-start(bf16[480,256]{1,0:T(8,128)(2,1)S(1)} %collective-permute-done.12), channel_id=1, source_target_pairs={{0,8},{8,16},{16,24},{24,28},{28,20},{20,12},{12,4},{4,0},{1,9},{9... | collective-permute-start | bytes 737288 | tf_op jit(solution)/shard_map/ppermute | solution.py:109
  185.5 76.2 %all-to-all-start.2 = ((bf16[8,960,128]{2,1,0:T(8,128)(2,1)}), bf16[8,960,128]{2,1,0:T(8,128)(2,1)S(1)}, u32[]{:S(2)}, u32[]{:S(2)}) async-start(bf16[8,960,128]{2,1,0:T(8,128)(2,1)} %get-tuple-element.126), calls=%async_computation.2 | async-start | bytes 3932160 | tf_op jit(solution)/shard_map/all_to_all | solution.py:899
  189.2 217.2 %reduce-scatter.3.cloned.1.call-start = ((), (), s32[]{:S(2)}) async-start(), calls=%async_computation.9 | async-start | bytes 2949120 | tf_op jit(solution)/shard_map/reduce_scatter | solution.py:909
  190.8 21.5 %collective-permute-start.27 = (bf16[1024,512]{1,0:T(8,128)(2,1)}, bf16[1024,512]{1,0:T(8,128)(2,1)S(1)}, u32[]{:S(2)}, u32[]{:S(2)}) collective-permute-start(bf16[1024,512]{1,0:T(8,128)(2,1)} %pad_maximum_fusion.refs_4_), channel_id=1, source_target_pairs={{0,1},{1,0},{2,3},{3,2},{4,5},{5,4},{6,7},{7,6},{8,9},{9,8},{10,11... | collective-permute-start | bytes 3145736 | tf_op jit(solution)/shard_map/ppermute | solution.py:42
  191.7 22.1 %collective-permute-start.28 = (bf16[1024,512]{1,0:T(8,128)(2,1)}, bf16[1024,512]{1,0:T(8,128)(2,1)S(1)}, u32[]{:S(2)}, u32[]{:S(2)}) collective-permute-start(bf16[1024,512]{1,0:T(8,128)(2,1)} %collective-permute-done.19.refs_5_), channel_id=1, source_target_pairs={{0,1},{1,0},{2,3},{3,2},{4,5},{5,4},{6,7},{7,6},{8,9},{9,8},{10,11... | collective-permute-start | bytes 3145736 | tf_op jit(solution)/shard_map/ppermute | solution.py:42
  211.6 12.8 %collective-permute-start.24 = (bf16[2,816,128]{2,1,0:T(8,128)(2,1)}, bf16[2,816,128]{2,1,0:T(8,128)(2,1)S(1)}, u32[]{:S(2)}, u32[]{:S(2)}) collective-permute-start(bf16[2,816,128]{2,1,0:T(8,128)(2,1)} %get-tuple-element.120), channel_id=1, source_target_pairs={{0,2},{1,3},{2,0},{3,1},{4,6},{5,7},{6,4},{7,5},{8,10},{9,11},{10,... | collective-permute-start | bytes 1253384 | tf_op jit(solution)/shard_map/ppermute | solution.py:42
  212.3 19.5 %collective-permute-start.26 = (bf16[2,816,128]{2,1,0:T(8,128)(2,1)}, bf16[2,816,128]{2,1,0:T(8,128)(2,1)S(1)}, u32[]{:S(2)}, u32[]{:S(2)}) collective-permute-start(bf16[2,816,128]{2,1,0:T(8,128)(2,1)} %get-tuple-element.122), channel_id=1, source_target_pairs={{0,3},{1,2},{2,1},{3,0},{4,7},{5,6},{6,5},{7,4},{8,11},{9,10},{10,... | collective-permute-start | bytes 1253384 | tf_op jit(solution)/shard_map/ppermute | solution.py:42
  273.3 175.2 %reduce-scatter.5.cloned.1.call-start = ((), (), s32[]{:S(2)}) async-start(), calls=%async_computation.11 | async-start | bytes 4128768 | tf_op jit(solution)/shard_map/reduce_scatter | solution.py:914
  274.3 12.5 %collective-permute-start.32 = (bf16[2,816,128]{2,1,0:T(8,128)(2,1)S(1)}, bf16[2,816,128]{2,1,0:T(8,128)(2,1)S(1)}, u32[]{:S(2)}, u32[]{:S(2)}) collective-permute-start(bf16[2,816,128]{2,1,0:T(8,128)(2,1)S(1)} %copy-done.54), channel_id=1, source_target_pairs={{0,2},{1,3},{2,0},{3,1},{4,6},{5,7},{6,4},{7,5},{8,10},{9,11},{10,... | collective-permute-start | bytes 1253384 | tf_op jit(solution)/shard_map/ppermute | solution.py:42
  275.0 19.6 %collective-permute-start.34 = (bf16[2,816,128]{2,1,0:T(8,128)(2,1)S(1)}, bf16[2,816,128]{2,1,0:T(8,128)(2,1)S(1)}, u32[]{:S(2)}, u32[]{:S(2)}) collective-permute-start(bf16[2,816,128]{2,1,0:T(8,128)(2,1)S(1)} %copy-done.52), channel_id=1, source_target_pairs={{0,3},{1,2},{2,1},{3,0},{4,7},{5,6},{6,5},{7,4},{8,11},{9,10},{10,... | collective-permute-start | bytes 1253384 | tf_op jit(solution)/shard_map/ppermute | solution.py:42
  324.7 51.4 %all-to-all-start.3 = ((bf16[4,816,128]{2,1,0:T(8,128)(2,1)}), bf16[4,816,128]{2,1,0:T(8,128)(2,1)}, u32[]{:S(2)}, u32[]{:S(2)}) async-start(bf16[4,816,128]{2,1,0:T(8,128)(2,1)} %get-tuple-element.146), calls=%async_computation.3 | async-start | bytes 1671168 | tf_op jit(solution)/shard_map/all_to_all | solution.py:923
  380.4 24.7 %collective-permute-start.49 = (bf16[8,480,128]{2,1,0:T(8,128)(2,1)S(1)}, bf16[8,480,128]{2,1,0:T(8,128)(2,1)S(1)}, u32[]{:S(2)}, u32[]{:S(2)}) collective-permute-start(bf16[8,480,128]{2,1,0:T(8,128)(2,1)S(1)} %add_convert_fusion.1), channel_id=1, source_target_pairs={{0,2},{1,3},{2,0},{3,1},{4,6},{5,7},{6,4},{7,5},{8,10},{9,11},{10,... | collective-permute-start | bytes 2949128 | tf_op jit(solution)/shard_map/ppermute | solution.py:42
  381.6 65.0 %collective-permute-start.61 = (bf16[8,960,128]{2,1,0:T(8,128)(2,1)S(1)}, bf16[8,960,128]{2,1,0:T(8,128)(2,1)}, u32[]{:S(2)}, u32[]{:S(2)}) collective-permute-start(bf16[8,960,128]{2,1,0:T(8,128)(2,1)S(1)} %all-to-all-done.2.refs_0_), channel_id=1, source_target_pairs={{0,2},{1,3},{2,0},{3,1},{4,6},{5,7},{6,4},{7,5},{8,10},{9,11},{10,... | collective-permute-start | bytes 5898248 | tf_op jit(solution)/shard_map/ppermute | solution.py:42
  406.4 46.4 %all-to-all-start.4 = ((bf16[8,480,128]{2,1,0:T(8,128)(2,1)}), bf16[8,480,128]{2,1,0:T(8,128)(2,1)}, u32[]{:S(2)}, u32[]{:S(2)}) async-start(bf16[8,480,128]{2,1,0:T(8,128)(2,1)} %convert_add_fusion), calls=%async_computation.5 | async-start | bytes 1966080 | tf_op jit(solution)/shard_map/all_to_all | solution.py:149
  410.7 91.2 %all-gather.8.cloned.1.call-start = ((), (), s32[]{:S(2)}) async-start(), calls=%async_computation.10 | async-start | bytes 1179648 | tf_op jit(solution)/shard_map/all_gather | solution.py:948
  410.7 91.2 %collective-permute-start.62 = (bf16[8,960,128]{2,1,0:T(8,128)(2,1)S(1)}, bf16[8,960,128]{2,1,0:T(8,128)(2,1)}, u32[]{:S(2)}, u32[]{:S(2)}) collective-permute-start(bf16[8,960,128]{2,1,0:T(8,128)(2,1)S(1)} %all-to-all-done.2.refs_0_), channel_id=1, source_target_pairs={{0,1},{1,0},{2,3},{3,2},{4,5},{5,4},{6,7},{7,6},{8,9},{9,8},{10,11... | collective-permute-start | bytes 5898248 | tf_op jit(solution)/shard_map/ppermute | solution.py:42
  446.5 55.4 %collective-permute-start.63 = (bf16[8,960,128]{2,1,0:T(8,128)(2,1)}, bf16[8,960,128]{2,1,0:T(8,128)(2,1)}, u32[]{:S(2)}, u32[]{:S(2)}) collective-permute-start(bf16[8,960,128]{2,1,0:T(8,128)(2,1)} %collective-permute-done.61.refs_1_), channel_id=1, source_target_pairs={{0,1},{1,0},{2,3},{3,2},{4,5},{5,4},{6,7},{7,6},{8,9},{9,8},{10,11... | collective-permute-start | bytes 5898248 | tf_op jit(solution)/shard_map/ppermute | solution.py:42
  455.5 15.3 %collective-permute-start.53 = (bf16[496,128]{1,0:T(8,128)(2,1)S(1)}, bf16[496,128]{1,0:T(8,128)(2,1)S(1)}, u32[]{:S(2)}, u32[]{:S(2)}) collective-permute-start(bf16[496,128]{1,0:T(8,128)(2,1)S(1)} %get-tuple-element.224), channel_id=1, source_target_pairs={{0,8},{8,16},{16,24},{24,28},{28,20},{20,12},{12,4},{4,0},{1,9},{9... | collective-permute-start | bytes 380936 | tf_op jit(solution)/shard_map/ppermute | solution.py:109
  470.7 45.3 %collective-permute-start.50 = (bf16[3264,128]{1,0:T(8,128)(2,1)}, bf16[3264,128]{1,0:T(8,128)(2,1)}, u32[]{:S(2)}, u32[]{:S(2)}) collective-permute-start(bf16[3264,128]{1,0:T(8,128)(2,1)} %get-tuple-element.165), channel_id=1, source_target_pairs={{0,1},{1,0},{2,3},{3,2},{4,5},{5,4},{6,7},{7,6},{8,9},{9,8},{10,11... | collective-permute-start | bytes 2506760 | tf_op jit(solution)/shard_map/ppermute | solution.py:42
  470.8 27.1 %collective-permute-start.51 = (bf16[3264,128]{1,0:T(8,128)(2,1)}, bf16[3264,128]{1,0:T(8,128)(2,1)S(1)}, u32[]{:S(2)}, u32[]{:S(2)}) collective-permute-start(bf16[3264,128]{1,0:T(8,128)(2,1)} %get-tuple-element.167), channel_id=1, source_target_pairs={{0,1},{1,0},{2,3},{3,2},{4,5},{5,4},{6,7},{7,6},{8,9},{9,8},{10,11... | collective-permute-start | bytes 2506760 | tf_op jit(solution)/shard_map/ppermute | solution.py:42
  499.0 20.3 %collective-permute-start.52 = (bf16[3264,128]{1,0:T(8,128)(2,1)}, bf16[3264,128]{1,0:T(8,128)(2,1)}, u32[]{:S(2)}, u32[]{:S(2)}) collective-permute-start(bf16[3264,128]{1,0:T(8,128)(2,1)} %add_convert_fusion.2), channel_id=1, source_target_pairs={{0,2},{1,3},{2,0},{3,1},{4,6},{5,7},{6,4},{7,5},{8,10},{9,11},{10,... | collective-permute-start | bytes 2506760 | tf_op jit(solution)/shard_map/ppermute | solution.py:42
  (101 other events, 1137.0 us)
Sparse Core Ops, SparseCore 0:
  61.2 49.1 all-gather.3
  122.9 62.5 all-gather.5
  273.5 74.3 reduce-scatter.2
  351.4 97.1 reduce-scatter.4
  459.1 41.2 all-gather.7
